TPU v7x, 512 devices: a whole 4x8x8 slice. The times are simulated.
512 devices in a mesh: samp: 64 (over z, y), trait: 8 (over x, core).
Axes of the slice: x: 4, y: 8, z: 8, core: 2. Of those that a mesh axis runs over, the one named last changes fastest.
Arguments:
- samples: bfloat16 [32768, 2048], P('samp'), may hold values from -18 to 18
- traits: bfloat16 [32768, 2048], P('samp', 'trait'), may hold values from -6 to 6
- whitening: bfloat16 [2048, 2048], P(None, 'trait'), may hold values from -0.0017089844 to 0.0017089844
- singular: float32 [2048], replicated, may hold values from 0.3 to 3
- lambdas: float32 [4], replicated, may hold values from 0.1 to 10
Outputs:
- loo_residual: float32 [4, 32768, 2048], P(None, 'samp', 'trait')
All inputs are finite; a program needn't handle non-finite values.
Results may differ from a plain program's by a relative error of at most 0.0041.
Values may be sent and summed in bfloat16 or wider, within the bound.
No kernel may reach another device: no remote copies, remote signals or barrier semaphores. Data moves between devices by JAX's collectives and lax.ppermute only.
A program may use at most 64 MiB of HBM per device.

v0:
```python
import jax
import jax.numpy as jnp
from jax import lax
from jax.sharding import PartitionSpec as P


def local(samples, traits, whitening, singular, lambdas):
    squared_values = singular * singular
    shrink = squared_values[:, None] / (squared_values[:, None] + lambdas[None, :])
    own_components = jnp.dot(samples, whitening, preferred_element_type=jnp.float32).astype(
        jnp.bfloat16
    )
    components = lax.all_gather(own_components, "trait", axis=1, tiled=True)
    wide_float = components.astype(jnp.float32)
    leverage = jnp.dot(wide_float * wide_float, shrink, precision=lax.Precision.HIGHEST)
    contract_rows = (((0,), (0,)), ((), ()))
    partial_terms = lax.dot_general(
        components, traits, contract_rows, preferred_element_type=jnp.float32
    )
    projected = lax.psum(partial_terms, "samp").astype(jnp.bfloat16)
    scaled = (shrink.T[:, :, None] * projected.astype(jnp.float32)[None]).astype(jnp.bfloat16)
    fitted = jnp.einsum("np,lpt->lnt", components, scaled, preferred_element_type=jnp.float32)
    divisor = jnp.maximum(1.0 - leverage.T[:, :, None], 0.25)
    return (traits.astype(jnp.float32)[None] - fitted) / divisor


def solution(mesh):
    return jax.shard_map(
        local,
        mesh=mesh,
        in_specs=(P("samp", None), P("samp", "trait"), P(None, "trait"), P(), P()),
        out_specs=P(None, "samp", "trait"),
        check_vma=False,
    )
```

profile of v0, /device:TPU:4, one launch (start us, length us, event | category | flops | bytes accessed | tf_op | source)
XLA Modules:
  0.0 373.7 jit_solution(3277918667649687094)
XLA Ops:
  6.5 0.0 copy-start
  6.5 0.0 copy-start.4
  6.5 0.0 copy-start.2
  6.5 0.0 copy-start.5
  6.5 0.0 all-gather.2.cloned.1.call-start
  6.6 1.5 copy-done
  8.1 2.6 convolution_convert_fusion
  10.8 0.0 all-gather.2.cloned.1.call-update
  10.8 0.0 copy-done.4
  10.8 0.0 copy-done.2
  10.8 0.9 copy.6
  11.8 0.0 copy-done.5
  11.8 0.1 add_divide_fusion
  11.9 35.5 %all-gather.2.cloned.1.call-done = bf16[512,2048]{1,0:T(8,128)(2,1)} async-done(((bf16[512,256]{1,0:T(8,128)(2,1)}), bf16[512,2048]{1,0:T(8,128)(2,1)}) %all-gather.2.cloned.1.call-update) | async-done | bytes 2097168 | tf_op jit(solution)/shard_map/all_gather | solution.py:13
  47.3 3.7 fusion.20
  51.0 303.7 %all-reduce.1 = bf16[2048,256]{0,1:T(8,128)(2,1)S(1)} all-reduce(f32[2048,256]{0,1:T(8,128)} %fusion.20), channel_id=1, replica_groups=mesh['samp'=64,'trait'=8] {'samp'}, use_global_device_ids=true, to_apply=%region_0.0 | all-reduce | flops 524288 | bytes 3145728 | tf_op jit(solution)/shard_map/psum | solution.py:20
  354.7 0.0 copy-start.1
  354.7 0.2 convert_element_type.39
  354.9 1.4 copy-done.1
  356.3 0.0 copy-start.3
  356.3 3.9 %fusion.13 = f32[4,512]{1,0:T(4,128)S(1)} fusion(bf16[512,2048]{1,0:T(8,128)(2,1)S(1)} %copy-done.1, f32[4]{0:T(128)S(1)} %copy-done.5, f32[2048]{0:T(1024)S(1)} %mul.19), kind=kOutput, calls=%fused_computation.12 | convolution fusion | flops 52449280 | bytes 2113552 | tf_op jit(solution)/shard_map/dot_general | solution.py:15
  360.2 0.0 copy-done.3
  360.2 3.7 %fusion.6 = f32[4,512,256]{1,2,0:T(8,128)} fusion(bf16[512,2048]{1,0:T(8,128)(2,1)S(1)} %copy-done.1, f32[2048,256]{0,1:T(8,128)S(1)} %convert_element_type.39, f32[4,2048]{1,0:T(4,128)S(1)} %add_divide_fusion, f32[4,512]{1,0:T(4,128)S(1)} %fusion.13, f32[512,256]{0,1:T(8,128)S(1)} %copy-done.3), kind=kOutput, calls=%fused_computation.8 | convolution fusion | flops 2152726528 | bytes 6856704 | tf_op jit(solution)/shard_map/np,lpt->lnt/dot_general | solution.py:22
  364.0 2.9 copy.7
  (1 shorter events, 0.0 us)
Async XLA Ops:
  6.5 1.6 copy-start
  6.5 4.3 %copy-start.4 = (f32[2048]{0:T(1024)S(1)}, f32[2048]{0:T(1024)}, u32[]{:S(2)}) copy-start(f32[2048]{0:T(1024)} %param.8) | copy-start | bytes 24580
  6.5 4.3 %copy-start.2 = (bf16[512,256]{1,0:T(8,128)(2,1)S(1)}, bf16[512,256]{1,0:T(8,128)(2,1)}, u32[]{:S(2)}) copy-start(bf16[512,256]{1,0:T(8,128)(2,1)} %param.6) | copy-start | bytes 786436
  6.5 5.2 %copy-start.5 = (f32[4]{0:T(128)S(1)}, f32[4]{0:T(128)}, u32[]{:S(2)}) copy-start(f32[4]{0:T(128)} %param.9) | copy-start | bytes 52
  6.5 40.8 %all-gather.2.cloned.1.call-start = ((), (), s32[]{:S(2)}) async-start(), calls=%async_computation | async-start | bytes 2359296 | tf_op jit(solution)/shard_map/all_gather | solution.py:13
  354.7 1.6 copy-start.1
  356.3 3.9 %copy-start.3 = (f32[512,256]{0,1:T(8,128)S(1)}, f32[512,256]{0,1:T(8,128)}, u32[]{:S(2)}) copy-start(f32[512,256]{0,1:T(8,128)} %copy.6) | copy-start | bytes 1572868
Sparse Core Ops, SparseCore 0:
  10.9 36.3 all-gather.1
where the time goes:
time: 374 us
  blocking collectives  304 us (81%)
  waiting for transfers between devices  35.5 us (9%)
  matrix products  14 us (4%)
  between operations  13.5 us (4%)
  local copies, waits for them, and re-layouts  6.74 us (2%)
    psum x1, blocking collectives, local(): projected = lax.psum(partial_terms, 'samp').astype(jnp.bfloat16)  304 us
    all_gather x1, waiting for transfers between devices, local(): components = lax.all_gather(own_components, 'trait', axis=1, tiled=True)  35.5 us
  transfers between devices with their start and end apart: 1, of which 1 were waited for; matrix products, arithmetic and copies ran while one was open for 0% of the time, Pallas kernels for 0%

commit v1 on v0

v1 whole, which is shorter than its diff:
```python
import jax
import jax.numpy as jnp
from jax import lax
from jax.sharding import Mesh, PartitionSpec as P

SAMP = ("z", "y")
TRAIT = ("x", "core")


def local(samples, traits, whitening, singular, lambdas):
    depth = whitening.shape[1]
    rows = samples.shape[0]
    width = traits.shape[1]
    n_x, n_core = lax.axis_size("x"), lax.axis_size("core")
    n_samp = lax.axis_size("z") * lax.axis_size("y")
    core = lax.axis_index("core")

    own = jnp.dot(samples, whitening, preferred_element_type=jnp.float32).astype(jnp.bfloat16)
    mine = lax.all_to_all(jnp.broadcast_to(own[None], (n_x, rows, depth)), "x", 0, 0)
    other = lax.ppermute(mine, "core", [(0, 1), (1, 0)])
    halves = [
        jnp.moveaxis(half, 0, 1).reshape(rows, n_x * depth) for half in (mine, other)
    ]

    squared = (singular * singular).reshape(n_x, n_core, depth)
    squared = jnp.moveaxis(squared, 1, 0).reshape(n_core, n_x * depth)
    squared = jnp.where(core == 0, squared, squared[::-1])
    shrink = squared[None] / (squared[None] + lambdas[:, None, None])

    flipped = traits.T
    partial = jnp.stack(
        [jnp.dot(flipped, half, preferred_element_type=jnp.float32) for half in halves]
    ).astype(jnp.bfloat16)
    pieces = partial.reshape(n_samp, -1, n_x * depth)
    arrived = lax.all_to_all(pieces, SAMP, 0, 0)
    total = jnp.sum(arrived.astype(jnp.float32), axis=0).astype(jnp.bfloat16)
    spread = lax.all_to_all(jnp.broadcast_to(total[None], pieces.shape), SAMP, 0, 0)
    projected = spread.reshape(n_core, width, n_x * depth)

    leverage = 0.0
    fitted = 0.0
    for i, half in enumerate(halves):
        wide = half.astype(jnp.float32)
        leverage = leverage + jnp.dot(
            shrink[:, i], (wide * wide).T, precision=lax.Precision.HIGHEST
        )
        scaled = (shrink[:, i, None, :] * projected[i].astype(jnp.float32)[None]).astype(jnp.bfloat16)
        fitted = fitted + jnp.einsum("np,ltp->lnt", half, scaled, preferred_element_type=jnp.float32)
    divisor = jnp.maximum(1.0 - leverage[:, :, None], 0.25)
    return (traits.astype(jnp.float32)[None] - fitted) / divisor


def solution(mesh):
    split = Mesh(mesh.devices.reshape(8, 8, 4, 2), SAMP + TRAIT)
    return jax.shard_map(
        local,
        mesh=split,
        in_specs=(P(SAMP, None), P(SAMP, TRAIT), P(None, TRAIT), P(), P()),
        out_specs=P(None, SAMP, TRAIT),
        check_vma=False,
    )
```

time: 374 us -> 124 us (0.33)
  the two profiles are of different devices: /device:TPU:4 before, /device:TPU:8 now
where the time goes in v1:
time: 124 us; the launch traced here: 123 us
  blocking collectives  65.3 us (53%)
  waiting for transfers between devices  20.8 us (17%)
  local copies, waits for them, and re-layouts  13.7 us (11%)
  starting transfers between devices  9.12 us (7%)
  matrix products  8.98 us (7%)
  other arithmetic  5 us (4%)
    all_to_all x1, blocking collectives, local(): arrived = lax.all_to_all(pieces, SAMP, 0, 0)  46.1 us
    all_to_all x1, blocking collectives, local(): lax.all_to_all(jnp.broadcast_to(own[None], (n_x, rows, depth)), 'x', 0, 0)  19.2 us
    all_to_all x1, waiting for transfers between devices, local(): lax.all_to_all(jnp.broadcast_to(total[None], pieces.shape), SAMP, 0, 0)  18.6 us
    all_to_all x1, starting transfers between devices, local(): lax.all_to_all(jnp.broadcast_to(total[None], pieces.shape), SAMP, 0, 0)  7.22 us
    dot_general x2, matrix products, local(): jnp.einsum('np,ltp->lnt', half, scaled, preferred_element_type=jnp.float32)  3.89 us
    div x1, local copies, waits for them, and re-layouts, local(): return (traits.astype(jnp.float32)[None] - fitted) / divisor  2.88 us
    reshape x2, local copies, waits for them, and re-layouts, local(): jnp.moveaxis(half, 0, 1).reshape(rows, n_x * depth)  2.7 us
    unnamed x16, local copies, waits for them, and re-layouts  2.64 us
  transfers between devices with their start and end apart: 2, of which 2 were waited for; matrix products, arithmetic and copies ran while one was open for 8% of the time, Pallas kernels for 0%

profile of v1, /device:TPU:8, one launch (start us, length us, event | category | flops | bytes accessed | tf_op | source)
XLA Modules:
  0.0 123.1 jit_solution(16342966001318790646)
XLA Ops:
  0.0 0.0 copy-start
  0.0 1.6 %copy-done = bf16[512,2048]{1,0:T(8,128)(2,1)S(1)} copy-done((bf16[512,2048]{1,0:T(8,128)(2,1)S(1)}, bf16[512,2048]{1,0:T(8,128)(2,1)}, u32[]{:S(2)}) %copy-start) | copy-done | bytes 2097176
  1.6 1.9 %convolution_convert_fusion.2 = bf16[512,256]{1,0:T(8,128)(2,1)S(1)} fusion(bf16[512,2048]{1,0:T(8,128)(2,1)S(1)} %copy-done, bf16[2048,256]{1,0:T(8,128)(2,1)} %param.7), kind=kOutput, calls=%fused_computation.16 | convolution fusion | flops 537001984 | bytes 3407872 | tf_op jit(solution)/shard_map/dot_general | solution.py:18
  3.5 0.1 broadcast_in_dim.4
  3.6 19.2 %all_to_all.15 = bf16[4,512,256]{2,1,0:T(8,128)(2,1)S(1)} all-to-all(bf16[4,512,256]{2,1,0:T(8,128)(2,1)S(1)} %broadcast_in_dim.4), channel_id=1, replica_groups=mesh['z'=8,'y'=8,'x'=4,'core'=2] {'x'}, dimensions={0} | all-to-all | bytes 2097152 | tf_op jit(solution)/shard_map/all_to_all | solution.py:19
  22.8 0.0 copy-start.3
  22.8 1.3 %copy.17 = bf16[4,512,256]{1,2,0:T(8,128)(2,1)} copy(bf16[4,512,256]{2,1,0:T(8,128)(2,1)S(1)} %all_to_all.15) | data formatting | bytes 2097152 | tf_op jit(solution)/shard_map/all_to_all | solution.py:19
  24.1 1.9 %collective-permute-start = (bf16[4,512,256]{1,2,0:T(8,128)(2,1)}, bf16[4,512,256]{1,2,0:T(8,128)(2,1)S(1)}, u32[]{:S(2)}, u32[]{:S(2)}) collective-permute-start(bf16[4,512,256]{1,2,0:T(8,128)(2,1)} %copy.17), channel_id=1, source_target_pairs={{0,1},{1,0},{2,3},{3,2},{4,5},{5,4},{6,7},{7,6},{8,9},{9,8},{10,11... | collective-permute-start | bytes 3145736 | tf_op jit(solution)/shard_map/ppermute | solution.py:20
  26.0 0.1 copy.22
  26.1 0.0 copy-done.3
  26.2 0.5 fusion.7
  26.7 2.2 %collective-permute-done = bf16[4,512,256]{1,2,0:T(8,128)(2,1)S(1)} collective-permute-done((bf16[4,512,256]{1,2,0:T(8,128)(2,1)}, bf16[4,512,256]{1,2,0:T(8,128)(2,1)S(1)}, u32[]{:S(2)}, u32[]{:S(2)}) %collective-permute-start) | collective-permute-done | bytes 1048608 | tf_op jit(solution)/shard_map/ppermute | solution.py:20
  28.9 0.0 copy-start.1
  28.9 1.0 copy-done.1
  29.9 0.5 fusion.8
  30.4 0.1 pad_maximum_fusion
  30.5 46.1 %all_to_all.16 = bf16[64,8,1024]{2,1,0:T(8,128)(2,1)} all-to-all(bf16[64,8,1024]{2,1,0:T(8,128)(2,1)S(1)} %bitcast.63), channel_id=1, replica_groups=mesh['z'=8,'y'=8,'x'=4,'core'=2] {'z','y'}, dimensions={0} | all-to-all | bytes 2097152 | tf_op jit(solution)/shard_map/all_to_all | solution.py:35
  76.6 1.4 %reduce_sum.12 = bf16[8,1024]{1,0:T(8,128)(2,1)S(1)} reduce(bf16[64,8,1024]{2,1,0:T(8,128)(2,1)} %all_to_all.16, bf16[]{:T(256)} %constant.3.clone.1), dimensions={0}, to_apply=%region_0.1 | reduce | flops 516096 | bytes 1064962 | tf_op jit(solution)/shard_map/reduce_sum | solution.py:36
  78.0 0.0 copy-start.6
  78.0 0.0 copy-start.7
  78.0 1.1 broadcast_in_dim.5
  79.1 7.2 %all-to-all-start.2 = ((bf16[64,8,1024]{2,1,0:T(8,128)(2,1)}), bf16[64,8,1024]{2,1,0:T(8,128)(2,1)}, u32[]{:S(2)}, u32[]{:S(2)}) async-start(bf16[64,8,1024]{2,1,0:T(8,128)(2,1)} %broadcast_in_dim.5), calls=%async_computation.2 | async-start | bytes 2097152 | tf_op jit(solution)/shard_map/all_to_all | solution.py:37
  86.3 1.0 copy.14
  87.3 0.0 copy-done.6
  87.3 0.2 rev.3
  87.6 0.0 copy-done.7
  87.6 0.1 add_divide_fusion
  87.7 1.8 %copy.16 = bf16[512,4,256]{2,1,0:T(4,128)(2,1)} copy(bf16[512,4,256]{2,0,1:T(8,128)(2,1)S(1)} %bitcast.57) | data formatting | bytes 2097152 | tf_op jit(solution)/shard_map/transpose | solution.py:22
  89.5 2.6 %reshape.50 = bf16[512,1024,1]{1,0,2:T(8,128)(2,1)} reshape(bf16[512,4,256]{2,1,0:T(4,128)(2,1)} %copy.16) | data formatting | bytes 2097152 | tf_op jit(solution)/shard_map/reshape | solution.py:22
  92.0 0.0 copy-start.2
  92.1 1.6 %convert_multiply_fusion.1 = f32[512,4,256]{0,2,1:T(8,128)S(1)} fusion(bf16[4,512,256]{1,2,0:T(8,128)(2,1)} %copy.17), kind=kLoop, calls=%fused_computation.7 | loop fusion | flops 1048576 | bytes 3145728 | tf_op jit(solution)/shard_map/mul | solution.py:45
  93.7 1.1 fusion.13
  94.7 0.0 copy-done.2
  94.8 0.3 convert_multiply_fusion
  95.0 1.1 fusion.10
  96.1 18.6 %all-to-all-done.2 = bf16[64,8,1024]{2,1,0:T(8,128)(2,1)} async-done(((bf16[64,8,1024]{2,1,0:T(8,128)(2,1)}), bf16[64,8,1024]{2,1,0:T(8,128)(2,1)}, u32[]{:S(2)}, u32[]{:S(2)}) %all-to-all-start.2) | async-done | bytes 1048608 | tf_op jit(solution)/shard_map/all_to_all | solution.py:37
  114.8 0.0 copy-start.4
  114.8 1.5 %fusion.11 = (f32[256,1024]{1,0:T(8,128)S(1)}, f32[256,1024]{1,0:T(8,128)S(1)}) fusion(bf16[64,8,1024]{2,1,0:T(8,128)(2,1)} %all-to-all-done.2), kind=kLoop, calls=%fused_computation.22 | loop fusion | flops 524288 | bytes 3145728 | tf_op jit(solution)/shard_map/convert_element_type | solution.py:47
  116.3 0.0 copy-done.4
  116.3 0.0 copy-start.5
  116.3 1.3 %fusion = f32[4,256,512]{2,1,0:T(8,128)S(1)} fusion(bf16[512,1024,1]{1,0,2:T(8,128)(2,1)S(1)} %copy-done.4, f32[256,1024]{1,0:T(8,128)S(1)} %get-tuple-element.6, f32[4,1024]{1,0:T(4,128)S(1)} %get-tuple-element.8), kind=kOutput, calls=%fused_computation.2 | convolution fusion | flops 1075838976 | bytes 4210688 | tf_op jit(solution)/shard_map/np,ltp->lnt/dot_general | solution.py:48
  117.6 0.0 copy-done.5
  117.6 2.6 %fusion.2 = f32[4,512,256]{1,2,0:T(8,128)} fusion(f32[4,256,512]{2,1,0:T(8,128)S(1)} %fusion, bf16[512,1024,1]{0,1,2:T(8,128)(2,1)S(1)} %bitcast.61, f32[256,1024]{1,0:T(8,128)S(1)} %get-tuple-element.5, f32[4,1024]{1,0:T(4,128)S(1)} %get-tuple-element.7, f32[4,512]{1,0:T(4,128)S(1)} %fusion.10, f32[512,256]{0,1:T(8,128)S(1)} %copy-done.5), kind=kOutput, calls=%fused_computation.5 | convolution fusion | flops 1077411840 | bytes 6840320 | tf_op jit(solution)/shard_map/np,ltp->lnt/dot_general | solution.py:48
  120.2 2.9 %copy.19 = f32[4,512,256]{2,1,0:T(8,128)} copy(f32[4,512,256]{1,2,0:T(8,128)} %fusion.2) | data formatting | bytes 4194304 | tf_op jit(solution)/shard_map/div | solution.py:50
  (4 shorter events, 0.0 us)
Async XLA Ops:
  0.0 1.6 %copy-start = (bf16[512,2048]{1,0:T(8,128)(2,1)S(1)}, bf16[512,2048]{1,0:T(8,128)(2,1)}, u32[]{:S(2)}) copy-start(bf16[512,2048]{1,0:T(8,128)(2,1)} %param.5) | copy-start | bytes 6291460
  22.8 3.4 %copy-start.3 = (bf16[512,256]{1,0:T(8,128)(2,1)S(1)}, bf16[512,256]{1,0:T(8,128)(2,1)}, u32[]{:S(2)}) copy-start(bf16[512,256]{1,0:T(8,128)(2,1)} %param.6) | copy-start | bytes 786436
  24.1 4.8 %collective-permute-start = (bf16[4,512,256]{1,2,0:T(8,128)(2,1)}, bf16[4,512,256]{1,2,0:T(8,128)(2,1)S(1)}, u32[]{:S(2)}, u32[]{:S(2)}) collective-permute-start(bf16[4,512,256]{1,2,0:T(8,128)(2,1)} %copy.17), channel_id=1, source_target_pairs={{0,1},{1,0},{2,3},{3,2},{4,5},{5,4},{6,7},{7,6},{8,9},{9,8},{10,11... | collective-permute-start | bytes 3145736 | tf_op jit(solution)/shard_map/ppermute | solution.py:20
  28.9 1.0 copy-start.1
  78.0 9.3 %copy-start.6 = (f32[2048]{0:T(1024)S(1)}, f32[2048]{0:T(1024)}, u32[]{:S(2)}) copy-start(f32[2048]{0:T(1024)} %param.8) | copy-start | bytes 24580
  78.0 9.6 %copy-start.7 = (f32[4]{0:T(128)S(1)}, f32[4]{0:T(128)}, u32[]{:S(2)}) copy-start(f32[4]{0:T(128)} %param.9) | copy-start | bytes 52
  79.1 35.6 %all-to-all-start.2 = ((bf16[64,8,1024]{2,1,0:T(8,128)(2,1)}), bf16[64,8,1024]{2,1,0:T(8,128)(2,1)}, u32[]{:S(2)}, u32[]{:S(2)}) async-start(bf16[64,8,1024]{2,1,0:T(8,128)(2,1)} %broadcast_in_dim.5), calls=%async_computation.2 | async-start | bytes 2097152 | tf_op jit(solution)/shard_map/all_to_all | solution.py:37
  92.0 2.7 %copy-start.2 = (bf16[4,512,256]{1,2,0:T(8,128)(2,1)S(1)}, bf16[4,512,256]{1,2,0:T(8,128)(2,1)}, u32[]{:S(2)}) copy-start(bf16[4,512,256]{1,2,0:T(8,128)(2,1)} %copy-done.1) | copy-start | bytes 3145732
  114.8 1.5 %copy-start.4 = (bf16[512,1024,1]{1,0,2:T(8,128)(2,1)S(1)}, bf16[512,1024,1]{1,0,2:T(8,128)(2,1)}, u32[]{:S(2)}) copy-start(bf16[512,1024,1]{1,0,2:T(8,128)(2,1)} %reshape.50) | copy-start | bytes 3145732
  116.3 1.3 %copy-start.5 = (f32[512,256]{0,1:T(8,128)S(1)}, f32[512,256]{0,1:T(8,128)}, u32[]{:S(2)}) copy-start(f32[512,256]{0,1:T(8,128)} %copy.14) | copy-start | bytes 1572868

commit v2 on v0

v2 whole, which is shorter than its diff:
```python
import jax
import jax.numpy as jnp
from jax import lax
from jax.experimental import pallas as pl
from jax.experimental.pallas import tpu as pltpu
from jax.sharding import Mesh, PartitionSpec as P

SAMP = ("z", "y")
TRAIT = ("x", "core")
MIB = 1 << 20


def whole(*shape):
    return pl.BlockSpec(shape, lambda *_: (0,) * len(shape))


def call(body, out, grid, in_specs, out_specs, flops, moved, vmem, scratch=()):
    return pl.pallas_call(
        body,
        out_shape=out,
        grid=grid,
        in_specs=in_specs,
        out_specs=out_specs,
        scratch_shapes=list(scratch),
        compiler_params=pltpu.CompilerParams(vmem_limit_bytes=vmem * MIB),
        cost_estimate=pl.CostEstimate(flops=flops, bytes_accessed=moved, transcendentals=0),
    )


def own_body(samples, whitening, out):
    block = jnp.dot(samples[...], whitening[...], preferred_element_type=jnp.float32)
    out[...] = jnp.broadcast_to(block.astype(jnp.bfloat16)[None], out.shape)


def partial_body(traits, mine, other, out):
    flipped = traits[...].T
    n_x, _, depth = mine.shape
    groups = out.shape[0] // 2
    for half, source in enumerate((mine, other)):
        for j in range(n_x):
            piece = jnp.dot(flipped, source[j], preferred_element_type=jnp.float32)
            out[half * groups : (half + 1) * groups, :, j * depth : (j + 1) * depth] = (
                piece.astype(jnp.bfloat16).reshape(groups, -1, depth)
            )


def sum_body(arrived, out):
    total = arrived[0].astype(jnp.float32)
    for i in range(1, arrived.shape[0]):
        total = total + arrived[i].astype(jnp.float32)
    total = total.astype(jnp.bfloat16)
    for i in range(out.shape[0]):
        out[i] = total


def leverage_body(core, lambdas, squared, mine, other, joined, inverse):
    n_x, rows, depth = mine.shape
    n_l = inverse.shape[0]
    step = 128
    sums = [jnp.zeros((rows, step), jnp.float32) for _ in range(n_l)]
    for half, source in enumerate((mine, other)):
        line = squared[pl.ds(lax.rem(core[0] + half, 2), 1), :]
        for j in range(n_x):
            for at in range(0, depth, step):
                here = j * depth + at
                value = source[j, :, at : at + step]
                start = half * n_x * depth + here
                joined[:, start : start + step] = value
                wide = value.astype(jnp.float32)
                wide = wide * wide
                top = line[:, here : here + step]
                for l in range(n_l):
                    sums[l] = sums[l] + wide * (top / (top + lambdas[l]))
    for l in range(n_l):
        level = jnp.sum(sums[l], axis=1, keepdims=True)
        inverse[l] = 1.0 / jnp.maximum(1.0 - level, 0.25)


def fitted_body(core, lambdas, squared, joined, projected, traits, inverse, out, scaled):
    l = pl.program_id(0)
    groups = projected.shape[0] // 2
    span = projected.shape[2]
    for half in range(2):
        top = squared[pl.ds(lax.rem(core[0] + half, 2), 1), :]
        shrink = top / (top + lambdas[l])
        values = projected[half * groups : (half + 1) * groups].reshape(-1, span)
        scaled[:, half * span : (half + 1) * span] = (
            values.astype(jnp.float32) * shrink
        ).astype(jnp.bfloat16)
    fitted = lax.dot_general(
        joined[...], scaled[...], (((1,), (1,)), ((), ())), preferred_element_type=jnp.float32
    )
    out[0] = (traits[...].astype(jnp.float32) - fitted) * inverse[0]


def local(samples, traits, whitening, singular, lambdas):
    features, depth = whitening.shape
    rows, width = traits.shape
    n_x, n_core = lax.axis_size("x"), lax.axis_size("core")
    n_samp = lax.axis_size("z") * lax.axis_size("y")
    n_l = lambdas.shape[0]
    span = n_x * depth
    every = n_core * span
    bf16, f32 = jnp.bfloat16, jnp.float32
    core = lax.axis_index("core").astype(jnp.int32).reshape(1)
    squared = jnp.moveaxis((singular * singular).reshape(n_x, n_core, depth), 1, 0)
    squared = squared.reshape(n_core, span)
    scalar = pl.BlockSpec(memory_space=pltpu.SMEM)

    block = 128
    own = call(
        own_body,
        jax.ShapeDtypeStruct((n_x, rows, depth), bf16),
        (rows // block,),
        [pl.BlockSpec((block, features), lambda i: (i, 0)), whole(features, depth)],
        pl.BlockSpec((n_x, block, depth), lambda i: (0, i, 0)),
        2 * rows * features * depth,
        2 * (rows * features + features * depth + n_x * rows * depth),
        12,
    )(samples, whitening)
    mine = lax.all_to_all(own, "x", 0, 0)
    other = lax.ppermute(mine, "core", [(0, 1), (1, 0)])

    pieces = (n_samp, n_core * width // n_samp, span)
    partial = call(
        partial_body,
        jax.ShapeDtypeStruct(pieces, bf16),
        (1,),
        [whole(rows, width), whole(n_x, rows, depth), whole(n_x, rows, depth)],
        whole(*pieces),
        2 * rows * width * every,
        2 * (rows * width + rows * every + every * width),
        16,
    )(traits, mine, other)
    arrived = lax.all_to_all(partial, SAMP, 0, 0)
    total = call(
        sum_body,
        jax.ShapeDtypeStruct(pieces, bf16),
        (1,),
        [whole(*pieces)],
        whole(*pieces),
        every * width,
        4 * every * width,
        8,
    )(arrived)
    projected = lax.all_to_all(total, SAMP, 0, 0)

    joined, inverse = call(
        leverage_body,
        (
            jax.ShapeDtypeStruct((rows, every), bf16),
            jax.ShapeDtypeStruct((n_l, rows, 1), f32),
        ),
        (rows // block,),
        [
            scalar,
            scalar,
            whole(n_core, span),
            pl.BlockSpec((n_x, block, depth), lambda i: (0, i, 0)),
            pl.BlockSpec((n_x, block, depth), lambda i: (0, i, 0)),
        ],
        (
            pl.BlockSpec((block, every), lambda i: (i, 0)),
            pl.BlockSpec((n_l, block, 1), lambda i: (0, i, 0)),
        ),
        10 * rows * every,
        4 * rows * every,
        16,
    )(core, lambdas, squared, mine, other)
    return call(
        fitted_body,
        jax.ShapeDtypeStruct((n_l, rows, width), f32),
        (n_l,),
        [
            scalar,
            scalar,
            whole(n_core, span),
            whole(rows, every),
            whole(*pieces),
            whole(rows, width),
            pl.BlockSpec((1, rows, 1), lambda l: (l, 0, 0)),
        ],
        pl.BlockSpec((1, rows, width), lambda l: (l, 0, 0)),
        2 * n_l * rows * every * width,
        2 * rows * every + 2 * every * width + 4 * n_l * rows * width,
        16,
        [pltpu.VMEM((width, every), bf16)],
    )(core, lambdas, squared, joined, projected, traits, inverse)


def solution(mesh):
    split = Mesh(mesh.devices.reshape(8, 8, 4, 2), SAMP + TRAIT)
    return jax.shard_map(
        local,
        mesh=split,
        in_specs=(P(SAMP, None), P(SAMP, TRAIT), P(None, TRAIT), P(), P()),
        out_specs=P(None, SAMP, TRAIT),
        check_vma=False,
    )
```

time: 374 us -> 119 us (0.32)
  the two profiles are of different devices: /device:TPU:4 before, /device:TPU:8 now
where the time goes in v2:
time: 119 us
  blocking collectives  65.3 us (55%)
  waiting for transfers between devices  25.8 us (22%)
  Pallas kernels  10.8 us (9%)
  starting transfers between devices  8.94 us (8%)
  local copies, waits for them, and re-layouts  7.97 us (7%)
    all_to_all x1, blocking collectives, local(): arrived = lax.all_to_all(partial, SAMP, 0, 0)  46 us
    all_to_all x1, waiting for transfers between devices, local(): projected = lax.all_to_all(total, SAMP, 0, 0)  23.2 us
    all_to_all x1, blocking collectives, local(): mine = lax.all_to_all(own, 'x', 0, 0)  19.3 us
    unnamed x18, local copies, waits for them, and re-layouts  7.96 us
    all_to_all x1, starting transfers between devices, local(): projected = lax.all_to_all(total, SAMP, 0, 0)  7.03 us
    pallas_call x1, Pallas kernels, local(): call(fitted_body, jax.ShapeDtypeStruct((n_l, rows, width), f32), (n_l,),...  4.6 us
    pallas_call x1, Pallas kernels, local(): call(leverage_body, (jax.ShapeDtypeStruct((rows, every), bf16), jax.Shape...  2.91 us
    ppermute x1, waiting for transfers between devices, local(): other = lax.ppermute(mine, 'core', [(0, 1), (1, 0)])  2.63 us
  transfers between devices with their start and end apart: 2, of which 2 were waited for; matrix products, arithmetic and copies ran while one was open for 0% of the time, Pallas kernels for 2%

profile of v2, /device:TPU:8, one launch (start us, length us, event | category | flops | bytes accessed | tf_op | source)
XLA Modules:
  0.0 119.0 jit_solution(3411675356706932212)
XLA Ops:
  0.0 0.0 copy-start
  0.0 1.6 %copy-done = bf16[512,2048]{1,0:T(8,128)(2,1)S(1)} copy-done((bf16[512,2048]{1,0:T(8,128)(2,1)S(1)}, bf16[512,2048]{1,0:T(8,128)(2,1)}, u32[]{:S(2)}) %copy-start) | copy-done | bytes 2097176
  1.6 0.0 copy-start.1
  1.6 1.2 %copy-done.1 = bf16[2048,256]{1,0:T(8,128)(2,1)S(1)} copy-done((bf16[2048,256]{1,0:T(8,128)(2,1)S(1)}, bf16[2048,256]{1,0:T(8,128)(2,1)}, u32[]{:S(2)}) %copy-start.1) | copy-done | bytes 1048600
  2.8 1.3 %shard_map.55 = bf16[4,512,256]{2,1,0:T(8,128)(2,1)S(1)} custom-call(bf16[512,2048]{1,0:T(8,128)(2,1)S(1)} %copy-done, bf16[2048,256]{1,0:T(8,128)(2,1)S(1)} %copy-done.1), custom_call_target="tpu_custom_call" | custom-call | flops 536870912 | bytes 4194304 | tf_op jit(solution)/shard_map/pallas_call | solution.py:111
  4.2 0.0 copy-start.2
  4.2 19.3 %all_to_all.15.mine = bf16[4,512,256]{2,1,0:T(8,128)(2,1)S(1)} all-to-all(bf16[4,512,256]{2,1,0:T(8,128)(2,1)S(1)} %shard_map.55), channel_id=1, replica_groups=mesh['z'=8,'y'=8,'x'=4,'core'=2] {'x'}, dimensions={0} | all-to-all | bytes 2097152 | tf_op jit(solution)/shard_map/all_to_all | solution.py:121
  23.5 1.9 %collective-permute-start = (bf16[4,512,256]{2,1,0:T(8,128)(2,1)S(1)}, bf16[4,512,256]{2,1,0:T(8,128)(2,1)S(1)}, u32[]{:S(2)}, u32[]{:S(2)}) collective-permute-start(bf16[4,512,256]{2,1,0:T(8,128)(2,1)S(1)} %all_to_all.15.mine), channel_id=1, source_target_pairs={{0,1},{1,0},{2,3},{3,2},{4,5},{5,4},{6,7},{7,6},{8,9},{9,8},{10,11... | collective-permute-start | bytes 3145736 | tf_op jit(solution)/shard_map/ppermute | solution.py:122
  25.4 2.6 %collective-permute-done.other = bf16[4,512,256]{2,1,0:T(8,128)(2,1)S(1)} collective-permute-done((bf16[4,512,256]{2,1,0:T(8,128)(2,1)S(1)}, bf16[4,512,256]{2,1,0:T(8,128)(2,1)S(1)}, u32[]{:S(2)}, u32[]{:S(2)}) %collective-permute-start) | collective-permute-done | bytes 1048608 | tf_op jit(solution)/shard_map/ppermute | solution.py:122
  28.0 0.0 copy-done.2
  28.0 0.7 shard_map.57
  28.8 46.0 %all_to_all.16.arrived = bf16[64,8,1024]{2,1,0:T(8,128)(2,1)S(1)} all-to-all(bf16[64,8,1024]{2,1,0:T(8,128)(2,1)S(1)} %shard_map.57), channel_id=1, replica_groups=mesh['z'=8,'y'=8,'x'=4,'core'=2] {'z','y'}, dimensions={0} | all-to-all | bytes 2097152 | tf_op jit(solution)/shard_map/all_to_all | solution.py:135
  74.8 0.0 copy-start.8
  74.8 0.0 copy-start.3
  74.8 1.2 %shard_map.58 = bf16[64,8,1024]{2,1,0:T(8,128)(2,1)} custom-call(bf16[64,8,1024]{2,1,0:T(8,128)(2,1)S(1)} %all_to_all.16.arrived), custom_call_target="tpu_custom_call" | custom-call | flops 524288 | bytes 2097152 | tf_op jit(solution)/shard_map/pallas_call | solution.py:136
  76.0 7.0 %all-to-all-start.2 = ((bf16[64,8,1024]{2,1,0:T(8,128)(2,1)}), bf16[64,8,1024]{2,1,0:T(8,128)(2,1)S(1)}, u32[]{:S(2)}, u32[]{:S(2)}) async-start(bf16[64,8,1024]{2,1,0:T(8,128)(2,1)} %shard_map.58), calls=%async_computation.2 | async-start | bytes 2097152 | tf_op jit(solution)/shard_map/all_to_all | solution.py:146
  83.1 0.0 copy-done.8
  83.1 0.0 copy-done.3
  83.1 2.9 %shard_map.56 = (bf16[512,2048]{1,0:T(8,128)(2,1)S(1)}, f32[4,512,1]{2,1,0:T(8,128)S(1)}) custom-call(s32[1]{0:T(128)} %bitcast.core, f32[4]{0:T(128)S(1)} %copy-done.3, f32[2,1024]{1,0:T(2,128)S(1)} %bitcast.4, bf16[4,512,256]{2,1,0:T(8,128)(2,1)S(1)} %all_to_all.15.mine, bf16[4,512,256]{2,1,0:T(8,128)(2,1)S(1)} %collective-permute-done.other), custom_call_target="tpu_custom_call" | custom-call | flops 10485760 | bytes 4194304 | tf_op jit(solution)/shard_map/pallas_call | solution.py:148
  86.0 0.0 copy-start.4
  86.0 1.3 %copy-done.4 = bf16[512,2048]{1,0:T(8,128)(2,1)} copy-done((bf16[512,2048]{1,0:T(8,128)(2,1)}, bf16[512,2048]{1,0:T(8,128)(2,1)S(1)}, u32[]{:S(2)}) %copy-start.4) | copy-done | bytes 2097176
  87.3 0.0 copy-start.6
  87.3 1.0 copy-done.6
  88.3 23.2 %all-to-all-done.2.projected = bf16[64,8,1024]{2,1,0:T(8,128)(2,1)S(1)} async-done(((bf16[64,8,1024]{2,1,0:T(8,128)(2,1)}), bf16[64,8,1024]{2,1,0:T(8,128)(2,1)S(1)}, u32[]{:S(2)}, u32[]{:S(2)}) %all-to-all-start.2) | async-done | bytes 1048608 | tf_op jit(solution)/shard_map/all_to_all | solution.py:146
  111.6 0.0 copy-start.5
  111.6 1.6 %copy-done.5 = bf16[512,2048]{1,0:T(8,128)(2,1)S(1)} copy-done((bf16[512,2048]{1,0:T(8,128)(2,1)S(1)}, bf16[512,2048]{1,0:T(8,128)(2,1)}, u32[]{:S(2)}) %copy-start.5) | copy-done | bytes 2097176
  113.1 0.0 copy-start.7
  113.1 1.2 %copy-done.7 = f32[4,512,1]{2,1,0:T(8,128)S(1)} copy-done((f32[4,512,1]{2,1,0:T(8,128)S(1)}, f32[4,512,1]{2,1,0:T(8,128)}, u32[]{:S(2)}) %copy-start.7) | copy-done | bytes 8216
  114.4 4.6 %shard_map.59 = f32[4,512,256]{2,1,0:T(8,128)} custom-call(s32[1]{0:T(128)} %bitcast.core, f32[4]{0:T(128)S(1)} %copy-done.3, f32[2,1024]{1,0:T(2,128)S(1)} %bitcast.5, bf16[512,2048]{1,0:T(8,128)(2,1)S(1)} %copy-done.5, bf16[64,8,1024]{2,1,0:T(8,128)(2,1)S(1)} %all-to-all-done.2.projected, bf16[512,256]{1,0:T(8,128)(2,1)S(1)} %copy-done.2, ...), custom_call_target="tpu_custom_call" | custom-call | flops 2147483648 | bytes 5242880 | tf_op jit(solution)/shard_map/pallas_call | solution.py:170
  (2 shorter events, 0.0 us)
Async XLA Ops:
  0.0 1.6 %copy-start = (bf16[512,2048]{1,0:T(8,128)(2,1)S(1)}, bf16[512,2048]{1,0:T(8,128)(2,1)}, u32[]{:S(2)}) copy-start(bf16[512,2048]{1,0:T(8,128)(2,1)} %samples.1) | copy-start | bytes 6291460
  1.6 1.2 %copy-start.1 = (bf16[2048,256]{1,0:T(8,128)(2,1)S(1)}, bf16[2048,256]{1,0:T(8,128)(2,1)}, u32[]{:S(2)}) copy-start(bf16[2048,256]{1,0:T(8,128)(2,1)} %whitening.1) | copy-start | bytes 3145732
  4.2 23.9 %copy-start.2 = (bf16[512,256]{1,0:T(8,128)(2,1)S(1)}, bf16[512,256]{1,0:T(8,128)(2,1)}, u32[]{:S(2)}) copy-start(bf16[512,256]{1,0:T(8,128)(2,1)} %traits.3) | copy-start | bytes 786436
  23.5 4.5 %collective-permute-start = (bf16[4,512,256]{2,1,0:T(8,128)(2,1)S(1)}, bf16[4,512,256]{2,1,0:T(8,128)(2,1)S(1)}, u32[]{:S(2)}, u32[]{:S(2)}) collective-permute-start(bf16[4,512,256]{2,1,0:T(8,128)(2,1)S(1)} %all_to_all.15.mine), channel_id=1, source_target_pairs={{0,1},{1,0},{2,3},{3,2},{4,5},{5,4},{6,7},{7,6},{8,9},{9,8},{10,11... | collective-permute-start | bytes 3145736 | tf_op jit(solution)/shard_map/ppermute | solution.py:122
  74.8 8.3 %copy-start.8 = (f32[2048]{0:T(1024)S(1)}, f32[2048]{0:T(1024)}, u32[]{:S(2)}) copy-start(f32[2048]{0:T(1024)} %param.8) | copy-start | bytes 24580
  74.8 8.3 %copy-start.3 = (f32[4]{0:T(128)S(1)}, f32[4]{0:T(128)}, u32[]{:S(2)}) copy-start(f32[4]{0:T(128)} %lambdas.3) | copy-start | bytes 52
  76.0 35.5 %all-to-all-start.2 = ((bf16[64,8,1024]{2,1,0:T(8,128)(2,1)}), bf16[64,8,1024]{2,1,0:T(8,128)(2,1)S(1)}, u32[]{:S(2)}, u32[]{:S(2)}) async-start(bf16[64,8,1024]{2,1,0:T(8,128)(2,1)} %shard_map.58), calls=%async_computation.2 | async-start | bytes 2097152 | tf_op jit(solution)/shard_map/all_to_all | solution.py:146
  86.0 1.3 %copy-start.4 = (bf16[512,2048]{1,0:T(8,128)(2,1)}, bf16[512,2048]{1,0:T(8,128)(2,1)S(1)}, u32[]{:S(2)}) copy-start(bf16[512,2048]{1,0:T(8,128)(2,1)S(1)} %get-tuple-element.7.joined) | copy-start | bytes 6291460
  87.3 1.0 copy-start.6
  111.6 1.6 %copy-start.5 = (bf16[512,2048]{1,0:T(8,128)(2,1)S(1)}, bf16[512,2048]{1,0:T(8,128)(2,1)}, u32[]{:S(2)}) copy-start(bf16[512,2048]{1,0:T(8,128)(2,1)} %copy-done.4) | copy-start | bytes 6291460
  113.1 1.2 %copy-start.7 = (f32[4,512,1]{2,1,0:T(8,128)S(1)}, f32[4,512,1]{2,1,0:T(8,128)}, u32[]{:S(2)}) copy-start(f32[4,512,1]{2,1,0:T(8,128)} %copy-done.6) | copy-start | bytes 24580

commit v3 on v0

v3 whole, which is shorter than its diff:
```python
import jax
import jax.numpy as jnp
from jax import lax
from jax.experimental import pallas as pl
from jax.experimental.pallas import tpu as pltpu
from jax.sharding import Mesh, PartitionSpec as P


SAMP = ("z", "y")
TRAIT = ("x", "core")
FULL = 67043328
SMALL = 8 << 20
EARLY = ((0, 0), (0, 1), (1, 0), (3, 0))
LATE = ((1, 1), (3, 1), (2, 0), (2, 1))
HBM = pl.BlockSpec(memory_space=pltpu.HBM)
SCALAR = pl.BlockSpec(memory_space=pltpu.SMEM)


def whole(*shape):
    return pl.BlockSpec(shape, lambda *_: (0,) * len(shape))


def call(body, out, in_specs, out_specs, flops, moved, vmem, scratch=(), grid=(1,)):
    return pl.pallas_call(
        body,
        out_shape=out,
        grid=grid,
        in_specs=in_specs,
        out_specs=out_specs,
        scratch_shapes=list(scratch),
        compiler_params=pltpu.CompilerParams(vmem_limit_bytes=vmem),
        cost_estimate=pl.CostEstimate(flops=flops, bytes_accessed=moved, transcendentals=0),
    )


def cross_body(samples, traits, out, samples_v, traits_v, sems):
    n = samples_v.shape[0]
    _, cols = samples_v.shape[1:]
    copies = [pltpu.make_async_copy(traits, traits_v, sems.at[n])]
    for i in range(n):
        copies.append(
            pltpu.make_async_copy(
                samples.at[:, i * cols : (i + 1) * cols], samples_v.at[i], sems.at[i]
            )
        )
    for copy in copies:
        copy.start()
    copies[0].wait()
    flipped = traits_v[...].T
    span = out.shape[2]
    groups = out.shape[0] // 2
    for i in range(n):
        copies[i + 1].wait()
        piece = jnp.dot(flipped, samples_v[i], preferred_element_type=jnp.float32)
        half, at = divmod(i * cols, span)
        out[half * groups : (half + 1) * groups, :, at : at + cols] = piece.astype(
            jnp.bfloat16
        ).reshape(groups, -1, cols)


def sum_body(arrived, out):
    total = arrived[0].astype(jnp.float32)
    for i in range(1, arrived.shape[0]):
        total = total + arrived[i].astype(jnp.float32)
    total = total.astype(jnp.bfloat16)
    for i in range(out.shape[0]):
        out[i] = total


def row_of(place, shift, swap):
    return lax.rem(place[0] + 4 - shift, 4) * 2 + lax.rem(place[1] + swap, 2)


def components_body(first, order, *refs):
    n = len(order)
    place, lambdas, squared, samples = refs[:4]
    blocks = refs[4 : 4 + n]
    before = () if first else (refs[4 + n],)
    out, level, samples_v, blocks_v, sems = refs[-5:]
    copies = [pltpu.make_async_copy(samples, samples_v, sems.at[n])]
    for i in range(n):
        copies.append(pltpu.make_async_copy(blocks[i], blocks_v.at[i], sems.at[i]))
    for copy in copies:
        copy.start()
    copies[0].wait()
    rows, depth = samples_v.shape[0], blocks_v.shape[2]
    n_l = level.shape[0]
    step = 128
    sums = [jnp.zeros((rows, step), jnp.float32) for _ in range(n_l)]
    for i, (shift, swap) in enumerate(order):
        copies[i + 1].wait()
        value = jnp.dot(samples_v[...], blocks_v[i], preferred_element_type=jnp.float32)
        value = value.astype(jnp.bfloat16)
        out[:, i * depth : (i + 1) * depth] = value
        wide = value.astype(jnp.float32)
        wide = wide * wide
        top = squared[pl.ds(row_of(place, shift, swap), 1), :]
        for l in range(n_l):
            shrink = top / (top + lambdas[l])
            for at in range(0, depth, step):
                sums[l] = sums[l] + wide[:, at : at + step] * shrink[:, at : at + step]
    for l in range(n_l):
        total = jnp.sum(sums[l], axis=1, keepdims=True)
        if first:
            level[l] = total
        else:
            level[l] = 1.0 / jnp.maximum(1.0 - (before[0][l] + total), 0.25)


def fitted_body(order, *refs):
    n = len(order)
    place, lambdas, squared, inverse, early, late, cross, traits = refs[:8]
    blocks = refs[8 : 8 + n]
    out, cross_v, early_v, late_v, traits_v, blocks_v, projected, scaled, sems = refs[-9:]
    l = pl.program_id(0)
    depth = blocks_v.shape[2]
    span = cross_v.shape[2]
    groups = cross_v.shape[0] // 2

    @pl.when(l == 0)
    def _():
        pairs = [(cross, cross_v)]
        pairs += [(blocks[i], blocks_v.at[i]) for i in range(n)]
        pairs += [(early, early_v), (late, late_v), (traits, traits_v)]
        copies = [
            pltpu.make_async_copy(source, target, sems.at[i])
            for i, (source, target) in enumerate(pairs)
        ]
        for copy in copies:
            copy.start()
        copies[0].wait()
        for i in range(n):
            copies[i + 1].wait()
            value = 0.0
            for half in range(2):
                value = value + jnp.dot(
                    cross_v[half * groups : (half + 1) * groups].reshape(-1, span),
                    blocks_v[i, half * span : (half + 1) * span, :],
                    preferred_element_type=jnp.float32,
                )
            projected[:, i * depth : (i + 1) * depth] = value.astype(jnp.bfloat16)
        for copy in copies[n + 1 :]:
            copy.wait()

    for i, (shift, swap) in enumerate(order):
        top = squared[pl.ds(row_of(place, shift, swap), 1), :]
        shrink = top / (top + lambdas[l])
        here = slice(i * depth, (i + 1) * depth)
        scaled[:, here] = (projected[:, here].astype(jnp.float32) * shrink).astype(jnp.bfloat16)
    contract = (((1,), (1,)), ((), ()))
    middle = early_v.shape[1]
    fitted = lax.dot_general(
        early_v[...], scaled[:, :middle], contract, preferred_element_type=jnp.float32
    ) + lax.dot_general(
        late_v[...], scaled[:, middle:], contract, preferred_element_type=jnp.float32
    )
    out[0] = (traits_v[...].astype(jnp.float32) - fitted) * inverse[0]


def compute(samples, traits, whitening, singular, lambdas):
    features, depth = whitening.shape
    rows, width = traits.shape
    n_x, n_core = lax.axis_size("x"), lax.axis_size("core")
    n_samp = lax.axis_size("z") * lax.axis_size("y")
    n_l = lambdas.shape[0]
    every = n_x * n_core * depth
    n_blocks = n_x * n_core
    bf16, f32 = jnp.bfloat16, jnp.float32
    place = jnp.stack([lax.axis_index("x"), lax.axis_index("core")]).astype(jnp.int32)
    squared = (singular * singular).reshape(n_blocks, depth)
    dma = pltpu.SemaphoreType.DMA

    pieces = (n_samp, 2 * width // n_samp, features // 2)
    partial = call(
        cross_body,
        jax.ShapeDtypeStruct(pieces, bf16),
        [HBM, HBM],
        whole(*pieces),
        2 * rows * width * features,
        2 * (rows * width + rows * features + features * width),
        FULL,
        [
            pltpu.VMEM((8, rows, features // 8), bf16),
            pltpu.VMEM((rows, width), bf16),
            dma((9,)),
        ],
    )(samples, traits)
    arrived = lax.all_to_all(partial, SAMP, 0, 0)

    shifts = {}
    for shift in (1, 3, 2):
        shifts[shift] = lax.ppermute(
            whitening, "x", [(i, (i + shift) % n_x) for i in range(n_x)]
        )
    blocks = {(0, 0): whitening}
    for shift in (0, 1, 3, 2):
        if shift:
            blocks[shift, 0] = shifts[shift]
        blocks[shift, 1] = lax.ppermute(blocks[shift, 0], "core", [(0, 1), (1, 0)])

    total = call(
        sum_body,
        jax.ShapeDtypeStruct(pieces, bf16),
        [whole(*pieces)],
        whole(*pieces),
        features * width,
        4 * features * width,
        SMALL,
    )(arrived)
    cross = lax.all_to_all(total, SAMP, 0, 0)

    def components(order, first, extra):
        n = len(order)
        return call(
            lambda *refs: components_body(first, order, *refs),
            (
                jax.ShapeDtypeStruct((rows, n * depth), bf16),
                jax.ShapeDtypeStruct((n_l, rows, 1), f32),
            ),
            [SCALAR, SCALAR, whole(n_blocks, depth)]
            + [HBM] * (n + 1)
            + [whole(n_l, rows, 1)] * (not first),
            (whole(rows, n * depth), whole(n_l, rows, 1)),
            2 * rows * features * n * depth,
            2 * (rows * features + features * n * depth + rows * n * depth),
            FULL,
            [
                pltpu.VMEM((rows, features), bf16),
                pltpu.VMEM((n, features, depth), bf16),
                dma((n + 1,)),
            ],
        )(place, lambdas, squared, samples, *[blocks[b] for b in order], *extra)

    early, level = components(EARLY, True, ())
    late, inverse = components(LATE, False, (level,))

    order = EARLY + LATE
    return call(
        lambda *refs: fitted_body(order, *refs),
        jax.ShapeDtypeStruct((n_l, rows, width), f32),
        [
            SCALAR,
            SCALAR,
            whole(n_blocks, depth),
            pl.BlockSpec((1, rows, 1), lambda l: (l, 0, 0)),
        ]
        + [HBM] * (n_blocks + 4),
        pl.BlockSpec((1, rows, width), lambda l: (l, 0, 0)),
        2 * n_l * rows * every * width,
        2 * rows * every + 2 * every * width + 4 * n_l * rows * width,
        FULL,
        [
            pltpu.VMEM(pieces, bf16),
            pltpu.VMEM((rows, every // 2), bf16),
            pltpu.VMEM((rows, every // 2), bf16),
            pltpu.VMEM((rows, width), bf16),
            pltpu.VMEM((n_blocks, features, depth), bf16),
            pltpu.VMEM((width, every), bf16),
            pltpu.VMEM((width, every), bf16),
            dma((n_blocks + 4,)),
        ],
        grid=(n_l,),
    )(
        place, lambdas, squared, inverse, early, late, cross, traits,
        *[blocks[b] for b in order],
    )


def solution(mesh):
    split = Mesh(mesh.devices.reshape(8, 8, 4, 2), SAMP + TRAIT)
    return jax.shard_map(
        compute,
        mesh=split,
        in_specs=(P(SAMP, None), P(SAMP, TRAIT), P(None, TRAIT), P(), P()),
        out_specs=P(None, SAMP, TRAIT),
        check_vma=False,
    )
```

time: 374 us -> 111 us (0.30)
  the two profiles are of different devices: /device:TPU:4 before, /device:TPU:1 now
where the time goes in v3:
time: 111 us; the launch traced here: 110 us
  starting transfers between devices  46.7 us (42%)
  Pallas kernels  36.8 us (33%)
  waiting for transfers between devices  25 us (23%)
    pallas_call x2, Pallas kernels, components(): call(lambda *refs: components_body(first, order, *refs), (jax.ShapeDtypeS...  18.6 us
    all_to_all x1, waiting for transfers between devices, compute(): arrived = lax.all_to_all(partial, SAMP, 0, 0)  17.5 us
    all_to_all x1, starting transfers between devices, compute(): arrived = lax.all_to_all(partial, SAMP, 0, 0)  17.3 us
    pallas_call x1, Pallas kernels, compute(): call(lambda *refs: fitted_body(order, *refs), jax.ShapeDtypeStruct((n_l,...  12.5 us
    ppermute x4, starting transfers between devices, compute(): blocks[shift, 1] = lax.ppermute(blocks[shift, 0], 'core', [(0, 1), (1, 0)])  11.4 us
    ppermute x3, starting transfers between devices, compute(): lax.ppermute(whitening, 'x', [(i, (i + shift) % n_x) for i in range(n_x)])  9.94 us
    all_to_all x1, starting transfers between devices, compute(): cross = lax.all_to_all(total, SAMP, 0, 0)  8.04 us
    ppermute x3, waiting for transfers between devices, compute(): lax.ppermute(whitening, 'x', [(i, (i + shift) % n_x) for i in range(n_x)])  7.46 us
  transfers between devices with their start and end apart: 9, of which 2 were waited for; matrix products, arithmetic and copies ran while one was open for 1% of the time, Pallas kernels for 18%

profile of v3, /device:TPU:1, one launch (start us, length us, event | category | flops | bytes accessed | tf_op | source)
XLA Modules:
  0.0 110.1 jit_solution(9112500987940284322)
XLA Ops:
  0.0 4.4 %shard_map.57 = bf16[64,8,1024]{2,1,0:T(8,128)(2,1)} custom-call(bf16[512,2048]{1,0:T(8,128)(2,1)} %samples.1, bf16[512,256]{1,0:T(8,128)(2,1)} %refs_7_.1), custom_call_target="tpu_custom_call" | custom-call | flops 536870912 | bytes 3407872 | tf_op jit(solution)/shard_map/pallas_call | solution.py:174
  4.4 0.0 copy-start
  4.4 17.3 %all-to-all-start = ((bf16[64,8,1024]{2,1,0:T(8,128)(2,1)}), bf16[64,8,1024]{2,1,0:T(8,128)(2,1)S(1)}, u32[]{:S(2)}, u32[]{:S(2)}) async-start(bf16[64,8,1024]{2,1,0:T(8,128)(2,1)} %shard_map.57), calls=%async_computation | async-start | bytes 2097152 | tf_op jit(solution)/shard_map/all_to_all | solution.py:188
  21.7 0.0 copy-done
  21.7 0.0 copy-start.1
  21.7 4.7 %collective-permute-start.4 = (bf16[2048,256]{1,0:T(8,128)(2,1)S(1)}, bf16[2048,256]{1,0:T(8,128)(2,1)}, u32[]{:S(2)}, u32[]{:S(2)}) collective-permute-start(bf16[2048,256]{1,0:T(8,128)(2,1)S(1)} %copy-done), channel_id=1, source_target_pairs={{0,4},{2,6},{4,0},{6,2},{1,5},{3,7},{5,1},{7,3},{8,12},{10,14},{12... | collective-permute-start | bytes 3145736 | tf_op jit(solution)/shard_map/ppermute | solution.py:192
  26.4 2.8 %collective-permute-start.2 = (bf16[2048,256]{1,0:T(8,128)(2,1)S(1)}, bf16[2048,256]{1,0:T(8,128)(2,1)}, u32[]{:S(2)}, u32[]{:S(2)}) collective-permute-start(bf16[2048,256]{1,0:T(8,128)(2,1)S(1)} %copy-done), channel_id=1, source_target_pairs={{0,6},{2,0},{4,2},{6,4},{1,7},{3,1},{5,3},{7,5},{8,14},{10,8},{12,... | collective-permute-start | bytes 3145736 | tf_op jit(solution)/shard_map/ppermute | solution.py:192
  29.2 2.5 %collective-permute-start = (bf16[2048,256]{1,0:T(8,128)(2,1)S(1)}, bf16[2048,256]{1,0:T(8,128)(2,1)}, u32[]{:S(2)}, u32[]{:S(2)}) collective-permute-start(bf16[2048,256]{1,0:T(8,128)(2,1)S(1)} %copy-done), channel_id=1, source_target_pairs={{0,2},{2,4},{4,6},{6,0},{1,3},{3,5},{5,7},{7,1},{8,10},{10,12},{12... | collective-permute-start | bytes 3145736 | tf_op jit(solution)/shard_map/ppermute | solution.py:192
  31.7 17.5 %all-to-all-done.arrived = bf16[64,8,1024]{2,1,0:T(8,128)(2,1)S(1)} async-done(((bf16[64,8,1024]{2,1,0:T(8,128)(2,1)}), bf16[64,8,1024]{2,1,0:T(8,128)(2,1)S(1)}, u32[]{:S(2)}, u32[]{:S(2)}) %all-to-all-start) | async-done | bytes 1048608 | tf_op jit(solution)/shard_map/all_to_all | solution.py:188
  49.2 1.3 %shard_map.58 = bf16[64,8,1024]{2,1,0:T(8,128)(2,1)} custom-call(bf16[64,8,1024]{2,1,0:T(8,128)(2,1)S(1)} %all-to-all-done.arrived), custom_call_target="tpu_custom_call" | custom-call | flops 524288 | bytes 2097152 | tf_op jit(solution)/shard_map/pallas_call | solution.py:201
  50.4 8.0 %all-to-all-start.1 = ((bf16[64,8,1024]{2,1,0:T(8,128)(2,1)}), bf16[64,8,1024]{2,1,0:T(8,128)(2,1)}, u32[]{:S(2)}, u32[]{:S(2)}) async-start(bf16[64,8,1024]{2,1,0:T(8,128)(2,1)} %shard_map.58), calls=%async_computation.1 | async-start | bytes 2097152 | tf_op jit(solution)/shard_map/all_to_all | solution.py:210
  58.5 3.9 %collective-permute-start.6 = (bf16[2048,256]{1,0:T(8,128)(2,1)S(1)}, bf16[2048,256]{1,0:T(8,128)(2,1)}, u32[]{:S(2)}, u32[]{:S(2)}) collective-permute-start(bf16[2048,256]{1,0:T(8,128)(2,1)S(1)} %copy-done), channel_id=1, source_target_pairs={{0,1},{1,0},{2,3},{3,2},{4,5},{5,4},{6,7},{7,6},{8,9},{9,8},{10,11... | collective-permute-start | bytes 3145736 | tf_op jit(solution)/shard_map/ppermute | solution.py:199
  62.3 0.0 collective-permute-done.4.refs_6_.refs_14_
  62.4 1.9 %collective-permute-start.5 = (bf16[2048,256]{1,0:T(8,128)(2,1)}, bf16[2048,256]{1,0:T(8,128)(2,1)}, u32[]{:S(2)}, u32[]{:S(2)}) collective-permute-start(bf16[2048,256]{1,0:T(8,128)(2,1)} %collective-permute-done.4.refs_6_.refs_14_), channel_id=1, source_target_pairs={{0,1},{1,0},{2,3},{3,2},{4,5},{5,4},{6,7},{7,6},{8,9},{9,8},{10,11... | collective-permute-start | bytes 3145736 | tf_op jit(solution)/shard_map/ppermute | solution.py:199
  64.3 7.5 %collective-permute-done.2.refs_7_.refs_11_ = bf16[2048,256]{1,0:T(8,128)(2,1)} collective-permute-done((bf16[2048,256]{1,0:T(8,128)(2,1)S(1)}, bf16[2048,256]{1,0:T(8,128)(2,1)}, u32[]{:S(2)}, u32[]{:S(2)}) %collective-permute-start.2) | collective-permute-done | bytes 1048608 | tf_op jit(solution)/shard_map/ppermute | solution.py:192
  71.7 3.6 %collective-permute-start.3 = (bf16[2048,256]{1,0:T(8,128)(2,1)}, bf16[2048,256]{1,0:T(8,128)(2,1)}, u32[]{:S(2)}, u32[]{:S(2)}) collective-permute-start(bf16[2048,256]{1,0:T(8,128)(2,1)} %collective-permute-done.2.refs_7_.refs_11_), channel_id=1, source_target_pairs={{0,1},{1,0},{2,3},{3,2},{4,5},{5,4},{6,7},{7,6},{8,9},{9,8},{10,11... | collective-permute-start | bytes 3145736 | tf_op jit(solution)/shard_map/ppermute | solution.py:199
  75.3 0.0 collective-permute-done.refs_6_.refs_10_
  75.3 2.1 %collective-permute-start.1 = (bf16[2048,256]{1,0:T(8,128)(2,1)}, bf16[2048,256]{1,0:T(8,128)(2,1)}, u32[]{:S(2)}, u32[]{:S(2)}) collective-permute-start(bf16[2048,256]{1,0:T(8,128)(2,1)} %collective-permute-done.refs_6_.refs_10_), channel_id=1, source_target_pairs={{0,1},{1,0},{2,3},{3,2},{4,5},{5,4},{6,7},{7,6},{8,9},{9,8},{10,11... | collective-permute-start | bytes 3145736 | tf_op jit(solution)/shard_map/ppermute | solution.py:199
  77.4 0.0 copy-done.1
  77.5 0.6 reshape.3.refs_2_
  78.1 0.7 pad_add_fusion.refs_0_
  78.7 0.0 collective-permute-done.6.refs_5_.refs_9_
  78.7 9.0 %shard_map.55 = (bf16[512,1024]{1,0:T(8,128)(2,1)}, f32[4,512,1]{2,1,0:T(8,128)}) custom-call(s32[2]{0:T(128)} %pad_add_fusion.refs_0_, f32[4]{0:T(128)} %refs_1_.5, f32[8,256]{1,0:T(8,128)} %reshape.3.refs_2_, bf16[512,2048]{1,0:T(8,128)(2,1)} %samples.1, bf16[2048,256]{1,0:T(8,128)(2,1)} %refs_8_.1, ...), custom_call_target="tpu_custom_call" | custom-call | flops 2147483648 | bytes 7340032 | tf_op jit(solution)/shard_map/pallas_call | solution.py:214
  87.7 0.0 collective-permute-done.5.refs_7_.refs_15_
  87.8 0.0 collective-permute-done.3.refs_5_.refs_13_
  87.8 0.0 collective-permute-done.1.refs_4_.refs_12_
  87.8 9.6 %shard_map.56 = (bf16[512,1024]{1,0:T(8,128)(2,1)}, f32[4,512,1]{2,1,0:T(8,128)}) custom-call(s32[2]{0:T(128)} %pad_add_fusion.refs_0_, f32[4]{0:T(128)} %refs_1_.5, f32[8,256]{1,0:T(8,128)} %reshape.3.refs_2_, bf16[512,2048]{1,0:T(8,128)(2,1)} %samples.1, bf16[2048,256]{1,0:T(8,128)(2,1)} %collective-permute-done.1.refs_4_.refs_12_, ...), custom_call_target="tpu_custom_call" | custom-call | flops 2147483648 | bytes 7340032 | tf_op jit(solution)/shard_map/pallas_call | solution.py:214
  97.4 0.0 all-to-all-done.1.refs_6_
  97.4 12.5 %shard_map.59 = f32[4,512,256]{2,1,0:T(8,128)} custom-call(s32[2]{0:T(128)} %pad_add_fusion.refs_0_, f32[4]{0:T(128)} %refs_1_.5, f32[8,256]{1,0:T(8,128)} %reshape.3.refs_2_, f32[4,512,1]{2,1,0:T(8,128)} %get-tuple-element.10.refs_3_, bf16[512,1024]{1,0:T(8,128)(2,1)} %get-tuple-element.11.refs_4_, bf16[512,1024]{1,0:T(8,128)(2,1)} %get-tuple-element.12.refs_5_, ...), custom_call_target="tpu_custom_call" | custom-call | flops 2147483648 | bytes 5242880 | tf_op jit(solution)/shard_map/pallas_call | solution.py:238
  (1 shorter events, 0.0 us)
Async XLA Ops:
  4.4 17.3 %copy-start = (bf16[2048,256]{1,0:T(8,128)(2,1)S(1)}, bf16[2048,256]{1,0:T(8,128)(2,1)}, u32[]{:S(2)}) copy-start(bf16[2048,256]{1,0:T(8,128)(2,1)} %refs_8_.1) | copy-start | bytes 3145732
  4.4 44.8 %all-to-all-start = ((bf16[64,8,1024]{2,1,0:T(8,128)(2,1)}), bf16[64,8,1024]{2,1,0:T(8,128)(2,1)S(1)}, u32[]{:S(2)}, u32[]{:S(2)}) async-start(bf16[64,8,1024]{2,1,0:T(8,128)(2,1)} %shard_map.57), calls=%async_computation | async-start | bytes 2097152 | tf_op jit(solution)/shard_map/all_to_all | solution.py:188
  21.7 55.7 %copy-start.1 = (f32[2048]{0:T(1024)S(1)}, f32[2048]{0:T(1024)}, u32[]{:S(2)}) copy-start(f32[2048]{0:T(1024)} %param.8) | copy-start | bytes 24580
  21.7 40.6 %collective-permute-start.4 = (bf16[2048,256]{1,0:T(8,128)(2,1)S(1)}, bf16[2048,256]{1,0:T(8,128)(2,1)}, u32[]{:S(2)}, u32[]{:S(2)}) collective-permute-start(bf16[2048,256]{1,0:T(8,128)(2,1)S(1)} %copy-done), channel_id=1, source_target_pairs={{0,4},{2,6},{4,0},{6,2},{1,5},{3,7},{5,1},{7,3},{8,12},{10,14},{12... | collective-permute-start | bytes 3145736 | tf_op jit(solution)/shard_map/ppermute | solution.py:192
  26.4 45.4 %collective-permute-start.2 = (bf16[2048,256]{1,0:T(8,128)(2,1)S(1)}, bf16[2048,256]{1,0:T(8,128)(2,1)}, u32[]{:S(2)}, u32[]{:S(2)}) collective-permute-start(bf16[2048,256]{1,0:T(8,128)(2,1)S(1)} %copy-done), channel_id=1, source_target_pairs={{0,6},{2,0},{4,2},{6,4},{1,7},{3,1},{5,3},{7,5},{8,14},{10,8},{12,... | collective-permute-start | bytes 3145736 | tf_op jit(solution)/shard_map/ppermute | solution.py:192
  29.2 46.1 %collective-permute-start = (bf16[2048,256]{1,0:T(8,128)(2,1)S(1)}, bf16[2048,256]{1,0:T(8,128)(2,1)}, u32[]{:S(2)}, u32[]{:S(2)}) collective-permute-start(bf16[2048,256]{1,0:T(8,128)(2,1)S(1)} %copy-done), channel_id=1, source_target_pairs={{0,2},{2,4},{4,6},{6,0},{1,3},{3,5},{5,7},{7,1},{8,10},{10,12},{12... | collective-permute-start | bytes 3145736 | tf_op jit(solution)/shard_map/ppermute | solution.py:192
  50.4 46.9 %all-to-all-start.1 = ((bf16[64,8,1024]{2,1,0:T(8,128)(2,1)}), bf16[64,8,1024]{2,1,0:T(8,128)(2,1)}, u32[]{:S(2)}, u32[]{:S(2)}) async-start(bf16[64,8,1024]{2,1,0:T(8,128)(2,1)} %shard_map.58), calls=%async_computation.1 | async-start | bytes 2097152 | tf_op jit(solution)/shard_map/all_to_all | solution.py:210
  58.5 20.2 %collective-permute-start.6 = (bf16[2048,256]{1,0:T(8,128)(2,1)S(1)}, bf16[2048,256]{1,0:T(8,128)(2,1)}, u32[]{:S(2)}, u32[]{:S(2)}) collective-permute-start(bf16[2048,256]{1,0:T(8,128)(2,1)S(1)} %copy-done), channel_id=1, source_target_pairs={{0,1},{1,0},{2,3},{3,2},{4,5},{5,4},{6,7},{7,6},{8,9},{9,8},{10,11... | collective-permute-start | bytes 3145736 | tf_op jit(solution)/shard_map/ppermute | solution.py:199
  62.4 25.4 %collective-permute-start.5 = (bf16[2048,256]{1,0:T(8,128)(2,1)}, bf16[2048,256]{1,0:T(8,128)(2,1)}, u32[]{:S(2)}, u32[]{:S(2)}) collective-permute-start(bf16[2048,256]{1,0:T(8,128)(2,1)} %collective-permute-done.4.refs_6_.refs_14_), channel_id=1, source_target_pairs={{0,1},{1,0},{2,3},{3,2},{4,5},{5,4},{6,7},{7,6},{8,9},{9,8},{10,11... | collective-permute-start | bytes 3145736 | tf_op jit(solution)/shard_map/ppermute | solution.py:199
  71.7 16.0 %collective-permute-start.3 = (bf16[2048,256]{1,0:T(8,128)(2,1)}, bf16[2048,256]{1,0:T(8,128)(2,1)}, u32[]{:S(2)}, u32[]{:S(2)}) collective-permute-start(bf16[2048,256]{1,0:T(8,128)(2,1)} %collective-permute-done.2.refs_7_.refs_11_), channel_id=1, source_target_pairs={{0,1},{1,0},{2,3},{3,2},{4,5},{5,4},{6,7},{7,6},{8,9},{9,8},{10,11... | collective-permute-start | bytes 3145736 | tf_op jit(solution)/shard_map/ppermute | solution.py:199
  75.3 12.4 %collective-permute-start.1 = (bf16[2048,256]{1,0:T(8,128)(2,1)}, bf16[2048,256]{1,0:T(8,128)(2,1)}, u32[]{:S(2)}, u32[]{:S(2)}) collective-permute-start(bf16[2048,256]{1,0:T(8,128)(2,1)} %collective-permute-done.refs_6_.refs_10_), channel_id=1, source_target_pairs={{0,1},{1,0},{2,3},{3,2},{4,5},{5,4},{6,7},{7,6},{8,9},{9,8},{10,11... | collective-permute-start | bytes 3145736 | tf_op jit(solution)/shard_map/ppermute | solution.py:199

commit v4 on v3

v4 whole, which is shorter than its diff:
```python
import jax
import jax.numpy as jnp
from jax import lax
from jax.experimental import pallas as pl
from jax.experimental.pallas import tpu as pltpu
from jax.sharding import Mesh, PartitionSpec as P


SAMP = ("z", "y")
TRAIT = ("x", "core")
FULL = 67043328
SMALL = 8 << 20
GROUPS = (((0, 0), (0, 1)), ((2, 0), (2, 1)), ((1, 0), (3, 0), (1, 1), (3, 1)))
HBM = pl.BlockSpec(memory_space=pltpu.HBM)
SCALAR = pl.BlockSpec(memory_space=pltpu.SMEM)


def whole(*shape):
    return pl.BlockSpec(shape, lambda *_: (0,) * len(shape))


def call(body, out, in_specs, out_specs, flops, moved, vmem, scratch=(), grid=(1,)):
    return pl.pallas_call(
        body,
        out_shape=out,
        grid=grid,
        in_specs=in_specs,
        out_specs=out_specs,
        scratch_shapes=list(scratch),
        compiler_params=pltpu.CompilerParams(vmem_limit_bytes=vmem),
        cost_estimate=pl.CostEstimate(flops=flops, bytes_accessed=moved, transcendentals=0),
    )


def cross_body(samples, traits, out, samples_v, traits_v, sems):
    n = samples_v.shape[0]
    _, cols = samples_v.shape[1:]
    copies = [pltpu.make_async_copy(traits, traits_v, sems.at[n])]
    for i in range(n):
        copies.append(
            pltpu.make_async_copy(
                samples.at[:, i * cols : (i + 1) * cols], samples_v.at[i], sems.at[i]
            )
        )
    for copy in copies:
        copy.start()
    copies[0].wait()
    flipped = traits_v[...].T
    span = out.shape[2]
    groups = out.shape[0] // 2
    for i in range(n):
        copies[i + 1].wait()
        piece = jnp.dot(flipped, samples_v[i], preferred_element_type=jnp.float32)
        half, at = divmod(i * cols, span)
        out[half * groups : (half + 1) * groups, :, at : at + cols] = piece.astype(
            jnp.bfloat16
        ).reshape(groups, -1, cols)


def sum_body(arrived, out):
    total = arrived[0].astype(jnp.float32)
    for i in range(1, arrived.shape[0]):
        total = total + arrived[i].astype(jnp.float32)
    total = total.astype(jnp.bfloat16)
    for i in range(out.shape[0]):
        out[i] = total


def row_of(place, shift, swap):
    return lax.rem(place[0] + 4 - shift, 4) * 2 + lax.rem(place[1] + swap, 2)


def split(value):
    top = value.astype(jnp.bfloat16)
    return top, value - top.astype(jnp.float32)


def shrink_of(place, squared, lambdas, block, penalties):
    top = squared[pl.ds(row_of(place, *block), 1), :]
    return [top / (top + lambdas[l]) for l in penalties]


def components_body(first, last, order, *refs):
    n = len(order)
    place, lambdas, squared, samples = refs[:4]
    blocks = refs[4 : 4 + n]
    out, level, samples_v, blocks_v, sems = refs[-5:]
    copies = [pltpu.make_async_copy(samples, samples_v, sems.at[n])]
    for i in range(n):
        copies.append(pltpu.make_async_copy(blocks[i], blocks_v.at[i], sems.at[i]))
    for copy in copies:
        copy.start()
    depth = blocks_v.shape[2]
    n_l = lambdas.shape[0]
    total = jnp.zeros((samples_v.shape[0], 2 * n_l), jnp.float32) if first else refs[4 + n][...]
    copies[0].wait()
    for i, block in enumerate(order):
        copies[i + 1].wait()
        value = jnp.dot(samples_v[...], blocks_v[i], preferred_element_type=jnp.float32)
        value = value.astype(jnp.bfloat16)
        out[:, i * depth : (i + 1) * depth] = value
        wide = value.astype(jnp.float32)
        high, low = split(wide * wide)
        shrink = jnp.concatenate(shrink_of(place, squared, lambdas, block, range(n_l)), axis=0)
        coarse, fine = split(shrink)
        weight = jnp.concatenate([coarse.astype(jnp.float32), fine], axis=0).astype(jnp.bfloat16)
        for part in (high, low.astype(jnp.bfloat16)):
            total = total + lax.dot_general(
                part, weight, (((1,), (1,)), ((), ())), preferred_element_type=jnp.float32
            )
    if last:
        level[...] = 1.0 / jnp.maximum(1.0 - (total[:, :n_l] + total[:, n_l:]), 0.25)
    else:
        level[...] = total


def fitted_body(groups_of, order, *refs):
    n, n_groups = len(order), len(groups_of)
    place, lambdas, squared, inverse, cross, traits = refs[:6]
    parts = refs[6 : 6 + n_groups]
    blocks = refs[6 + n_groups : 6 + n_groups + n]
    out, cross_v, joined, traits_v, blocks_v, projected, scaled, out_v, sems, out_sems = refs[-10:]
    depth = blocks_v.shape[2]
    span = cross_v.shape[2]
    half_groups = cross_v.shape[0] // 2
    pairs = [(cross, cross_v)]
    pairs += [(blocks[i], blocks_v.at[i]) for i in range(n)]
    at = 0
    for part in parts:
        pairs.append((part, joined.at[:, at : at + part.shape[1]]))
        at += part.shape[1]
    pairs.append((traits, traits_v))
    copies = [
        pltpu.make_async_copy(source, target, sems.at[i])
        for i, (source, target) in enumerate(pairs)
    ]
    for copy in copies:
        copy.start()
    copies[0].wait()
    halves = [
        cross_v[half * half_groups : (half + 1) * half_groups].reshape(-1, span)
        for half in range(2)
    ]
    for i in range(n):
        copies[i + 1].wait()
        value = 0.0
        for half in range(2):
            value = value + jnp.dot(
                halves[half],
                blocks_v[i, half * span : (half + 1) * span, :],
                preferred_element_type=jnp.float32,
            )
        projected[:, i * depth : (i + 1) * depth] = value.astype(jnp.bfloat16)
    for copy in copies[n + 1 :]:
        copy.wait()
    n_l = lambdas.shape[0]
    results = []
    for l in range(n_l):
        for i, block in enumerate(order):
            (shrink,) = shrink_of(place, squared, lambdas, block, (l,))
            here = slice(i * depth, (i + 1) * depth)
            scaled[l % 2, :, here] = (projected[:, here].astype(jnp.float32) * shrink).astype(
                jnp.bfloat16
            )
        fitted = lax.dot_general(
            joined[...],
            scaled[l % 2],
            (((1,), (1,)), ((), ())),
            preferred_element_type=jnp.float32,
        )
        out_v[l] = (traits_v[...].astype(jnp.float32) - fitted) * inverse[:, l : l + 1]
        results.append(pltpu.make_async_copy(out_v.at[l], out.at[l], out_sems.at[l]))
        results[-1].start()
    for copy in results:
        copy.wait()


def compute(samples, traits, whitening, singular, lambdas):
    features, depth = whitening.shape
    rows, width = traits.shape
    n_x, n_core = lax.axis_size("x"), lax.axis_size("core")
    n_samp = lax.axis_size("z") * lax.axis_size("y")
    n_l = lambdas.shape[0]
    every = n_x * n_core * depth
    n_blocks = n_x * n_core
    bf16, f32 = jnp.bfloat16, jnp.float32
    place = jnp.stack([lax.axis_index("x"), lax.axis_index("core")]).astype(jnp.int32)
    squared = (singular * singular).reshape(n_blocks, depth)
    dma = pltpu.SemaphoreType.DMA

    pieces = (n_samp, 2 * width // n_samp, features // 2)
    partial = call(
        cross_body,
        jax.ShapeDtypeStruct(pieces, bf16),
        [HBM, HBM],
        whole(*pieces),
        2 * rows * width * features,
        2 * (rows * width + rows * features + features * width),
        FULL,
        [pltpu.VMEM((8, rows, features // 8), bf16), pltpu.VMEM((rows, width), bf16), dma((9,))],
    )(samples, traits)
    arrived = lax.all_to_all(partial, SAMP, 0, 0)

    shifts = {}
    for shift in (2, 1, 3):
        shifts[shift] = lax.ppermute(whitening, "x", [(i, (i + shift) % n_x) for i in range(n_x)])
    blocks = {(0, 0): whitening}
    for shift in (0, 2, 1, 3):
        if shift:
            blocks[shift, 0] = shifts[shift]
        blocks[shift, 1] = lax.ppermute(blocks[shift, 0], "core", [(0, 1), (1, 0)])

    total = call(
        sum_body,
        jax.ShapeDtypeStruct(pieces, bf16),
        [whole(*pieces)],
        whole(*pieces),
        features * width,
        4 * features * width,
        SMALL,
    )(arrived)
    cross = lax.all_to_all(total, SAMP, 0, 0)

    def components(order, extra, last):
        n = len(order)
        first = not extra
        columns = n_l if last else 2 * n_l
        return call(
            lambda *refs: components_body(first, last, order, *refs),
            (
                jax.ShapeDtypeStruct((rows, n * depth), bf16),
                jax.ShapeDtypeStruct((rows, columns), f32),
            ),
            [SCALAR, SCALAR, whole(n_blocks, depth)]
            + [HBM] * (n + 1)
            + [whole(rows, 2 * n_l)] * len(extra),
            (whole(rows, n * depth), whole(rows, columns)),
            2 * rows * features * n * depth,
            2 * (rows * features + features * n * depth + rows * n * depth),
            FULL,
            [
                pltpu.VMEM((rows, features), bf16),
                pltpu.VMEM((n, features, depth), bf16),
                dma((n + 1,)),
            ],
        )(place, lambdas, squared, samples, *[blocks[b] for b in order], *extra)

    parts, state = [], ()
    for i, group in enumerate(GROUPS):
        part, level = components(group, state, i == len(GROUPS) - 1)
        parts.append(part)
        state = (level,)

    order = sum(GROUPS, ())
    return call(
        lambda *refs: fitted_body(GROUPS, order, *refs),
        jax.ShapeDtypeStruct((n_l, rows, width), f32),
        [SCALAR, SCALAR, whole(n_blocks, depth), whole(rows, n_l)]
        + [HBM] * (n_blocks + len(GROUPS) + 2),
        HBM,
        2 * n_l * rows * every * width,
        2 * rows * every + 2 * every * width + 4 * n_l * rows * width,
        FULL,
        [
            pltpu.VMEM(pieces, bf16),
            pltpu.VMEM((rows, every), bf16),
            pltpu.VMEM((rows, width), bf16),
            pltpu.VMEM((n_blocks, features, depth), bf16),
            pltpu.VMEM((width, every), bf16),
            pltpu.VMEM((2, width, every), bf16),
            pltpu.VMEM((n_l, rows, width), f32),
            dma((n_blocks + len(GROUPS) + 2,)),
            dma((n_l,)),
        ],
    )(
        place, lambdas, squared, level, cross, traits,
        *parts,
        *[blocks[b] for b in order],
    )


def solution(mesh):
    split = Mesh(mesh.devices.reshape(8, 8, 4, 2), SAMP + TRAIT)
    return jax.shard_map(
        compute,
        mesh=split,
        in_specs=(P(SAMP, None), P(SAMP, TRAIT), P(None, TRAIT), P(), P()),
        out_specs=P(None, SAMP, TRAIT),
        check_vma=False,
    )
```

time: 111 us -> 113 us (1.018)
  Pallas kernels: 36.8 us -> 38.8 us
    pallas_call x3 -> x4, Pallas kernels: 31.1 us -> 33.1 us  [the longest x3 21.4 us: components(): call(lambda *refs: components_body(first, last, order, *refs), (jax.Shape...]
  transfers between devices with their start and end apart: 9 -> 9, of which waited for: 2 -> 2; matrix products, arithmetic and copies ran while one was open for 1% -> 1% of each run, Pallas kernels for 18% -> 20%
where the time goes in v4:
time: 113 us; the launch traced here: 112 us
  starting transfers between devices  46.7 us (41%)
  Pallas kernels  38.8 us (34%)
  waiting for transfers between devices  25 us (22%)
    pallas_call x3, Pallas kernels, components(): call(lambda *refs: components_body(first, last, order, *refs), (jax.Shape...  21.4 us
    all_to_all x1, waiting for transfers between devices, compute(): arrived = lax.all_to_all(partial, SAMP, 0, 0)  17.5 us
    all_to_all x1, starting transfers between devices, compute(): arrived = lax.all_to_all(partial, SAMP, 0, 0)  17.3 us
    pallas_call x1, Pallas kernels, compute(): call(lambda *refs: fitted_body(GROUPS, order, *refs), jax.ShapeDtypeStruc...  11.7 us
    ppermute x4, starting transfers between devices, compute(): blocks[shift, 1] = lax.ppermute(blocks[shift, 0], 'core', [(0, 1), (1, 0)])  11.4 us
    ppermute x3, starting transfers between devices, compute(): lax.ppermute(whitening, 'x', [(i, (i + shift) % n_x) for i in range(n_x)])  9.94 us
    all_to_all x1, starting transfers between devices, compute(): cross = lax.all_to_all(total, SAMP, 0, 0)  8.04 us
    ppermute x3, waiting for transfers between devices, compute(): lax.ppermute(whitening, 'x', [(i, (i + shift) % n_x) for i in range(n_x)])  7.49 us
  transfers between devices with their start and end apart: 9, of which 2 were waited for; matrix products, arithmetic and copies ran while one was open for 1% of the time, Pallas kernels for 20%

profile of v4, /device:TPU:1, one launch (start us, length us, event | category | flops | bytes accessed | tf_op | source)
XLA Modules:
  0.0 112.1 jit_solution(12711522741893147171)
XLA Ops:
  0.0 4.4 %shard_map.58 = bf16[64,8,1024]{2,1,0:T(8,128)(2,1)} custom-call(bf16[512,2048]{1,0:T(8,128)(2,1)} %samples.1, bf16[512,256]{1,0:T(8,128)(2,1)} %refs_5_.1), custom_call_target="tpu_custom_call" | custom-call | flops 536870912 | bytes 3407872 | tf_op jit(solution)/shard_map/pallas_call | solution.py:192
  4.4 0.0 copy-start
  4.4 17.3 %all-to-all-start = ((bf16[64,8,1024]{2,1,0:T(8,128)(2,1)}), bf16[64,8,1024]{2,1,0:T(8,128)(2,1)S(1)}, u32[]{:S(2)}, u32[]{:S(2)}) async-start(bf16[64,8,1024]{2,1,0:T(8,128)(2,1)} %shard_map.58), calls=%async_computation | async-start | bytes 2097152 | tf_op jit(solution)/shard_map/all_to_all | solution.py:202
  21.7 0.0 copy-done
  21.7 0.0 copy-start.1
  21.7 4.7 %collective-permute-start.4 = (bf16[2048,256]{1,0:T(8,128)(2,1)S(1)}, bf16[2048,256]{1,0:T(8,128)(2,1)}, u32[]{:S(2)}, u32[]{:S(2)}) collective-permute-start(bf16[2048,256]{1,0:T(8,128)(2,1)S(1)} %copy-done), channel_id=1, source_target_pairs={{0,4},{2,6},{4,0},{6,2},{1,5},{3,7},{5,1},{7,3},{8,12},{10,14},{12... | collective-permute-start | bytes 3145736 | tf_op jit(solution)/shard_map/ppermute | solution.py:206
  26.4 2.8 %collective-permute-start.1 = (bf16[2048,256]{1,0:T(8,128)(2,1)S(1)}, bf16[2048,256]{1,0:T(8,128)(2,1)}, u32[]{:S(2)}, u32[]{:S(2)}) collective-permute-start(bf16[2048,256]{1,0:T(8,128)(2,1)S(1)} %copy-done), channel_id=1, source_target_pairs={{0,6},{2,0},{4,2},{6,4},{1,7},{3,1},{5,3},{7,5},{8,14},{10,8},{12,... | collective-permute-start | bytes 3145736 | tf_op jit(solution)/shard_map/ppermute | solution.py:206
  29.2 2.5 %collective-permute-start = (bf16[2048,256]{1,0:T(8,128)(2,1)S(1)}, bf16[2048,256]{1,0:T(8,128)(2,1)}, u32[]{:S(2)}, u32[]{:S(2)}) collective-permute-start(bf16[2048,256]{1,0:T(8,128)(2,1)S(1)} %copy-done), channel_id=1, source_target_pairs={{0,2},{2,4},{4,6},{6,0},{1,3},{3,5},{5,7},{7,1},{8,10},{10,12},{12... | collective-permute-start | bytes 3145736 | tf_op jit(solution)/shard_map/ppermute | solution.py:206
  31.7 17.5 %all-to-all-done.arrived = bf16[64,8,1024]{2,1,0:T(8,128)(2,1)S(1)} async-done(((bf16[64,8,1024]{2,1,0:T(8,128)(2,1)}), bf16[64,8,1024]{2,1,0:T(8,128)(2,1)S(1)}, u32[]{:S(2)}, u32[]{:S(2)}) %all-to-all-start) | async-done | bytes 1048608 | tf_op jit(solution)/shard_map/all_to_all | solution.py:202
  49.2 1.2 %shard_map.59 = bf16[64,8,1024]{2,1,0:T(8,128)(2,1)} custom-call(bf16[64,8,1024]{2,1,0:T(8,128)(2,1)S(1)} %all-to-all-done.arrived), custom_call_target="tpu_custom_call" | custom-call | flops 524288 | bytes 2097152 | tf_op jit(solution)/shard_map/pallas_call | solution.py:213
  50.4 8.0 %all-to-all-start.1 = ((bf16[64,8,1024]{2,1,0:T(8,128)(2,1)}), bf16[64,8,1024]{2,1,0:T(8,128)(2,1)}, u32[]{:S(2)}, u32[]{:S(2)}) async-start(bf16[64,8,1024]{2,1,0:T(8,128)(2,1)} %shard_map.59), calls=%async_computation.1 | async-start | bytes 2097152 | tf_op jit(solution)/shard_map/all_to_all | solution.py:222
  58.5 3.9 %collective-permute-start.6 = (bf16[2048,256]{1,0:T(8,128)(2,1)S(1)}, bf16[2048,256]{1,0:T(8,128)(2,1)}, u32[]{:S(2)}, u32[]{:S(2)}) collective-permute-start(bf16[2048,256]{1,0:T(8,128)(2,1)S(1)} %copy-done), channel_id=1, source_target_pairs={{0,1},{1,0},{2,3},{3,2},{4,5},{5,4},{6,7},{7,6},{8,9},{9,8},{10,11... | collective-permute-start | bytes 3145736 | tf_op jit(solution)/shard_map/ppermute | solution.py:211
  62.3 0.0 collective-permute-done.4.refs_4_.refs_11_
  62.3 1.9 %collective-permute-start.5 = (bf16[2048,256]{1,0:T(8,128)(2,1)}, bf16[2048,256]{1,0:T(8,128)(2,1)}, u32[]{:S(2)}, u32[]{:S(2)}) collective-permute-start(bf16[2048,256]{1,0:T(8,128)(2,1)} %collective-permute-done.4.refs_4_.refs_11_), channel_id=1, source_target_pairs={{0,1},{1,0},{2,3},{3,2},{4,5},{5,4},{6,7},{7,6},{8,9},{9,8},{10,11... | collective-permute-start | bytes 3145736 | tf_op jit(solution)/shard_map/ppermute | solution.py:211
  64.3 7.5 %collective-permute-done.1.refs_5_.refs_14_ = bf16[2048,256]{1,0:T(8,128)(2,1)} collective-permute-done((bf16[2048,256]{1,0:T(8,128)(2,1)S(1)}, bf16[2048,256]{1,0:T(8,128)(2,1)}, u32[]{:S(2)}, u32[]{:S(2)}) %collective-permute-start.1) | collective-permute-done | bytes 1048608 | tf_op jit(solution)/shard_map/ppermute | solution.py:206
  71.7 3.6 %collective-permute-start.3 = (bf16[2048,256]{1,0:T(8,128)(2,1)}, bf16[2048,256]{1,0:T(8,128)(2,1)}, u32[]{:S(2)}, u32[]{:S(2)}) collective-permute-start(bf16[2048,256]{1,0:T(8,128)(2,1)} %collective-permute-done.1.refs_5_.refs_14_), channel_id=1, source_target_pairs={{0,1},{1,0},{2,3},{3,2},{4,5},{5,4},{6,7},{7,6},{8,9},{9,8},{10,11... | collective-permute-start | bytes 3145736 | tf_op jit(solution)/shard_map/ppermute | solution.py:211
  75.3 0.0 collective-permute-done.refs_4_.refs_13_
  75.3 2.1 %collective-permute-start.2 = (bf16[2048,256]{1,0:T(8,128)(2,1)}, bf16[2048,256]{1,0:T(8,128)(2,1)}, u32[]{:S(2)}, u32[]{:S(2)}) collective-permute-start(bf16[2048,256]{1,0:T(8,128)(2,1)} %collective-permute-done.refs_4_.refs_13_), channel_id=1, source_target_pairs={{0,1},{1,0},{2,3},{3,2},{4,5},{5,4},{6,7},{7,6},{8,9},{9,8},{10,11... | collective-permute-start | bytes 3145736 | tf_op jit(solution)/shard_map/ppermute | solution.py:211
  77.4 0.0 copy-done.1
  77.5 0.6 reshape.3.refs_2_
  78.1 0.7 pad_add_fusion.refs_0_
  78.7 0.0 collective-permute-done.6.refs_5_.refs_10_
  78.7 6.1 %shard_map.55 = (bf16[512,512]{1,0:T(8,128)(2,1)}, f32[512,8]{1,0:T(8,128)}) custom-call(s32[2]{0:T(128)} %pad_add_fusion.refs_0_, f32[4]{0:T(128)} %refs_1_.7, f32[8,256]{1,0:T(8,128)} %reshape.3.refs_2_, bf16[512,2048]{1,0:T(8,128)(2,1)} %samples.1, bf16[2048,256]{1,0:T(8,128)(2,1)} %refs_9_.1, bf16[2048,256]{1,0:T(8,128)(2,1)} %collective-permute-done.6.refs_5_.refs_10_), custom_call_target="tpu_custom_call" | custom-call | flops 1073741824 | bytes 4718592 | tf_op jit(solution)/shard_map/pallas_call | solution.py:228
  84.8 0.0 collective-permute-done.5.refs_5_.refs_12_
  84.8 6.3 %shard_map.56 = (bf16[512,512]{1,0:T(8,128)(2,1)}, f32[512,8]{1,0:T(8,128)}) custom-call(s32[2]{0:T(128)} %pad_add_fusion.refs_0_, f32[4]{0:T(128)} %refs_1_.7, f32[8,256]{1,0:T(8,128)} %reshape.3.refs_2_, bf16[512,2048]{1,0:T(8,128)(2,1)} %samples.1, bf16[2048,256]{1,0:T(8,128)(2,1)} %collective-permute-done.4.refs_4_.refs_11_, ...), custom_call_target="tpu_custom_call" | custom-call | flops 1073741824 | bytes 4718592 | tf_op jit(solution)/shard_map/pallas_call | solution.py:228
  91.1 0.0 collective-permute-done.3.refs_7_.refs_16_
  91.2 0.0 collective-permute-done.2.refs_6_.refs_15_
  91.2 9.0 %shard_map.57 = (bf16[512,1024]{1,0:T(8,128)(2,1)}, f32[512,4]{1,0:T(8,128)}) custom-call(s32[2]{0:T(128)} %pad_add_fusion.refs_0_, f32[4]{0:T(128)} %refs_1_.7, f32[8,256]{1,0:T(8,128)} %reshape.3.refs_2_, bf16[512,2048]{1,0:T(8,128)(2,1)} %samples.1, bf16[2048,256]{1,0:T(8,128)(2,1)} %collective-permute-done.refs_4_.refs_13_, ...), custom_call_target="tpu_custom_call" | custom-call | flops 2147483648 | bytes 7340032 | tf_op jit(solution)/shard_map/pallas_call | solution.py:228
  100.2 0.0 all-to-all-done.1.refs_4_
  100.2 11.7 %shard_map.60 = f32[4,512,256]{2,1,0:T(8,128)} custom-call(s32[2]{0:T(128)} %pad_add_fusion.refs_0_, f32[4]{0:T(128)} %refs_1_.7, f32[8,256]{1,0:T(8,128)} %reshape.3.refs_2_, f32[512,4]{1,0:T(8,128)} %get-tuple-element.13.refs_3_, bf16[64,8,1024]{2,1,0:T(8,128)(2,1)} %all-to-all-done.1.refs_4_, bf16[512,256]{1,0:T(8,128)(2,1)} %refs_5_.1, ...), custom_call_target="tpu_custom_call" | custom-call | flops 2147483648 | bytes 5242880 | tf_op jit(solution)/shard_map/pallas_call | solution.py:255
  (1 shorter events, 0.0 us)
Async XLA Ops:
  4.4 17.3 %copy-start = (bf16[2048,256]{1,0:T(8,128)(2,1)S(1)}, bf16[2048,256]{1,0:T(8,128)(2,1)}, u32[]{:S(2)}) copy-start(bf16[2048,256]{1,0:T(8,128)(2,1)} %refs_9_.1) | copy-start | bytes 3145732
  4.4 44.8 %all-to-all-start = ((bf16[64,8,1024]{2,1,0:T(8,128)(2,1)}), bf16[64,8,1024]{2,1,0:T(8,128)(2,1)S(1)}, u32[]{:S(2)}, u32[]{:S(2)}) async-start(bf16[64,8,1024]{2,1,0:T(8,128)(2,1)} %shard_map.58), calls=%async_computation | async-start | bytes 2097152 | tf_op jit(solution)/shard_map/all_to_all | solution.py:202
  21.7 55.7 %copy-start.1 = (f32[2048]{0:T(1024)S(1)}, f32[2048]{0:T(1024)}, u32[]{:S(2)}) copy-start(f32[2048]{0:T(1024)} %param.8) | copy-start | bytes 24580
  21.7 40.6 %collective-permute-start.4 = (bf16[2048,256]{1,0:T(8,128)(2,1)S(1)}, bf16[2048,256]{1,0:T(8,128)(2,1)}, u32[]{:S(2)}, u32[]{:S(2)}) collective-permute-start(bf16[2048,256]{1,0:T(8,128)(2,1)S(1)} %copy-done), channel_id=1, source_target_pairs={{0,4},{2,6},{4,0},{6,2},{1,5},{3,7},{5,1},{7,3},{8,12},{10,14},{12... | collective-permute-start | bytes 3145736 | tf_op jit(solution)/shard_map/ppermute | solution.py:206
  26.4 45.4 %collective-permute-start.1 = (bf16[2048,256]{1,0:T(8,128)(2,1)S(1)}, bf16[2048,256]{1,0:T(8,128)(2,1)}, u32[]{:S(2)}, u32[]{:S(2)}) collective-permute-start(bf16[2048,256]{1,0:T(8,128)(2,1)S(1)} %copy-done), channel_id=1, source_target_pairs={{0,6},{2,0},{4,2},{6,4},{1,7},{3,1},{5,3},{7,5},{8,14},{10,8},{12,... | collective-permute-start | bytes 3145736 | tf_op jit(solution)/shard_map/ppermute | solution.py:206
  29.2 46.1 %collective-permute-start = (bf16[2048,256]{1,0:T(8,128)(2,1)S(1)}, bf16[2048,256]{1,0:T(8,128)(2,1)}, u32[]{:S(2)}, u32[]{:S(2)}) collective-permute-start(bf16[2048,256]{1,0:T(8,128)(2,1)S(1)} %copy-done), channel_id=1, source_target_pairs={{0,2},{2,4},{4,6},{6,0},{1,3},{3,5},{5,7},{7,1},{8,10},{10,12},{12... | collective-permute-start | bytes 3145736 | tf_op jit(solution)/shard_map/ppermute | solution.py:206
  50.4 49.8 %all-to-all-start.1 = ((bf16[64,8,1024]{2,1,0:T(8,128)(2,1)}), bf16[64,8,1024]{2,1,0:T(8,128)(2,1)}, u32[]{:S(2)}, u32[]{:S(2)}) async-start(bf16[64,8,1024]{2,1,0:T(8,128)(2,1)} %shard_map.59), calls=%async_computation.1 | async-start | bytes 2097152 | tf_op jit(solution)/shard_map/all_to_all | solution.py:222
  58.5 20.3 %collective-permute-start.6 = (bf16[2048,256]{1,0:T(8,128)(2,1)S(1)}, bf16[2048,256]{1,0:T(8,128)(2,1)}, u32[]{:S(2)}, u32[]{:S(2)}) collective-permute-start(bf16[2048,256]{1,0:T(8,128)(2,1)S(1)} %copy-done), channel_id=1, source_target_pairs={{0,1},{1,0},{2,3},{3,2},{4,5},{5,4},{6,7},{7,6},{8,9},{9,8},{10,11... | collective-permute-start | bytes 3145736 | tf_op jit(solution)/shard_map/ppermute | solution.py:211
  62.3 22.5 %collective-permute-start.5 = (bf16[2048,256]{1,0:T(8,128)(2,1)}, bf16[2048,256]{1,0:T(8,128)(2,1)}, u32[]{:S(2)}, u32[]{:S(2)}) collective-permute-start(bf16[2048,256]{1,0:T(8,128)(2,1)} %collective-permute-done.4.refs_4_.refs_11_), channel_id=1, source_target_pairs={{0,1},{1,0},{2,3},{3,2},{4,5},{5,4},{6,7},{7,6},{8,9},{9,8},{10,11... | collective-permute-start | bytes 3145736 | tf_op jit(solution)/shard_map/ppermute | solution.py:211
  71.7 19.4 %collective-permute-start.3 = (bf16[2048,256]{1,0:T(8,128)(2,1)}, bf16[2048,256]{1,0:T(8,128)(2,1)}, u32[]{:S(2)}, u32[]{:S(2)}) collective-permute-start(bf16[2048,256]{1,0:T(8,128)(2,1)} %collective-permute-done.1.refs_5_.refs_14_), channel_id=1, source_target_pairs={{0,1},{1,0},{2,3},{3,2},{4,5},{5,4},{6,7},{7,6},{8,9},{9,8},{10,11... | collective-permute-start | bytes 3145736 | tf_op jit(solution)/shard_map/ppermute | solution.py:211
  75.3 15.8 %collective-permute-start.2 = (bf16[2048,256]{1,0:T(8,128)(2,1)}, bf16[2048,256]{1,0:T(8,128)(2,1)}, u32[]{:S(2)}, u32[]{:S(2)}) collective-permute-start(bf16[2048,256]{1,0:T(8,128)(2,1)} %collective-permute-done.refs_4_.refs_13_), channel_id=1, source_target_pairs={{0,1},{1,0},{2,3},{3,2},{4,5},{5,4},{6,7},{7,6},{8,9},{9,8},{10,11... | collective-permute-start | bytes 3145736 | tf_op jit(solution)/shard_map/ppermute | solution.py:211

commit v5 on v4

--- a/solution.py
+++ b/solution.py
@@ -10,7 +10,7 @@
 TRAIT = ("x", "core")
 FULL = 67043328
 SMALL = 8 << 20
-GROUPS = (((0, 0), (0, 1)), ((2, 0), (2, 1)), ((1, 0), (3, 0), (1, 1), (3, 1)))
+GROUPS = (((0, 0), (0, 1)), ((1, 0), (3, 0), (1, 1), (3, 1)), ((2, 0), (2, 1)))
 HBM = pl.BlockSpec(memory_space=pltpu.HBM)
 SCALAR = pl.BlockSpec(memory_space=pltpu.SMEM)
 
@@ -85,23 +85,36 @@
     place, lambdas, squared, samples = refs[:4]
     blocks = refs[4 : 4 + n]
     out, level, samples_v, blocks_v, sems = refs[-5:]
+    depth = blocks[0].shape[1]
+    n_l = lambdas.shape[0]
     copies = [pltpu.make_async_copy(samples, samples_v, sems.at[n])]
     for i in range(n):
-        copies.append(pltpu.make_async_copy(blocks[i], blocks_v.at[i], sems.at[i]))
+        copies.append(
+            pltpu.make_async_copy(
+                blocks[i], blocks_v.at[:, i * depth : (i + 1) * depth], sems.at[i]
+            )
+        )
     for copy in copies:
         copy.start()
-    depth = blocks_v.shape[2]
-    n_l = lambdas.shape[0]
     total = jnp.zeros((samples_v.shape[0], 2 * n_l), jnp.float32) if first else refs[4 + n][...]
     copies[0].wait()
-    for i, block in enumerate(order):
+    for i in range(0, n, 2):
         copies[i + 1].wait()
-        value = jnp.dot(samples_v[...], blocks_v[i], preferred_element_type=jnp.float32)
-        value = value.astype(jnp.bfloat16)
-        out[:, i * depth : (i + 1) * depth] = value
+        copies[i + 2].wait()
+        here = slice(i * depth, (i + 2) * depth)
+        value = jnp.dot(
+            samples_v[...], blocks_v[:, here], preferred_element_type=jnp.float32
+        ).astype(jnp.bfloat16)
+        out[:, here] = value
         wide = value.astype(jnp.float32)
         high, low = split(wide * wide)
-        shrink = jnp.concatenate(shrink_of(place, squared, lambdas, block, range(n_l)), axis=0)
+        shrink = jnp.concatenate(
+            [
+                jnp.concatenate(shrink_of(place, squared, lambdas, block, range(n_l)), axis=0)
+                for block in order[i : i + 2]
+            ],
+            axis=1,
+        )
         coarse, fine = split(shrink)
         weight = jnp.concatenate([coarse.astype(jnp.float32), fine], axis=0).astype(jnp.bfloat16)
         for part in (high, low.astype(jnp.bfloat16)):
@@ -120,11 +133,10 @@
     parts = refs[6 : 6 + n_groups]
     blocks = refs[6 + n_groups : 6 + n_groups + n]
     out, cross_v, joined, traits_v, blocks_v, projected, scaled, out_v, sems, out_sems = refs[-10:]
-    depth = blocks_v.shape[2]
-    span = cross_v.shape[2]
-    half_groups = cross_v.shape[0] // 2
-    pairs = [(cross, cross_v)]
-    pairs += [(blocks[i], blocks_v.at[i]) for i in range(n)]
+    depth = blocks[0].shape[1]
+    width, span = cross.shape[1:]
+    pairs = [(cross.at[half], cross_v.at[:, half * span : (half + 1) * span]) for half in range(2)]
+    pairs += [(blocks[i], blocks_v.at[:, i * depth : (i + 1) * depth]) for i in range(n)]
     at = 0
     for part in parts:
         pairs.append((part, joined.at[:, at : at + part.shape[1]]))
@@ -137,40 +149,41 @@
     for copy in copies:
         copy.start()
     copies[0].wait()
-    halves = [
-        cross_v[half * half_groups : (half + 1) * half_groups].reshape(-1, span)
-        for half in range(2)
-    ]
-    for i in range(n):
-        copies[i + 1].wait()
-        value = 0.0
-        for half in range(2):
-            value = value + jnp.dot(
-                halves[half],
-                blocks_v[i, half * span : (half + 1) * span, :],
-                preferred_element_type=jnp.float32,
-            )
-        projected[:, i * depth : (i + 1) * depth] = value.astype(jnp.bfloat16)
-    for copy in copies[n + 1 :]:
+    copies[1].wait()
+    for i in range(0, n, 2):
+        copies[i + 2].wait()
+        copies[i + 3].wait()
+        here = slice(i * depth, (i + 2) * depth)
+        projected[:, here] = jnp.dot(
+            cross_v[...], blocks_v[:, here], preferred_element_type=jnp.float32
+        ).astype(jnp.bfloat16)
+    for copy in copies[n + 2 :]:
         copy.wait()
     n_l = lambdas.shape[0]
     results = []
-    for l in range(n_l):
+    for pair in range(n_l // 2):
         for i, block in enumerate(order):
-            (shrink,) = shrink_of(place, squared, lambdas, block, (l,))
             here = slice(i * depth, (i + 1) * depth)
-            scaled[l % 2, :, here] = (projected[:, here].astype(jnp.float32) * shrink).astype(
-                jnp.bfloat16
-            )
+            value = projected[:, here].astype(jnp.float32)
+            for j, shrink in enumerate(
+                shrink_of(place, squared, lambdas, block, (2 * pair, 2 * pair + 1))
+            ):
+                scaled[pair, j * width : (j + 1) * width, here] = (value * shrink).astype(
+                    jnp.bfloat16
+                )
         fitted = lax.dot_general(
             joined[...],
-            scaled[l % 2],
+            scaled[pair],
             (((1,), (1,)), ((), ())),
             preferred_element_type=jnp.float32,
         )
-        out_v[l] = (traits_v[...].astype(jnp.float32) - fitted) * inverse[:, l : l + 1]
-        results.append(pltpu.make_async_copy(out_v.at[l], out.at[l], out_sems.at[l]))
-        results[-1].start()
+        for j in range(2):
+            l = 2 * pair + j
+            out_v[l] = (
+                traits_v[...].astype(jnp.float32) - fitted[:, j * width : (j + 1) * width]
+            ) * inverse[:, l : l + 1]
+            results.append(pltpu.make_async_copy(out_v.at[l], out.at[l], out_sems.at[l]))
+            results[-1].start()
     for copy in results:
         copy.wait()
 
@@ -240,7 +253,7 @@
             FULL,
             [
                 pltpu.VMEM((rows, features), bf16),
-                pltpu.VMEM((n, features, depth), bf16),
+                pltpu.VMEM((features, n * depth), bf16),
                 dma((n + 1,)),
             ],
         )(place, lambdas, squared, samples, *[blocks[b] for b in order], *extra)
@@ -262,18 +275,18 @@
         2 * rows * every + 2 * every * width + 4 * n_l * rows * width,
         FULL,
         [
-            pltpu.VMEM(pieces, bf16),
+            pltpu.VMEM((width, features), bf16),
             pltpu.VMEM((rows, every), bf16),
             pltpu.VMEM((rows, width), bf16),
-            pltpu.VMEM((n_blocks, features, depth), bf16),
+            pltpu.VMEM((features, every), bf16),
             pltpu.VMEM((width, every), bf16),
-            pltpu.VMEM((2, width, every), bf16),
+            pltpu.VMEM((n_l // 2, 2 * width, every), bf16),
             pltpu.VMEM((n_l, rows, width), f32),
-            dma((n_blocks + len(GROUPS) + 2,)),
+            dma((n_blocks + len(GROUPS) + 3,)),
             dma((n_l,)),
         ],
     )(
-        place, lambdas, squared, level, cross, traits,
+        place, lambdas, squared, level, cross.reshape(2, width, -1), traits,
         *parts,
         *[blocks[b] for b in order],
     )

time: 113 us -> 112 us (level)
  starting transfers between devices: 46.7 us -> 58.1 us
  waiting for transfers between devices: 25 us -> 17.5 us
  Pallas kernels: 38.8 us -> 34.2 us
    ppermute x4, starting transfers between devices: 11.4 us -> 22.9 us  [compute(): blocks[shift, 1] = lax.ppermute(blocks[shift, 0], 'core', [(0, 1), (1, 0)])]
    ppermute x3, waiting for transfers between devices: 7.49 us -> 0.01 us  [compute(): lax.ppermute(whitening, 'x', [(i, (i + shift) % n_x) for i in range(n_x)])]
    pallas_call x1, Pallas kernels: 11.7 us -> 9.32 us  [compute(): call(lambda *refs: fitted_body(GROUPS, order, *refs), jax.ShapeDtypeStruc...]
    pallas_call x3, Pallas kernels: 21.4 us -> 19.2 us  [components(): call(lambda *refs: components_body(first, last, order, *refs), (jax.Shape...]
  transfers between devices with their start and end apart: 9 -> 9, of which waited for: 2 -> 1; matrix products, arithmetic and copies ran while one was open for 1% -> 1% of each run, Pallas kernels for 20% -> 18%
where the time goes in v5:
time: 112 us; the launch traced here: 111 us
  starting transfers between devices  58.1 us (52%)
  Pallas kernels  34.2 us (31%)
  waiting for transfers between devices  17.5 us (16%)
    ppermute x4, starting transfers between devices, compute(): blocks[shift, 1] = lax.ppermute(blocks[shift, 0], 'core', [(0, 1), (1, 0)])  22.9 us
    pallas_call x3, Pallas kernels, components(): call(lambda *refs: components_body(first, last, order, *refs), (jax.Shape...  19.2 us
    all_to_all x1, waiting for transfers between devices, compute(): arrived = lax.all_to_all(partial, SAMP, 0, 0)  17.5 us
    all_to_all x1, starting transfers between devices, compute(): arrived = lax.all_to_all(partial, SAMP, 0, 0)  17.3 us
    ppermute x3, starting transfers between devices, compute(): lax.ppermute(whitening, 'x', [(i, (i + shift) % n_x) for i in range(n_x)])  9.94 us
    pallas_call x1, Pallas kernels, compute(): call(lambda *refs: fitted_body(GROUPS, order, *refs), jax.ShapeDtypeStruc...  9.32 us
    all_to_all x1, starting transfers between devices, compute(): cross = lax.all_to_all(total, SAMP, 0, 0)  8.04 us
    pallas_call x1, Pallas kernels, compute(): call(cross_body, jax.ShapeDtypeStruct(pieces, bf16), [HBM, HBM], whole(*p...  4.4 us
  transfers between devices with their start and end apart: 9, of which 1 were waited for; matrix products, arithmetic and copies ran while one was open for 1% of the time, Pallas kernels for 18%

profile of v5, /device:TPU:1, one launch (start us, length us, event | category | flops | bytes accessed | tf_op | source)
XLA Modules:
  0.0 111.4 jit_solution(11619240564406616618)
XLA Ops:
  0.0 4.4 %shard_map.58 = bf16[64,8,1024]{2,1,0:T(8,128)(2,1)} custom-call(bf16[512,2048]{1,0:T(8,128)(2,1)} %samples.1, bf16[512,256]{1,0:T(8,128)(2,1)} %refs_5_.1), custom_call_target="tpu_custom_call" | custom-call | flops 536870912 | bytes 3407872 | tf_op jit(solution)/shard_map/pallas_call | solution.py:205
  4.4 0.0 copy-start
  4.4 17.3 %all-to-all-start = ((bf16[64,8,1024]{2,1,0:T(8,128)(2,1)}), bf16[64,8,1024]{2,1,0:T(8,128)(2,1)S(1)}, u32[]{:S(2)}, u32[]{:S(2)}) async-start(bf16[64,8,1024]{2,1,0:T(8,128)(2,1)} %shard_map.58), calls=%async_computation | async-start | bytes 2097152 | tf_op jit(solution)/shard_map/all_to_all | solution.py:215
  21.7 0.0 copy-done
  21.7 0.0 copy-start.1
  21.7 4.4 %collective-permute-start.3 = (bf16[2048,256]{1,0:T(8,128)(2,1)S(1)}, bf16[2048,256]{1,0:T(8,128)(2,1)}, u32[]{:S(2)}, u32[]{:S(2)}) collective-permute-start(bf16[2048,256]{1,0:T(8,128)(2,1)S(1)} %copy-done), channel_id=1, source_target_pairs={{0,6},{2,0},{4,2},{6,4},{1,7},{3,1},{5,3},{7,5},{8,14},{10,8},{12,... | collective-permute-start | bytes 3145736 | tf_op jit(solution)/shard_map/ppermute | solution.py:219
  26.1 1.9 %collective-permute-start.2 = (bf16[2048,256]{1,0:T(8,128)(2,1)S(1)}, bf16[2048,256]{1,0:T(8,128)(2,1)}, u32[]{:S(2)}, u32[]{:S(2)}) collective-permute-start(bf16[2048,256]{1,0:T(8,128)(2,1)S(1)} %copy-done), channel_id=1, source_target_pairs={{0,2},{2,4},{4,6},{6,0},{1,3},{3,5},{5,7},{7,1},{8,10},{10,12},{12... | collective-permute-start | bytes 3145736 | tf_op jit(solution)/shard_map/ppermute | solution.py:219
  28.0 3.6 %collective-permute-start = (bf16[2048,256]{1,0:T(8,128)(2,1)S(1)}, bf16[2048,256]{1,0:T(8,128)(2,1)}, u32[]{:S(2)}, u32[]{:S(2)}) collective-permute-start(bf16[2048,256]{1,0:T(8,128)(2,1)S(1)} %copy-done), channel_id=1, source_target_pairs={{0,4},{2,6},{4,0},{6,2},{1,5},{3,7},{5,1},{7,3},{8,12},{10,14},{12... | collective-permute-start | bytes 3145736 | tf_op jit(solution)/shard_map/ppermute | solution.py:219
  31.7 17.5 %all-to-all-done.arrived = bf16[64,8,1024]{2,1,0:T(8,128)(2,1)S(1)} async-done(((bf16[64,8,1024]{2,1,0:T(8,128)(2,1)}), bf16[64,8,1024]{2,1,0:T(8,128)(2,1)S(1)}, u32[]{:S(2)}, u32[]{:S(2)}) %all-to-all-start) | async-done | bytes 1048608 | tf_op jit(solution)/shard_map/all_to_all | solution.py:215
  49.2 1.2 %shard_map.59 = bf16[64,8,1024]{2,1,0:T(8,128)(2,1)} custom-call(bf16[64,8,1024]{2,1,0:T(8,128)(2,1)S(1)} %all-to-all-done.arrived), custom_call_target="tpu_custom_call" | custom-call | flops 524288 | bytes 2097152 | tf_op jit(solution)/shard_map/pallas_call | solution.py:226
  50.4 8.0 %all-to-all-start.1 = ((bf16[64,8,1024]{2,1,0:T(8,128)(2,1)}), bf16[64,8,1024]{2,1,0:T(8,128)(2,1)}, u32[]{:S(2)}, u32[]{:S(2)}) async-start(bf16[64,8,1024]{2,1,0:T(8,128)(2,1)} %shard_map.59), calls=%async_computation.1 | async-start | bytes 2097152 | tf_op jit(solution)/shard_map/all_to_all | solution.py:235
  58.5 3.9 %collective-permute-start.6 = (bf16[2048,256]{1,0:T(8,128)(2,1)S(1)}, bf16[2048,256]{1,0:T(8,128)(2,1)}, u32[]{:S(2)}, u32[]{:S(2)}) collective-permute-start(bf16[2048,256]{1,0:T(8,128)(2,1)S(1)} %copy-done), channel_id=1, source_target_pairs={{0,1},{1,0},{2,3},{3,2},{4,5},{5,4},{6,7},{7,6},{8,9},{9,8},{10,11... | collective-permute-start | bytes 3145736 | tf_op jit(solution)/shard_map/ppermute | solution.py:224
  62.3 0.0 collective-permute-done.3.refs_5_.refs_12_
  62.3 11.5 %collective-permute-start.5 = (bf16[2048,256]{1,0:T(8,128)(2,1)}, bf16[2048,256]{1,0:T(8,128)(2,1)}, u32[]{:S(2)}, u32[]{:S(2)}) collective-permute-start(bf16[2048,256]{1,0:T(8,128)(2,1)} %collective-permute-done.3.refs_5_.refs_12_), channel_id=1, source_target_pairs={{0,1},{1,0},{2,3},{3,2},{4,5},{5,4},{6,7},{7,6},{8,9},{9,8},{10,11... | collective-permute-start | bytes 3145736 | tf_op jit(solution)/shard_map/ppermute | solution.py:224
  73.9 0.0 collective-permute-done.2.refs_4_.refs_11_
  73.9 5.4 %collective-permute-start.4 = (bf16[2048,256]{1,0:T(8,128)(2,1)}, bf16[2048,256]{1,0:T(8,128)(2,1)}, u32[]{:S(2)}, u32[]{:S(2)}) collective-permute-start(bf16[2048,256]{1,0:T(8,128)(2,1)} %collective-permute-done.2.refs_4_.refs_11_), channel_id=1, source_target_pairs={{0,1},{1,0},{2,3},{3,2},{4,5},{5,4},{6,7},{7,6},{8,9},{9,8},{10,11... | collective-permute-start | bytes 3145736 | tf_op jit(solution)/shard_map/ppermute | solution.py:224
  79.3 0.0 collective-permute-done.refs_4_.refs_15_
  79.3 2.1 %collective-permute-start.1 = (bf16[2048,256]{1,0:T(8,128)(2,1)}, bf16[2048,256]{1,0:T(8,128)(2,1)}, u32[]{:S(2)}, u32[]{:S(2)}) collective-permute-start(bf16[2048,256]{1,0:T(8,128)(2,1)} %collective-permute-done.refs_4_.refs_15_), channel_id=1, source_target_pairs={{0,1},{1,0},{2,3},{3,2},{4,5},{5,4},{6,7},{7,6},{8,9},{9,8},{10,11... | collective-permute-start | bytes 3145736 | tf_op jit(solution)/shard_map/ppermute | solution.py:224
  81.4 0.0 copy-done.1
  81.4 0.6 reshape.6.refs_2_
  82.0 0.7 pad_add_fusion.refs_0_
  82.7 0.0 collective-permute-done.6.refs_5_.refs_10_
  82.7 5.5 %shard_map.55 = (bf16[512,512]{1,0:T(8,128)(2,1)}, f32[512,8]{1,0:T(8,128)}) custom-call(s32[2]{0:T(128)} %pad_add_fusion.refs_0_, f32[4]{0:T(128)} %refs_1_.7, f32[8,256]{1,0:T(8,128)} %reshape.6.refs_2_, bf16[512,2048]{1,0:T(8,128)(2,1)} %samples.1, bf16[2048,256]{1,0:T(8,128)(2,1)} %refs_9_.1, bf16[2048,256]{1,0:T(8,128)(2,1)} %collective-permute-done.6.refs_5_.refs_10_), custom_call_target="tpu_custom_call" | custom-call | flops 1073741824 | bytes 4718592 | tf_op jit(solution)/shard_map/pallas_call | solution.py:241
  88.2 0.0 collective-permute-done.5.refs_7_.refs_14_
  88.2 0.0 collective-permute-done.4.refs_6_.refs_13_
  88.2 7.8 %shard_map.56 = (bf16[512,1024]{1,0:T(8,128)(2,1)}, f32[512,8]{1,0:T(8,128)}) custom-call(s32[2]{0:T(128)} %pad_add_fusion.refs_0_, f32[4]{0:T(128)} %refs_1_.7, f32[8,256]{1,0:T(8,128)} %reshape.6.refs_2_, bf16[512,2048]{1,0:T(8,128)(2,1)} %samples.1, bf16[2048,256]{1,0:T(8,128)(2,1)} %collective-permute-done.2.refs_4_.refs_11_, ...), custom_call_target="tpu_custom_call" | custom-call | flops 2147483648 | bytes 7340032 | tf_op jit(solution)/shard_map/pallas_call | solution.py:241
  96.0 0.0 collective-permute-done.1.refs_5_.refs_16_
  96.1 5.9 %shard_map.57 = (bf16[512,512]{1,0:T(8,128)(2,1)}, f32[512,4]{1,0:T(8,128)}) custom-call(s32[2]{0:T(128)} %pad_add_fusion.refs_0_, f32[4]{0:T(128)} %refs_1_.7, f32[8,256]{1,0:T(8,128)} %reshape.6.refs_2_, bf16[512,2048]{1,0:T(8,128)(2,1)} %samples.1, bf16[2048,256]{1,0:T(8,128)(2,1)} %collective-permute-done.refs_4_.refs_15_, ...), custom_call_target="tpu_custom_call" | custom-call | flops 1073741824 | bytes 4718592 | tf_op jit(solution)/shard_map/pallas_call | solution.py:241
  101.9 0.0 all-to-all-done.1
  102.0 9.3 %shard_map.60 = f32[4,512,256]{2,1,0:T(8,128)} custom-call(s32[2]{0:T(128)} %pad_add_fusion.refs_0_, f32[4]{0:T(128)} %refs_1_.7, f32[8,256]{1,0:T(8,128)} %reshape.6.refs_2_, f32[512,4]{1,0:T(8,128)} %get-tuple-element.13.refs_3_, bf16[2,256,1024]{2,1,0:T(8,128)(2,1)} %bitcast.2.refs_4_, bf16[512,256]{1,0:T(8,128)(2,1)} %refs_5_.1, ...), custom_call_target="tpu_custom_call" | custom-call | flops 2147483648 | bytes 5242880 | tf_op jit(solution)/shard_map/pallas_call | solution.py:268
  (1 shorter events, 0.0 us)
Async XLA Ops:
  4.4 17.3 %copy-start = (bf16[2048,256]{1,0:T(8,128)(2,1)S(1)}, bf16[2048,256]{1,0:T(8,128)(2,1)}, u32[]{:S(2)}) copy-start(bf16[2048,256]{1,0:T(8,128)(2,1)} %refs_9_.1) | copy-start | bytes 3145732
  4.4 44.8 %all-to-all-start = ((bf16[64,8,1024]{2,1,0:T(8,128)(2,1)}), bf16[64,8,1024]{2,1,0:T(8,128)(2,1)S(1)}, u32[]{:S(2)}, u32[]{:S(2)}) async-start(bf16[64,8,1024]{2,1,0:T(8,128)(2,1)} %shard_map.58), calls=%async_computation | async-start | bytes 2097152 | tf_op jit(solution)/shard_map/all_to_all | solution.py:215
  21.7 59.7 %copy-start.1 = (f32[2048]{0:T(1024)S(1)}, f32[2048]{0:T(1024)}, u32[]{:S(2)}) copy-start(f32[2048]{0:T(1024)} %param.8) | copy-start | bytes 24580
  21.7 40.6 %collective-permute-start.3 = (bf16[2048,256]{1,0:T(8,128)(2,1)S(1)}, bf16[2048,256]{1,0:T(8,128)(2,1)}, u32[]{:S(2)}, u32[]{:S(2)}) collective-permute-start(bf16[2048,256]{1,0:T(8,128)(2,1)S(1)} %copy-done), channel_id=1, source_target_pairs={{0,6},{2,0},{4,2},{6,4},{1,7},{3,1},{5,3},{7,5},{8,14},{10,8},{12,... | collective-permute-start | bytes 3145736 | tf_op jit(solution)/shard_map/ppermute | solution.py:219
  26.1 47.8 %collective-permute-start.2 = (bf16[2048,256]{1,0:T(8,128)(2,1)S(1)}, bf16[2048,256]{1,0:T(8,128)(2,1)}, u32[]{:S(2)}, u32[]{:S(2)}) collective-permute-start(bf16[2048,256]{1,0:T(8,128)(2,1)S(1)} %copy-done), channel_id=1, source_target_pairs={{0,2},{2,4},{4,6},{6,0},{1,3},{3,5},{5,7},{7,1},{8,10},{10,12},{12... | collective-permute-start | bytes 3145736 | tf_op jit(solution)/shard_map/ppermute | solution.py:219
  28.0 51.2 %collective-permute-start = (bf16[2048,256]{1,0:T(8,128)(2,1)S(1)}, bf16[2048,256]{1,0:T(8,128)(2,1)}, u32[]{:S(2)}, u32[]{:S(2)}) collective-permute-start(bf16[2048,256]{1,0:T(8,128)(2,1)S(1)} %copy-done), channel_id=1, source_target_pairs={{0,4},{2,6},{4,0},{6,2},{1,5},{3,7},{5,1},{7,3},{8,12},{10,14},{12... | collective-permute-start | bytes 3145736 | tf_op jit(solution)/shard_map/ppermute | solution.py:219
  50.4 51.5 %all-to-all-start.1 = ((bf16[64,8,1024]{2,1,0:T(8,128)(2,1)}), bf16[64,8,1024]{2,1,0:T(8,128)(2,1)}, u32[]{:S(2)}, u32[]{:S(2)}) async-start(bf16[64,8,1024]{2,1,0:T(8,128)(2,1)} %shard_map.59), calls=%async_computation.1 | async-start | bytes 2097152 | tf_op jit(solution)/shard_map/all_to_all | solution.py:235
  58.5 24.2 %collective-permute-start.6 = (bf16[2048,256]{1,0:T(8,128)(2,1)S(1)}, bf16[2048,256]{1,0:T(8,128)(2,1)}, u32[]{:S(2)}, u32[]{:S(2)}) collective-permute-start(bf16[2048,256]{1,0:T(8,128)(2,1)S(1)} %copy-done), channel_id=1, source_target_pairs={{0,1},{1,0},{2,3},{3,2},{4,5},{5,4},{6,7},{7,6},{8,9},{9,8},{10,11... | collective-permute-start | bytes 3145736 | tf_op jit(solution)/shard_map/ppermute | solution.py:224
  62.3 25.9 %collective-permute-start.5 = (bf16[2048,256]{1,0:T(8,128)(2,1)}, bf16[2048,256]{1,0:T(8,128)(2,1)}, u32[]{:S(2)}, u32[]{:S(2)}) collective-permute-start(bf16[2048,256]{1,0:T(8,128)(2,1)} %collective-permute-done.3.refs_5_.refs_12_), channel_id=1, source_target_pairs={{0,1},{1,0},{2,3},{3,2},{4,5},{5,4},{6,7},{7,6},{8,9},{9,8},{10,11... | collective-permute-start | bytes 3145736 | tf_op jit(solution)/shard_map/ppermute | solution.py:224
  73.9 14.3 %collective-permute-start.4 = (bf16[2048,256]{1,0:T(8,128)(2,1)}, bf16[2048,256]{1,0:T(8,128)(2,1)}, u32[]{:S(2)}, u32[]{:S(2)}) collective-permute-start(bf16[2048,256]{1,0:T(8,128)(2,1)} %collective-permute-done.2.refs_4_.refs_11_), channel_id=1, source_target_pairs={{0,1},{1,0},{2,3},{3,2},{4,5},{5,4},{6,7},{7,6},{8,9},{9,8},{10,11... | collective-permute-start | bytes 3145736 | tf_op jit(solution)/shard_map/ppermute | solution.py:224
  79.3 16.8 %collective-permute-start.1 = (bf16[2048,256]{1,0:T(8,128)(2,1)}, bf16[2048,256]{1,0:T(8,128)(2,1)}, u32[]{:S(2)}, u32[]{:S(2)}) collective-permute-start(bf16[2048,256]{1,0:T(8,128)(2,1)} %collective-permute-done.refs_4_.refs_15_), channel_id=1, source_target_pairs={{0,1},{1,0},{2,3},{3,2},{4,5},{5,4},{6,7},{7,6},{8,9},{9,8},{10,11... | collective-permute-start | bytes 3145736 | tf_op jit(solution)/shard_map/ppermute | solution.py:224

commit v6 on v5

--- a/solution.py
+++ b/solution.py
@@ -9,8 +9,8 @@
 SAMP = ("z", "y")
 TRAIT = ("x", "core")
 FULL = 67043328
-SMALL = 8 << 20
-GROUPS = (((0, 0), (0, 1)), ((1, 0), (3, 0), (1, 1), (3, 1)), ((2, 0), (2, 1)))
+GROUPS = (((0, 0), (0, 1)), ((2, 0), (2, 1)), ((1, 0), (3, 0)))
+LAST = ((1, 1), (3, 1))
 HBM = pl.BlockSpec(memory_space=pltpu.HBM)
 SCALAR = pl.BlockSpec(memory_space=pltpu.SMEM)
 
@@ -80,7 +80,28 @@
     return [top / (top + lambdas[l]) for l in penalties]
 
 
-def components_body(first, last, order, *refs):
+def levels(value, place, squared, lambdas, blocks):
+    penalties = range(lambdas.shape[0])
+    wide = value.astype(jnp.float32)
+    high, low = split(wide * wide)
+    shrink = jnp.concatenate(
+        [
+            jnp.concatenate(shrink_of(place, squared, lambdas, block, penalties), axis=0)
+            for block in blocks
+        ],
+        axis=1,
+    )
+    coarse, fine = split(shrink)
+    weight = jnp.concatenate([coarse.astype(jnp.float32), fine], axis=0).astype(jnp.bfloat16)
+    return sum(
+        lax.dot_general(
+            part, weight, (((1,), (1,)), ((), ())), preferred_element_type=jnp.float32
+        )
+        for part in (high, low.astype(jnp.bfloat16))
+    )
+
+
+def components_body(first, order, *refs):
     n = len(order)
     place, lambdas, squared, samples = refs[:4]
     blocks = refs[4 : 4 + n]
@@ -106,37 +127,22 @@
             samples_v[...], blocks_v[:, here], preferred_element_type=jnp.float32
         ).astype(jnp.bfloat16)
         out[:, here] = value
-        wide = value.astype(jnp.float32)
-        high, low = split(wide * wide)
-        shrink = jnp.concatenate(
-            [
-                jnp.concatenate(shrink_of(place, squared, lambdas, block, range(n_l)), axis=0)
-                for block in order[i : i + 2]
-            ],
-            axis=1,
-        )
-        coarse, fine = split(shrink)
-        weight = jnp.concatenate([coarse.astype(jnp.float32), fine], axis=0).astype(jnp.bfloat16)
-        for part in (high, low.astype(jnp.bfloat16)):
-            total = total + lax.dot_general(
-                part, weight, (((1,), (1,)), ((), ())), preferred_element_type=jnp.float32
-            )
-    if last:
-        level[...] = 1.0 / jnp.maximum(1.0 - (total[:, :n_l] + total[:, n_l:]), 0.25)
-    else:
-        level[...] = total
-
-
-def fitted_body(groups_of, order, *refs):
-    n, n_groups = len(order), len(groups_of)
-    place, lambdas, squared, inverse, cross, traits = refs[:6]
-    parts = refs[6 : 6 + n_groups]
-    blocks = refs[6 + n_groups : 6 + n_groups + n]
-    out, cross_v, joined, traits_v, blocks_v, projected, scaled, out_v, sems, out_sems = refs[-10:]
+        total = total + levels(value, place, squared, lambdas, order[i : i + 2])
+    level[...] = total
+
+
+def fitted_body(n_groups, order, *refs):
+    n = len(order)
+    place, lambdas, squared, level, cross, traits, samples = refs[:7]
+    parts = refs[7 : 7 + n_groups]
+    blocks = refs[7 + n_groups : 7 + n_groups + n]
+    out, cross_v, joined, traits_v, samples_v, blocks_v, projected = refs[-11:-4]
+    scaled, out_v, sems, out_sems = refs[-4:]
     depth = blocks[0].shape[1]
     width, span = cross.shape[1:]
     pairs = [(cross.at[half], cross_v.at[:, half * span : (half + 1) * span]) for half in range(2)]
     pairs += [(blocks[i], blocks_v.at[:, i * depth : (i + 1) * depth]) for i in range(n)]
+    pairs.append((samples, samples_v))
     at = 0
     for part in parts:
         pairs.append((part, joined.at[:, at : at + part.shape[1]]))
@@ -157,9 +163,17 @@
         projected[:, here] = jnp.dot(
             cross_v[...], blocks_v[:, here], preferred_element_type=jnp.float32
         ).astype(jnp.bfloat16)
-    for copy in copies[n + 2 :]:
+    copies[n + 2].wait()
+    here = slice(at, n * depth)
+    value = jnp.dot(
+        samples_v[...], blocks_v[:, here], preferred_element_type=jnp.float32
+    ).astype(jnp.bfloat16)
+    joined[:, here] = value
+    n_l = lambdas.shape[0]
+    total = level[...] + levels(value, place, squared, lambdas, order[at // depth :])
+    inverse = 1.0 / jnp.maximum(1.0 - (total[:, :n_l] + total[:, n_l:]), 0.25)
+    for copy in copies[n + 3 :]:
         copy.wait()
-    n_l = lambdas.shape[0]
     results = []
     for pair in range(n_l // 2):
         for i, block in enumerate(order):
@@ -226,20 +240,21 @@
     total = call(
         sum_body,
         jax.ShapeDtypeStruct(pieces, bf16),
-        [whole(*pieces)],
-        whole(*pieces),
+        [pl.BlockSpec((*pieces[:2], pieces[2] // 4), lambda i: (0, 0, i))],
+        pl.BlockSpec((*pieces[:2], pieces[2] // 4), lambda i: (0, 0, i)),
         features * width,
         4 * features * width,
-        SMALL,
+        FULL,
+        grid=(4,),
     )(arrived)
     cross = lax.all_to_all(total, SAMP, 0, 0)
 
-    def components(order, extra, last):
+    def components(order, extra):
         n = len(order)
         first = not extra
-        columns = n_l if last else 2 * n_l
+        columns = 2 * n_l
         return call(
-            lambda *refs: components_body(first, last, order, *refs),
+            lambda *refs: components_body(first, order, *refs),
             (
                 jax.ShapeDtypeStruct((rows, n * depth), bf16),
                 jax.ShapeDtypeStruct((rows, columns), f32),
@@ -259,17 +274,17 @@
         )(place, lambdas, squared, samples, *[blocks[b] for b in order], *extra)
 
     parts, state = [], ()
-    for i, group in enumerate(GROUPS):
-        part, level = components(group, state, i == len(GROUPS) - 1)
+    for group in GROUPS:
+        part, level = components(group, state)
         parts.append(part)
         state = (level,)
 
-    order = sum(GROUPS, ())
+    order = sum(GROUPS, ()) + LAST
     return call(
-        lambda *refs: fitted_body(GROUPS, order, *refs),
+        lambda *refs: fitted_body(len(GROUPS), order, *refs),
         jax.ShapeDtypeStruct((n_l, rows, width), f32),
-        [SCALAR, SCALAR, whole(n_blocks, depth), whole(rows, n_l)]
-        + [HBM] * (n_blocks + len(GROUPS) + 2),
+        [SCALAR, SCALAR, whole(n_blocks, depth), whole(rows, 2 * n_l)]
+        + [HBM] * (n_blocks + len(GROUPS) + 3),
         HBM,
         2 * n_l * rows * every * width,
         2 * rows * every + 2 * every * width + 4 * n_l * rows * width,
@@ -278,15 +293,16 @@
             pltpu.VMEM((width, features), bf16),
             pltpu.VMEM((rows, every), bf16),
             pltpu.VMEM((rows, width), bf16),
+            pltpu.VMEM((rows, features), bf16),
             pltpu.VMEM((features, every), bf16),
             pltpu.VMEM((width, every), bf16),
             pltpu.VMEM((n_l // 2, 2 * width, every), bf16),
             pltpu.VMEM((n_l, rows, width), f32),
-            dma((n_blocks + len(GROUPS) + 3,)),
+            dma((n_blocks + len(GROUPS) + 4,)),
             dma((n_l,)),
         ],
     )(
-        place, lambdas, squared, level, cross.reshape(2, width, -1), traits,
+        place, lambdas, squared, level, cross.reshape(2, width, -1), traits, samples,
         *parts,
         *[blocks[b] for b in order],
     )

time: 112 us -> 107 us (0.955)
  starting transfers between devices: 58.1 us -> 46.9 us
  waiting for transfers between devices: 17.5 us -> 22.9 us
  Pallas kernels: 34.2 us -> 35.4 us
    ppermute x4, starting transfers between devices: 22.9 us -> 11.3 us  [compute(): blocks[shift, 1] = lax.ppermute(blocks[shift, 0], 'core', [(0, 1), (1, 0)])]
    ppermute x3, waiting for transfers between devices: 0.01 us -> 5.54 us  [compute(): lax.ppermute(whitening, 'x', [(i, (i + shift) % n_x) for i in range(n_x)])]
    pallas_call x5, Pallas kernels: 29.8 us -> 31 us  [the longest x3 16.5 us: components(): call(lambda *refs: components_body(first, order, *refs), (jax.ShapeDtypeS...]
  transfers between devices with their start and end apart: 9 -> 9, of which waited for: 1 -> 2; matrix products, arithmetic and copies ran while one was open for 1% -> 1% of each run, Pallas kernels for 18% -> 19%
where the time goes in v6:
time: 107 us
  starting transfers between devices  46.9 us (44%)
  Pallas kernels  35.4 us (33%)
  waiting for transfers between devices  22.9 us (21%)
    all_to_all x1, starting transfers between devices, compute(): arrived = lax.all_to_all(partial, SAMP, 0, 0)  17.4 us
    all_to_all x1, waiting for transfers between devices, compute(): arrived = lax.all_to_all(partial, SAMP, 0, 0)  17.4 us
    pallas_call x3, Pallas kernels, components(): call(lambda *refs: components_body(first, order, *refs), (jax.ShapeDtypeS...  16.5 us
    ppermute x4, starting transfers between devices, compute(): blocks[shift, 1] = lax.ppermute(blocks[shift, 0], 'core', [(0, 1), (1, 0)])  11.3 us
    pallas_call x1, Pallas kernels, compute(): call(lambda *refs: fitted_body(len(GROUPS), order, *refs), jax.ShapeDtype...  11 us
    ppermute x3, starting transfers between devices, compute(): lax.ppermute(whitening, 'x', [(i, (i + shift) % n_x) for i in range(n_x)])  9.95 us
    all_to_all x1, starting transfers between devices, compute(): cross = lax.all_to_all(total, SAMP, 0, 0)  8.17 us
    ppermute x3, waiting for transfers between devices, compute(): lax.ppermute(whitening, 'x', [(i, (i + shift) % n_x) for i in range(n_x)])  5.54 us
  transfers between devices with their start and end apart: 9, of which 2 were waited for; matrix products, arithmetic and copies ran while one was open for 1% of the time, Pallas kernels for 19%

profile of v6, /device:TPU:1, one launch (start us, length us, event | category | flops | bytes accessed | tf_op | source)
XLA Modules:
  0.0 106.7 jit_solution(16056892374772659620)
XLA Ops:
  0.0 4.4 %shard_map.58 = bf16[64,8,1024]{2,1,0:T(8,128)(2,1)} custom-call(bf16[512,2048]{1,0:T(8,128)(2,1)} %refs_6_.1, bf16[512,256]{1,0:T(8,128)(2,1)} %refs_5_.1), custom_call_target="tpu_custom_call" | custom-call | flops 536870912 | bytes 3407872 | tf_op jit(solution)/shard_map/pallas_call | solution.py:219
  4.4 17.4 %all-to-all-start = ((bf16[64,8,1024]{2,1,0:T(8,128)(2,1)}), bf16[64,8,1024]{2,1,0:T(8,128)(2,1)}, u32[]{:S(2)}, u32[]{:S(2)}) async-start(bf16[64,8,1024]{2,1,0:T(8,128)(2,1)} %shard_map.58), calls=%async_computation | async-start | bytes 2097152 | tf_op jit(solution)/shard_map/all_to_all | solution.py:229
  21.8 4.7 %collective-permute-start.2 = (bf16[2048,256]{1,0:T(8,128)(2,1)}, bf16[2048,256]{1,0:T(8,128)(2,1)}, u32[]{:S(2)}, u32[]{:S(2)}) collective-permute-start(bf16[2048,256]{1,0:T(8,128)(2,1)} %refs_10_.1), channel_id=1, source_target_pairs={{0,4},{2,6},{4,0},{6,2},{1,5},{3,7},{5,1},{7,3},{8,12},{10,14},{12... | collective-permute-start | bytes 3145736 | tf_op jit(solution)/shard_map/ppermute | solution.py:233
  26.5 2.8 %collective-permute-start.1 = (bf16[2048,256]{1,0:T(8,128)(2,1)}, bf16[2048,256]{1,0:T(8,128)(2,1)}, u32[]{:S(2)}, u32[]{:S(2)}) collective-permute-start(bf16[2048,256]{1,0:T(8,128)(2,1)} %refs_10_.1), channel_id=1, source_target_pairs={{0,6},{2,0},{4,2},{6,4},{1,7},{3,1},{5,3},{7,5},{8,14},{10,8},{12,... | collective-permute-start | bytes 3145736 | tf_op jit(solution)/shard_map/ppermute | solution.py:233
  29.3 2.5 %collective-permute-start = (bf16[2048,256]{1,0:T(8,128)(2,1)}, bf16[2048,256]{1,0:T(8,128)(2,1)}, u32[]{:S(2)}, u32[]{:S(2)}) collective-permute-start(bf16[2048,256]{1,0:T(8,128)(2,1)} %refs_10_.1), channel_id=1, source_target_pairs={{0,2},{2,4},{4,6},{6,0},{1,3},{3,5},{5,7},{7,1},{8,10},{10,12},{12... | collective-permute-start | bytes 3145736 | tf_op jit(solution)/shard_map/ppermute | solution.py:233
  31.8 17.4 %all-to-all-done.arrived = bf16[64,8,1024]{2,1,0:T(8,128)(2,1)} async-done(((bf16[64,8,1024]{2,1,0:T(8,128)(2,1)}), bf16[64,8,1024]{2,1,0:T(8,128)(2,1)}, u32[]{:S(2)}, u32[]{:S(2)}) %all-to-all-start) | async-done | bytes 1048608 | tf_op jit(solution)/shard_map/all_to_all | solution.py:229
  49.1 3.5 %shard_map.59 = bf16[64,8,1024]{2,1,0:T(8,128)(2,1)} custom-call(bf16[64,8,1024]{2,1,0:T(8,128)(2,1)} %all-to-all-done.arrived), custom_call_target="tpu_custom_call" | custom-call | flops 524288 | bytes 2097152 | tf_op jit(solution)/shard_map/pallas_call | solution.py:240
  52.6 0.0 copy-start
  52.6 8.2 %all-to-all-start.1 = ((bf16[64,8,1024]{2,1,0:T(8,128)(2,1)}), bf16[64,8,1024]{2,1,0:T(8,128)(2,1)}, u32[]{:S(2)}, u32[]{:S(2)}) async-start(bf16[64,8,1024]{2,1,0:T(8,128)(2,1)} %shard_map.59), calls=%async_computation.1 | async-start | bytes 2097152 | tf_op jit(solution)/shard_map/all_to_all | solution.py:250
  60.8 3.9 %collective-permute-start.4 = (bf16[2048,256]{1,0:T(8,128)(2,1)}, bf16[2048,256]{1,0:T(8,128)(2,1)}, u32[]{:S(2)}, u32[]{:S(2)}) collective-permute-start(bf16[2048,256]{1,0:T(8,128)(2,1)} %refs_10_.1), channel_id=1, source_target_pairs={{0,1},{1,0},{2,3},{3,2},{4,5},{5,4},{6,7},{7,6},{8,9},{9,8},{10,11... | collective-permute-start | bytes 3145736 | tf_op jit(solution)/shard_map/ppermute | solution.py:238
  64.7 0.0 collective-permute-done.2.refs_4_.refs_12_
  64.7 1.9 %collective-permute-start.3 = (bf16[2048,256]{1,0:T(8,128)(2,1)}, bf16[2048,256]{1,0:T(8,128)(2,1)}, u32[]{:S(2)}, u32[]{:S(2)}) collective-permute-start(bf16[2048,256]{1,0:T(8,128)(2,1)} %collective-permute-done.2.refs_4_.refs_12_), channel_id=1, source_target_pairs={{0,1},{1,0},{2,3},{3,2},{4,5},{5,4},{6,7},{7,6},{8,9},{9,8},{10,11... | collective-permute-start | bytes 3145736 | tf_op jit(solution)/shard_map/ppermute | solution.py:238
  66.6 5.5 %collective-permute-done.1.refs_5_.refs_15_ = bf16[2048,256]{1,0:T(8,128)(2,1)} collective-permute-done((bf16[2048,256]{1,0:T(8,128)(2,1)}, bf16[2048,256]{1,0:T(8,128)(2,1)}, u32[]{:S(2)}, u32[]{:S(2)}) %collective-permute-start.1) | collective-permute-done | bytes 1048608 | tf_op jit(solution)/shard_map/ppermute | solution.py:233
  72.2 3.5 %collective-permute-start.6 = (bf16[2048,256]{1,0:T(8,128)(2,1)}, bf16[2048,256]{1,0:T(8,128)(2,1)}, u32[]{:S(2)}, u32[]{:S(2)}) collective-permute-start(bf16[2048,256]{1,0:T(8,128)(2,1)} %collective-permute-done.1.refs_5_.refs_15_), channel_id=1, source_target_pairs={{0,1},{1,0},{2,3},{3,2},{4,5},{5,4},{6,7},{7,6},{8,9},{9,8},{10,11... | collective-permute-start | bytes 3145736 | tf_op jit(solution)/shard_map/ppermute | solution.py:238
  75.6 0.0 collective-permute-done.refs_4_.refs_14_
  75.6 2.1 %collective-permute-start.5 = (bf16[2048,256]{1,0:T(8,128)(2,1)}, bf16[2048,256]{1,0:T(8,128)(2,1)}, u32[]{:S(2)}, u32[]{:S(2)}) collective-permute-start(bf16[2048,256]{1,0:T(8,128)(2,1)} %collective-permute-done.refs_4_.refs_14_), channel_id=1, source_target_pairs={{0,1},{1,0},{2,3},{3,2},{4,5},{5,4},{6,7},{7,6},{8,9},{9,8},{10,11... | collective-permute-start | bytes 3145736 | tf_op jit(solution)/shard_map/ppermute | solution.py:238
  77.7 0.0 copy-done
  77.8 0.6 reshape.6.refs_2_
  78.4 0.6 pad_add_fusion.refs_0_
  79.0 0.0 collective-permute-done.4.refs_5_.refs_11_
  79.0 5.5 %shard_map.55 = (bf16[512,512]{1,0:T(8,128)(2,1)}, f32[512,8]{1,0:T(8,128)}) custom-call(s32[2]{0:T(128)} %pad_add_fusion.refs_0_, f32[4]{0:T(128)} %refs_1_.7, f32[8,256]{1,0:T(8,128)} %reshape.6.refs_2_, bf16[512,2048]{1,0:T(8,128)(2,1)} %refs_6_.1, bf16[2048,256]{1,0:T(8,128)(2,1)} %refs_10_.1, bf16[2048,256]{1,0:T(8,128)(2,1)} %collective-permute-done.4.refs_5_.refs_11_), custom_call_target="tpu_custom_call" | custom-call | flops 1073741824 | bytes 4718592 | tf_op jit(solution)/shard_map/pallas_call | solution.py:256
  84.5 0.0 collective-permute-done.3.refs_5_.refs_13_
  84.5 5.5 %shard_map.56 = (bf16[512,512]{1,0:T(8,128)(2,1)}, f32[512,8]{1,0:T(8,128)}) custom-call(s32[2]{0:T(128)} %pad_add_fusion.refs_0_, f32[4]{0:T(128)} %refs_1_.7, f32[8,256]{1,0:T(8,128)} %reshape.6.refs_2_, bf16[512,2048]{1,0:T(8,128)(2,1)} %refs_6_.1, bf16[2048,256]{1,0:T(8,128)(2,1)} %collective-permute-done.2.refs_4_.refs_12_, ...), custom_call_target="tpu_custom_call" | custom-call | flops 1073741824 | bytes 4718592 | tf_op jit(solution)/shard_map/pallas_call | solution.py:256
  90.0 5.5 %shard_map.57 = (bf16[512,512]{1,0:T(8,128)(2,1)}, f32[512,8]{1,0:T(8,128)}) custom-call(s32[2]{0:T(128)} %pad_add_fusion.refs_0_, f32[4]{0:T(128)} %refs_1_.7, f32[8,256]{1,0:T(8,128)} %reshape.6.refs_2_, bf16[512,2048]{1,0:T(8,128)(2,1)} %refs_6_.1, bf16[2048,256]{1,0:T(8,128)(2,1)} %collective-permute-done.refs_4_.refs_14_, ...), custom_call_target="tpu_custom_call" | custom-call | flops 1073741824 | bytes 4718592 | tf_op jit(solution)/shard_map/pallas_call | solution.py:256
  95.5 0.0 collective-permute-done.6.refs_17_
  95.5 0.0 collective-permute-done.5.refs_16_
  95.5 0.0 all-to-all-done.1
  95.5 11.0 %shard_map.60 = f32[4,512,256]{2,1,0:T(8,128)} custom-call(s32[2]{0:T(128)} %pad_add_fusion.refs_0_, f32[4]{0:T(128)} %refs_1_.7, f32[8,256]{1,0:T(8,128)} %reshape.6.refs_2_, f32[512,8]{1,0:T(8,128)} %get-tuple-element.13.refs_3_, bf16[2,256,1024]{2,1,0:T(8,128)(2,1)} %bitcast.2.refs_4_, bf16[512,256]{1,0:T(8,128)(2,1)} %refs_5_.1, ...), custom_call_target="tpu_custom_call" | custom-call | flops 2147483648 | bytes 5242880 | tf_op jit(solution)/shard_map/pallas_call | solution.py:283
  (1 shorter events, 0.0 us)
Async XLA Ops:
  4.4 44.7 %all-to-all-start = ((bf16[64,8,1024]{2,1,0:T(8,128)(2,1)}), bf16[64,8,1024]{2,1,0:T(8,128)(2,1)}, u32[]{:S(2)}, u32[]{:S(2)}) async-start(bf16[64,8,1024]{2,1,0:T(8,128)(2,1)} %shard_map.58), calls=%async_computation | async-start | bytes 2097152 | tf_op jit(solution)/shard_map/all_to_all | solution.py:229
  21.8 42.9 %collective-permute-start.2 = (bf16[2048,256]{1,0:T(8,128)(2,1)}, bf16[2048,256]{1,0:T(8,128)(2,1)}, u32[]{:S(2)}, u32[]{:S(2)}) collective-permute-start(bf16[2048,256]{1,0:T(8,128)(2,1)} %refs_10_.1), channel_id=1, source_target_pairs={{0,4},{2,6},{4,0},{6,2},{1,5},{3,7},{5,1},{7,3},{8,12},{10,14},{12... | collective-permute-start | bytes 3145736 | tf_op jit(solution)/shard_map/ppermute | solution.py:233
  26.5 45.7 %collective-permute-start.1 = (bf16[2048,256]{1,0:T(8,128)(2,1)}, bf16[2048,256]{1,0:T(8,128)(2,1)}, u32[]{:S(2)}, u32[]{:S(2)}) collective-permute-start(bf16[2048,256]{1,0:T(8,128)(2,1)} %refs_10_.1), channel_id=1, source_target_pairs={{0,6},{2,0},{4,2},{6,4},{1,7},{3,1},{5,3},{7,5},{8,14},{10,8},{12,... | collective-permute-start | bytes 3145736 | tf_op jit(solution)/shard_map/ppermute | solution.py:233
  29.3 46.4 %collective-permute-start = (bf16[2048,256]{1,0:T(8,128)(2,1)}, bf16[2048,256]{1,0:T(8,128)(2,1)}, u32[]{:S(2)}, u32[]{:S(2)}) collective-permute-start(bf16[2048,256]{1,0:T(8,128)(2,1)} %refs_10_.1), channel_id=1, source_target_pairs={{0,2},{2,4},{4,6},{6,0},{1,3},{3,5},{5,7},{7,1},{8,10},{10,12},{12... | collective-permute-start | bytes 3145736 | tf_op jit(solution)/shard_map/ppermute | solution.py:233
  52.6 25.1 %copy-start = (f32[2048]{0:T(1024)S(1)}, f32[2048]{0:T(1024)}, u32[]{:S(2)}) copy-start(f32[2048]{0:T(1024)} %param.8) | copy-start | bytes 24580
  52.6 42.9 %all-to-all-start.1 = ((bf16[64,8,1024]{2,1,0:T(8,128)(2,1)}), bf16[64,8,1024]{2,1,0:T(8,128)(2,1)}, u32[]{:S(2)}, u32[]{:S(2)}) async-start(bf16[64,8,1024]{2,1,0:T(8,128)(2,1)} %shard_map.59), calls=%async_computation.1 | async-start | bytes 2097152 | tf_op jit(solution)/shard_map/all_to_all | solution.py:250
  60.8 18.2 %collective-permute-start.4 = (bf16[2048,256]{1,0:T(8,128)(2,1)}, bf16[2048,256]{1,0:T(8,128)(2,1)}, u32[]{:S(2)}, u32[]{:S(2)}) collective-permute-start(bf16[2048,256]{1,0:T(8,128)(2,1)} %refs_10_.1), channel_id=1, source_target_pairs={{0,1},{1,0},{2,3},{3,2},{4,5},{5,4},{6,7},{7,6},{8,9},{9,8},{10,11... | collective-permute-start | bytes 3145736 | tf_op jit(solution)/shard_map/ppermute | solution.py:238
  64.7 19.8 %collective-permute-start.3 = (bf16[2048,256]{1,0:T(8,128)(2,1)}, bf16[2048,256]{1,0:T(8,128)(2,1)}, u32[]{:S(2)}, u32[]{:S(2)}) collective-permute-start(bf16[2048,256]{1,0:T(8,128)(2,1)} %collective-permute-done.2.refs_4_.refs_12_), channel_id=1, source_target_pairs={{0,1},{1,0},{2,3},{3,2},{4,5},{5,4},{6,7},{7,6},{8,9},{9,8},{10,11... | collective-permute-start | bytes 3145736 | tf_op jit(solution)/shard_map/ppermute | solution.py:238
  72.2 23.3 %collective-permute-start.6 = (bf16[2048,256]{1,0:T(8,128)(2,1)}, bf16[2048,256]{1,0:T(8,128)(2,1)}, u32[]{:S(2)}, u32[]{:S(2)}) collective-permute-start(bf16[2048,256]{1,0:T(8,128)(2,1)} %collective-permute-done.1.refs_5_.refs_15_), channel_id=1, source_target_pairs={{0,1},{1,0},{2,3},{3,2},{4,5},{5,4},{6,7},{7,6},{8,9},{9,8},{10,11... | collective-permute-start | bytes 3145736 | tf_op jit(solution)/shard_map/ppermute | solution.py:238
  75.6 19.9 %collective-permute-start.5 = (bf16[2048,256]{1,0:T(8,128)(2,1)}, bf16[2048,256]{1,0:T(8,128)(2,1)}, u32[]{:S(2)}, u32[]{:S(2)}) collective-permute-start(bf16[2048,256]{1,0:T(8,128)(2,1)} %collective-permute-done.refs_4_.refs_14_), channel_id=1, source_target_pairs={{0,1},{1,0},{2,3},{3,2},{4,5},{5,4},{6,7},{7,6},{8,9},{9,8},{10,11... | collective-permute-start | bytes 3145736 | tf_op jit(solution)/shard_map/ppermute | solution.py:238

commit v7 on v6

--- a/solution.py
+++ b/solution.py
@@ -32,7 +32,7 @@
     )
 
 
-def cross_body(samples, traits, out, samples_v, traits_v, sems):
+def cross_body(samples, traits, out, samples_v, traits_v, out_v, sems, out_sems):
     n = samples_v.shape[0]
     _, cols = samples_v.shape[1:]
     copies = [pltpu.make_async_copy(traits, traits_v, sems.at[n])]
@@ -48,22 +48,53 @@
     flipped = traits_v[...].T
     span = out.shape[2]
     groups = out.shape[0] // 2
+    results = []
     for i in range(n):
         copies[i + 1].wait()
         piece = jnp.dot(flipped, samples_v[i], preferred_element_type=jnp.float32)
+        out_v[i] = piece.astype(jnp.bfloat16).reshape(groups, -1, cols)
         half, at = divmod(i * cols, span)
-        out[half * groups : (half + 1) * groups, :, at : at + cols] = piece.astype(
-            jnp.bfloat16
-        ).reshape(groups, -1, cols)
-
-
-def sum_body(arrived, out):
-    total = arrived[0].astype(jnp.float32)
-    for i in range(1, arrived.shape[0]):
-        total = total + arrived[i].astype(jnp.float32)
+        results.append(
+            pltpu.make_async_copy(
+                out_v.at[i],
+                out.at[half * groups : (half + 1) * groups, :, at : at + cols],
+                out_sems.at[i],
+            )
+        )
+        results[-1].start()
+    for copy in results:
+        copy.wait()
+
+
+def sum_body(arrived, out, arrived_v, out_v, sems, out_sems):
+    n = sems.shape[0]
+    part = arrived.shape[0] // n
+    copies = [
+        pltpu.make_async_copy(
+            arrived.at[i * part : (i + 1) * part],
+            arrived_v.at[i * part : (i + 1) * part],
+            sems.at[i],
+        )
+        for i in range(n)
+    ]
+    for copy in copies:
+        copy.start()
+    total = 0.0
+    for i in range(n):
+        copies[i].wait()
+        for j in range(i * part, (i + 1) * part):
+            total = total + arrived_v[j].astype(jnp.float32)
     total = total.astype(jnp.bfloat16)
-    for i in range(out.shape[0]):
-        out[i] = total
+    for i in range(part):
+        out_v[i] = total
+    results = [
+        pltpu.make_async_copy(out_v, out.at[i * part : (i + 1) * part], out_sems.at[i])
+        for i in range(n)
+    ]
+    for copy in results:
+        copy.start()
+    for copy in results:
+        copy.wait()
 
 
 def row_of(place, shift, swap):
@@ -136,10 +167,11 @@
     place, lambdas, squared, level, cross, traits, samples = refs[:7]
     parts = refs[7 : 7 + n_groups]
     blocks = refs[7 + n_groups : 7 + n_groups + n]
-    out, cross_v, joined, traits_v, samples_v, blocks_v, projected = refs[-11:-4]
+    out, cross_v, joined, traits_v, samples_v, blocks_v = refs[-10:-4]
     scaled, out_v, sems, out_sems = refs[-4:]
     depth = blocks[0].shape[1]
     width, span = cross.shape[1:]
+    n_l = lambdas.shape[0]
     pairs = [(cross.at[half], cross_v.at[:, half * span : (half + 1) * span]) for half in range(2)]
     pairs += [(blocks[i], blocks_v.at[:, i * depth : (i + 1) * depth]) for i in range(n)]
     pairs.append((samples, samples_v))
@@ -160,34 +192,29 @@
         copies[i + 2].wait()
         copies[i + 3].wait()
         here = slice(i * depth, (i + 2) * depth)
-        projected[:, here] = jnp.dot(
-            cross_v[...], blocks_v[:, here], preferred_element_type=jnp.float32
-        ).astype(jnp.bfloat16)
+        value = jnp.dot(cross_v[...], blocks_v[:, here], preferred_element_type=jnp.float32)
+        value = value.astype(jnp.bfloat16).astype(jnp.float32)
+        for j, block in enumerate(order[i : i + 2]):
+            columns = slice((i + j) * depth, (i + j + 1) * depth)
+            for l, shrink in enumerate(shrink_of(place, squared, lambdas, block, range(n_l))):
+                scaled[l * width : (l + 1) * width, columns] = (
+                    value[:, j * depth : (j + 1) * depth] * shrink
+                ).astype(jnp.bfloat16)
     copies[n + 2].wait()
     here = slice(at, n * depth)
     value = jnp.dot(
         samples_v[...], blocks_v[:, here], preferred_element_type=jnp.float32
     ).astype(jnp.bfloat16)
     joined[:, here] = value
-    n_l = lambdas.shape[0]
     total = level[...] + levels(value, place, squared, lambdas, order[at // depth :])
     inverse = 1.0 / jnp.maximum(1.0 - (total[:, :n_l] + total[:, n_l:]), 0.25)
     for copy in copies[n + 3 :]:
         copy.wait()
     results = []
     for pair in range(n_l // 2):
-        for i, block in enumerate(order):
-            here = slice(i * depth, (i + 1) * depth)
-            value = projected[:, here].astype(jnp.float32)
-            for j, shrink in enumerate(
-                shrink_of(place, squared, lambdas, block, (2 * pair, 2 * pair + 1))
-            ):
-                scaled[pair, j * width : (j + 1) * width, here] = (value * shrink).astype(
-                    jnp.bfloat16
-                )
         fitted = lax.dot_general(
             joined[...],
-            scaled[pair],
+            scaled[2 * pair * width : 2 * (pair + 1) * width],
             (((1,), (1,)), ((), ())),
             preferred_element_type=jnp.float32,
         )
@@ -220,11 +247,17 @@
         cross_body,
         jax.ShapeDtypeStruct(pieces, bf16),
         [HBM, HBM],
-        whole(*pieces),
+        HBM,
         2 * rows * width * features,
         2 * (rows * width + rows * features + features * width),
         FULL,
-        [pltpu.VMEM((8, rows, features // 8), bf16), pltpu.VMEM((rows, width), bf16), dma((9,))],
+        [
+            pltpu.VMEM((4, rows, features // 4), bf16),
+            pltpu.VMEM((rows, width), bf16),
+            pltpu.VMEM((4, pieces[0] // 2, pieces[1], features // 4), bf16),
+            dma((5,)),
+            dma((4,)),
+        ],
     )(samples, traits)
     arrived = lax.all_to_all(partial, SAMP, 0, 0)
 
@@ -240,12 +273,17 @@
     total = call(
         sum_body,
         jax.ShapeDtypeStruct(pieces, bf16),
-        [pl.BlockSpec((*pieces[:2], pieces[2] // 4), lambda i: (0, 0, i))],
-        pl.BlockSpec((*pieces[:2], pieces[2] // 4), lambda i: (0, 0, i)),
+        [HBM],
+        HBM,
         features * width,
         4 * features * width,
         FULL,
-        grid=(4,),
+        [
+            pltpu.VMEM(pieces, bf16),
+            pltpu.VMEM((pieces[0] // 4, *pieces[1:]), bf16),
+            dma((4,)),
+            dma((4,)),
+        ],
     )(arrived)
     cross = lax.all_to_all(total, SAMP, 0, 0)
 
@@ -295,8 +333,7 @@
             pltpu.VMEM((rows, width), bf16),
             pltpu.VMEM((rows, features), bf16),
             pltpu.VMEM((features, every), bf16),
-            pltpu.VMEM((width, every), bf16),
-            pltpu.VMEM((n_l // 2, 2 * width, every), bf16),
+            pltpu.VMEM((n_l * width, every), bf16),
             pltpu.VMEM((n_l, rows, width), f32),
             dma((n_blocks + len(GROUPS) + 4,)),
             dma((n_l,)),

time: 107 us -> 106 us (level)
  Pallas kernels: 35.4 us -> 33.1 us
  waiting for transfers between devices: 22.9 us -> 24.2 us
    pallas_call x2, Pallas kernels: 7.9 us -> 5.38 us  [the longest x1 3.11 us: compute(): call(cross_body, jax.ShapeDtypeStruct(pieces, bf16), [HBM, HBM], HBM, 2 *...]
    ppermute x3, waiting for transfers between devices: 5.54 us -> 6.87 us  [compute(): lax.ppermute(whitening, 'x', [(i, (i + shift) % n_x) for i in range(n_x)])]
  transfers between devices with their start and end apart: 9 -> 9, of which waited for: 2 -> 2; matrix products, arithmetic and copies ran while one was open for 1% -> 1% of each run, Pallas kernels for 19% -> 18%
where the time goes in v7:
time: 106 us; the launch traced here: 105 us
  starting transfers between devices  46.6 us (44%)
  Pallas kernels  33.1 us (31%)
  waiting for transfers between devices  24.2 us (23%)
    all_to_all x1, starting transfers between devices, compute(): arrived = lax.all_to_all(partial, SAMP, 0, 0)  17.4 us
    all_to_all x1, waiting for transfers between devices, compute(): arrived = lax.all_to_all(partial, SAMP, 0, 0)  17.4 us
    pallas_call x3, Pallas kernels, components(): call(lambda *refs: components_body(first, order, *refs), (jax.ShapeDtypeS...  16.5 us
    pallas_call x1, Pallas kernels, compute(): call(lambda *refs: fitted_body(len(GROUPS), order, *refs), jax.ShapeDtype...  11.3 us
    ppermute x4, starting transfers between devices, compute(): blocks[shift, 1] = lax.ppermute(blocks[shift, 0], 'core', [(0, 1), (1, 0)])  11.1 us
    ppermute x3, starting transfers between devices, compute(): lax.ppermute(whitening, 'x', [(i, (i + shift) % n_x) for i in range(n_x)])  9.95 us
    all_to_all x1, starting transfers between devices, compute(): cross = lax.all_to_all(total, SAMP, 0, 0)  8.05 us
    ppermute x3, waiting for transfers between devices, compute(): lax.ppermute(whitening, 'x', [(i, (i + shift) % n_x) for i in range(n_x)])  6.87 us
  transfers between devices with their start and end apart: 9, of which 2 were waited for; matrix products, arithmetic and copies ran while one was open for 1% of the time, Pallas kernels for 18%

profile of v7, /device:TPU:1, one launch (start us, length us, event | category | flops | bytes accessed | tf_op | source)
XLA Modules:
  0.0 105.3 jit_solution(8031872281500829398)
XLA Ops:
  0.0 3.1 %shard_map.58 = bf16[64,8,1024]{2,1,0:T(8,128)(2,1)} custom-call(bf16[512,2048]{1,0:T(8,128)(2,1)} %refs_6_.1, bf16[512,256]{1,0:T(8,128)(2,1)} %refs_5_.1), custom_call_target="tpu_custom_call" | custom-call | flops 536870912 | bytes 3407872 | tf_op jit(solution)/shard_map/pallas_call | solution.py:246
  3.1 17.4 %all-to-all-start = ((bf16[64,8,1024]{2,1,0:T(8,128)(2,1)}), bf16[64,8,1024]{2,1,0:T(8,128)(2,1)}, u32[]{:S(2)}, u32[]{:S(2)}) async-start(bf16[64,8,1024]{2,1,0:T(8,128)(2,1)} %shard_map.58), calls=%async_computation | async-start | bytes 2097152 | tf_op jit(solution)/shard_map/all_to_all | solution.py:262
  20.5 4.7 %collective-permute-start.2 = (bf16[2048,256]{1,0:T(8,128)(2,1)}, bf16[2048,256]{1,0:T(8,128)(2,1)}, u32[]{:S(2)}, u32[]{:S(2)}) collective-permute-start(bf16[2048,256]{1,0:T(8,128)(2,1)} %refs_10_.1), channel_id=1, source_target_pairs={{0,4},{2,6},{4,0},{6,2},{1,5},{3,7},{5,1},{7,3},{8,12},{10,14},{12... | collective-permute-start | bytes 3145736 | tf_op jit(solution)/shard_map/ppermute | solution.py:266
  25.2 2.8 %collective-permute-start.1 = (bf16[2048,256]{1,0:T(8,128)(2,1)}, bf16[2048,256]{1,0:T(8,128)(2,1)}, u32[]{:S(2)}, u32[]{:S(2)}) collective-permute-start(bf16[2048,256]{1,0:T(8,128)(2,1)} %refs_10_.1), channel_id=1, source_target_pairs={{0,6},{2,0},{4,2},{6,4},{1,7},{3,1},{5,3},{7,5},{8,14},{10,8},{12,... | collective-permute-start | bytes 3145736 | tf_op jit(solution)/shard_map/ppermute | solution.py:266
  28.0 2.5 %collective-permute-start = (bf16[2048,256]{1,0:T(8,128)(2,1)}, bf16[2048,256]{1,0:T(8,128)(2,1)}, u32[]{:S(2)}, u32[]{:S(2)}) collective-permute-start(bf16[2048,256]{1,0:T(8,128)(2,1)} %refs_10_.1), channel_id=1, source_target_pairs={{0,2},{2,4},{4,6},{6,0},{1,3},{3,5},{5,7},{7,1},{8,10},{10,12},{12... | collective-permute-start | bytes 3145736 | tf_op jit(solution)/shard_map/ppermute | solution.py:266
  30.5 17.4 %all-to-all-done.arrived = bf16[64,8,1024]{2,1,0:T(8,128)(2,1)} async-done(((bf16[64,8,1024]{2,1,0:T(8,128)(2,1)}), bf16[64,8,1024]{2,1,0:T(8,128)(2,1)}, u32[]{:S(2)}, u32[]{:S(2)}) %all-to-all-start) | async-done | bytes 1048608 | tf_op jit(solution)/shard_map/all_to_all | solution.py:262
  47.9 2.3 %shard_map.59 = bf16[64,8,1024]{2,1,0:T(8,128)(2,1)} custom-call(bf16[64,8,1024]{2,1,0:T(8,128)(2,1)} %all-to-all-done.arrived), custom_call_target="tpu_custom_call" | custom-call | flops 524288 | bytes 2097152 | tf_op jit(solution)/shard_map/pallas_call | solution.py:273
  50.1 0.0 copy-start
  50.1 8.1 %all-to-all-start.1 = ((bf16[64,8,1024]{2,1,0:T(8,128)(2,1)}), bf16[64,8,1024]{2,1,0:T(8,128)(2,1)}, u32[]{:S(2)}, u32[]{:S(2)}) async-start(bf16[64,8,1024]{2,1,0:T(8,128)(2,1)} %shard_map.59), calls=%async_computation.1 | async-start | bytes 2097152 | tf_op jit(solution)/shard_map/all_to_all | solution.py:288
  58.2 3.9 %collective-permute-start.4 = (bf16[2048,256]{1,0:T(8,128)(2,1)}, bf16[2048,256]{1,0:T(8,128)(2,1)}, u32[]{:S(2)}, u32[]{:S(2)}) collective-permute-start(bf16[2048,256]{1,0:T(8,128)(2,1)} %refs_10_.1), channel_id=1, source_target_pairs={{0,1},{1,0},{2,3},{3,2},{4,5},{5,4},{6,7},{7,6},{8,9},{9,8},{10,11... | collective-permute-start | bytes 3145736 | tf_op jit(solution)/shard_map/ppermute | solution.py:271
  62.1 0.0 collective-permute-done.2.refs_4_.refs_12_
  62.1 1.9 %collective-permute-start.3 = (bf16[2048,256]{1,0:T(8,128)(2,1)}, bf16[2048,256]{1,0:T(8,128)(2,1)}, u32[]{:S(2)}, u32[]{:S(2)}) collective-permute-start(bf16[2048,256]{1,0:T(8,128)(2,1)} %collective-permute-done.2.refs_4_.refs_12_), channel_id=1, source_target_pairs={{0,1},{1,0},{2,3},{3,2},{4,5},{5,4},{6,7},{7,6},{8,9},{9,8},{10,11... | collective-permute-start | bytes 3145736 | tf_op jit(solution)/shard_map/ppermute | solution.py:271
  64.0 6.9 %collective-permute-done.1.refs_5_.refs_15_ = bf16[2048,256]{1,0:T(8,128)(2,1)} collective-permute-done((bf16[2048,256]{1,0:T(8,128)(2,1)}, bf16[2048,256]{1,0:T(8,128)(2,1)}, u32[]{:S(2)}, u32[]{:S(2)}) %collective-permute-start.1) | collective-permute-done | bytes 1048608 | tf_op jit(solution)/shard_map/ppermute | solution.py:266
  70.9 3.5 %collective-permute-start.6 = (bf16[2048,256]{1,0:T(8,128)(2,1)}, bf16[2048,256]{1,0:T(8,128)(2,1)}, u32[]{:S(2)}, u32[]{:S(2)}) collective-permute-start(bf16[2048,256]{1,0:T(8,128)(2,1)} %collective-permute-done.1.refs_5_.refs_15_), channel_id=1, source_target_pairs={{0,1},{1,0},{2,3},{3,2},{4,5},{5,4},{6,7},{7,6},{8,9},{9,8},{10,11... | collective-permute-start | bytes 3145736 | tf_op jit(solution)/shard_map/ppermute | solution.py:271
  74.3 0.0 collective-permute-done.refs_4_.refs_14_
  74.3 1.9 %collective-permute-start.5 = (bf16[2048,256]{1,0:T(8,128)(2,1)}, bf16[2048,256]{1,0:T(8,128)(2,1)}, u32[]{:S(2)}, u32[]{:S(2)}) collective-permute-start(bf16[2048,256]{1,0:T(8,128)(2,1)} %collective-permute-done.refs_4_.refs_14_), channel_id=1, source_target_pairs={{0,1},{1,0},{2,3},{3,2},{4,5},{5,4},{6,7},{7,6},{8,9},{9,8},{10,11... | collective-permute-start | bytes 3145736 | tf_op jit(solution)/shard_map/ppermute | solution.py:271
  76.3 0.0 copy-done
  76.3 0.6 reshape.6.refs_2_
  76.9 0.6 pad_add_fusion.refs_0_
  77.5 0.0 collective-permute-done.4.refs_5_.refs_11_
  77.5 5.5 %shard_map.55 = (bf16[512,512]{1,0:T(8,128)(2,1)}, f32[512,8]{1,0:T(8,128)}) custom-call(s32[2]{0:T(128)} %pad_add_fusion.refs_0_, f32[4]{0:T(128)} %refs_1_.7, f32[8,256]{1,0:T(8,128)} %reshape.6.refs_2_, bf16[512,2048]{1,0:T(8,128)(2,1)} %refs_6_.1, bf16[2048,256]{1,0:T(8,128)(2,1)} %refs_10_.1, bf16[2048,256]{1,0:T(8,128)(2,1)} %collective-permute-done.4.refs_5_.refs_11_), custom_call_target="tpu_custom_call" | custom-call | flops 1073741824 | bytes 4718592 | tf_op jit(solution)/shard_map/pallas_call | solution.py:294
  83.0 0.0 collective-permute-done.3.refs_5_.refs_13_
  83.1 5.5 %shard_map.56 = (bf16[512,512]{1,0:T(8,128)(2,1)}, f32[512,8]{1,0:T(8,128)}) custom-call(s32[2]{0:T(128)} %pad_add_fusion.refs_0_, f32[4]{0:T(128)} %refs_1_.7, f32[8,256]{1,0:T(8,128)} %reshape.6.refs_2_, bf16[512,2048]{1,0:T(8,128)(2,1)} %refs_6_.1, bf16[2048,256]{1,0:T(8,128)(2,1)} %collective-permute-done.2.refs_4_.refs_12_, ...), custom_call_target="tpu_custom_call" | custom-call | flops 1073741824 | bytes 4718592 | tf_op jit(solution)/shard_map/pallas_call | solution.py:294
  88.5 5.5 %shard_map.57 = (bf16[512,512]{1,0:T(8,128)(2,1)}, f32[512,8]{1,0:T(8,128)}) custom-call(s32[2]{0:T(128)} %pad_add_fusion.refs_0_, f32[4]{0:T(128)} %refs_1_.7, f32[8,256]{1,0:T(8,128)} %reshape.6.refs_2_, bf16[512,2048]{1,0:T(8,128)(2,1)} %refs_6_.1, bf16[2048,256]{1,0:T(8,128)(2,1)} %collective-permute-done.refs_4_.refs_14_, ...), custom_call_target="tpu_custom_call" | custom-call | flops 1073741824 | bytes 4718592 | tf_op jit(solution)/shard_map/pallas_call | solution.py:294
  94.0 0.0 collective-permute-done.6.refs_17_
  94.0 0.0 collective-permute-done.5.refs_16_
  94.0 0.0 all-to-all-done.1
  94.1 11.3 %shard_map.60 = f32[4,512,256]{2,1,0:T(8,128)} custom-call(s32[2]{0:T(128)} %pad_add_fusion.refs_0_, f32[4]{0:T(128)} %refs_1_.7, f32[8,256]{1,0:T(8,128)} %reshape.6.refs_2_, f32[512,8]{1,0:T(8,128)} %get-tuple-element.13.refs_3_, bf16[2,256,1024]{2,1,0:T(8,128)(2,1)} %bitcast.2.refs_4_, bf16[512,256]{1,0:T(8,128)(2,1)} %refs_5_.1, ...), custom_call_target="tpu_custom_call" | custom-call | flops 2147483648 | bytes 5242880 | tf_op jit(solution)/shard_map/pallas_call | solution.py:321
  (1 shorter events, 0.0 us)
Async XLA Ops:
  3.1 44.7 %all-to-all-start = ((bf16[64,8,1024]{2,1,0:T(8,128)(2,1)}), bf16[64,8,1024]{2,1,0:T(8,128)(2,1)}, u32[]{:S(2)}, u32[]{:S(2)}) async-start(bf16[64,8,1024]{2,1,0:T(8,128)(2,1)} %shard_map.58), calls=%async_computation | async-start | bytes 2097152 | tf_op jit(solution)/shard_map/all_to_all | solution.py:262
  20.5 41.5 %collective-permute-start.2 = (bf16[2048,256]{1,0:T(8,128)(2,1)}, bf16[2048,256]{1,0:T(8,128)(2,1)}, u32[]{:S(2)}, u32[]{:S(2)}) collective-permute-start(bf16[2048,256]{1,0:T(8,128)(2,1)} %refs_10_.1), channel_id=1, source_target_pairs={{0,4},{2,6},{4,0},{6,2},{1,5},{3,7},{5,1},{7,3},{8,12},{10,14},{12... | collective-permute-start | bytes 3145736 | tf_op jit(solution)/shard_map/ppermute | solution.py:266
  25.2 45.7 %collective-permute-start.1 = (bf16[2048,256]{1,0:T(8,128)(2,1)}, bf16[2048,256]{1,0:T(8,128)(2,1)}, u32[]{:S(2)}, u32[]{:S(2)}) collective-permute-start(bf16[2048,256]{1,0:T(8,128)(2,1)} %refs_10_.1), channel_id=1, source_target_pairs={{0,6},{2,0},{4,2},{6,4},{1,7},{3,1},{5,3},{7,5},{8,14},{10,8},{12,... | collective-permute-start | bytes 3145736 | tf_op jit(solution)/shard_map/ppermute | solution.py:266
  28.0 46.4 %collective-permute-start = (bf16[2048,256]{1,0:T(8,128)(2,1)}, bf16[2048,256]{1,0:T(8,128)(2,1)}, u32[]{:S(2)}, u32[]{:S(2)}) collective-permute-start(bf16[2048,256]{1,0:T(8,128)(2,1)} %refs_10_.1), channel_id=1, source_target_pairs={{0,2},{2,4},{4,6},{6,0},{1,3},{3,5},{5,7},{7,1},{8,10},{10,12},{12... | collective-permute-start | bytes 3145736 | tf_op jit(solution)/shard_map/ppermute | solution.py:266
  50.1 26.1 %copy-start = (f32[2048]{0:T(1024)S(1)}, f32[2048]{0:T(1024)}, u32[]{:S(2)}) copy-start(f32[2048]{0:T(1024)} %param.8) | copy-start | bytes 24580
  50.1 43.9 %all-to-all-start.1 = ((bf16[64,8,1024]{2,1,0:T(8,128)(2,1)}), bf16[64,8,1024]{2,1,0:T(8,128)(2,1)}, u32[]{:S(2)}, u32[]{:S(2)}) async-start(bf16[64,8,1024]{2,1,0:T(8,128)(2,1)} %shard_map.59), calls=%async_computation.1 | async-start | bytes 2097152 | tf_op jit(solution)/shard_map/all_to_all | solution.py:288
  58.2 19.3 %collective-permute-start.4 = (bf16[2048,256]{1,0:T(8,128)(2,1)}, bf16[2048,256]{1,0:T(8,128)(2,1)}, u32[]{:S(2)}, u32[]{:S(2)}) collective-permute-start(bf16[2048,256]{1,0:T(8,128)(2,1)} %refs_10_.1), channel_id=1, source_target_pairs={{0,1},{1,0},{2,3},{3,2},{4,5},{5,4},{6,7},{7,6},{8,9},{9,8},{10,11... | collective-permute-start | bytes 3145736 | tf_op jit(solution)/shard_map/ppermute | solution.py:271
  62.1 21.0 %collective-permute-start.3 = (bf16[2048,256]{1,0:T(8,128)(2,1)}, bf16[2048,256]{1,0:T(8,128)(2,1)}, u32[]{:S(2)}, u32[]{:S(2)}) collective-permute-start(bf16[2048,256]{1,0:T(8,128)(2,1)} %collective-permute-done.2.refs_4_.refs_12_), channel_id=1, source_target_pairs={{0,1},{1,0},{2,3},{3,2},{4,5},{5,4},{6,7},{7,6},{8,9},{9,8},{10,11... | collective-permute-start | bytes 3145736 | tf_op jit(solution)/shard_map/ppermute | solution.py:271
  70.9 23.2 %collective-permute-start.6 = (bf16[2048,256]{1,0:T(8,128)(2,1)}, bf16[2048,256]{1,0:T(8,128)(2,1)}, u32[]{:S(2)}, u32[]{:S(2)}) collective-permute-start(bf16[2048,256]{1,0:T(8,128)(2,1)} %collective-permute-done.1.refs_5_.refs_15_), channel_id=1, source_target_pairs={{0,1},{1,0},{2,3},{3,2},{4,5},{5,4},{6,7},{7,6},{8,9},{9,8},{10,11... | collective-permute-start | bytes 3145736 | tf_op jit(solution)/shard_map/ppermute | solution.py:271
  74.3 19.7 %collective-permute-start.5 = (bf16[2048,256]{1,0:T(8,128)(2,1)}, bf16[2048,256]{1,0:T(8,128)(2,1)}, u32[]{:S(2)}, u32[]{:S(2)}) collective-permute-start(bf16[2048,256]{1,0:T(8,128)(2,1)} %collective-permute-done.refs_4_.refs_14_), channel_id=1, source_target_pairs={{0,1},{1,0},{2,3},{3,2},{4,5},{5,4},{6,7},{7,6},{8,9},{9,8},{10,11... | collective-permute-start | bytes 3145736 | tf_op jit(solution)/shard_map/ppermute | solution.py:271

commit v8 on v7

--- a/solution.py
+++ b/solution.py
@@ -184,13 +184,17 @@
         pltpu.make_async_copy(source, target, sems.at[i])
         for i, (source, target) in enumerate(pairs)
     ]
-    for copy in copies:
+    stages = (copies[6:8], copies[8 : n + 3], copies[n + 3 :])
+    for copy in copies[:6]:
         copy.start()
     copies[0].wait()
     copies[1].wait()
     for i in range(0, n, 2):
         copies[i + 2].wait()
         copies[i + 3].wait()
+        if i // 2 < len(stages):
+            for copy in stages[i // 2]:
+                copy.start()
         here = slice(i * depth, (i + 2) * depth)
         value = jnp.dot(cross_v[...], blocks_v[:, here], preferred_element_type=jnp.float32)
         value = value.astype(jnp.bfloat16).astype(jnp.float32)

time: 106 us -> 106 us (level)
  no operation moved by 1% of the time
where the time goes in v8:
time: 106 us; the launch traced here: 105 us
  starting transfers between devices  46.6 us (44%)
  Pallas kernels  33.2 us (31%)
  waiting for transfers between devices  24.2 us (23%)
    all_to_all x1, starting transfers between devices, compute(): arrived = lax.all_to_all(partial, SAMP, 0, 0)  17.4 us
    all_to_all x1, waiting for transfers between devices, compute(): arrived = lax.all_to_all(partial, SAMP, 0, 0)  17.4 us
    pallas_call x3, Pallas kernels, components(): call(lambda *refs: components_body(first, order, *refs), (jax.ShapeDtypeS...  16.5 us
    pallas_call x1, Pallas kernels, compute(): call(lambda *refs: fitted_body(len(GROUPS), order, *refs), jax.ShapeDtype...  11.4 us
    ppermute x4, starting transfers between devices, compute(): blocks[shift, 1] = lax.ppermute(blocks[shift, 0], 'core', [(0, 1), (1, 0)])  11.1 us
    ppermute x3, starting transfers between devices, compute(): lax.ppermute(whitening, 'x', [(i, (i + shift) % n_x) for i in range(n_x)])  9.95 us
    all_to_all x1, starting transfers between devices, compute(): cross = lax.all_to_all(total, SAMP, 0, 0)  8.05 us
    ppermute x3, waiting for transfers between devices, compute(): lax.ppermute(whitening, 'x', [(i, (i + shift) % n_x) for i in range(n_x)])  6.87 us
  transfers between devices with their start and end apart: 9, of which 2 were waited for; matrix products, arithmetic and copies ran while one was open for 1% of the time, Pallas kernels for 18%

profile of v8, /device:TPU:1, one launch (start us, length us, event | category | flops | bytes accessed | tf_op | source)
XLA Modules:
  0.0 105.4 jit_solution(10158518593774268978)
XLA Ops:
  0.0 3.1 %shard_map.58 = bf16[64,8,1024]{2,1,0:T(8,128)(2,1)} custom-call(bf16[512,2048]{1,0:T(8,128)(2,1)} %refs_6_.1, bf16[512,256]{1,0:T(8,128)(2,1)} %refs_5_.1), custom_call_target="tpu_custom_call" | custom-call | flops 536870912 | bytes 3407872 | tf_op jit(solution)/shard_map/pallas_call | solution.py:250
  3.1 17.4 %all-to-all-start = ((bf16[64,8,1024]{2,1,0:T(8,128)(2,1)}), bf16[64,8,1024]{2,1,0:T(8,128)(2,1)}, u32[]{:S(2)}, u32[]{:S(2)}) async-start(bf16[64,8,1024]{2,1,0:T(8,128)(2,1)} %shard_map.58), calls=%async_computation | async-start | bytes 2097152 | tf_op jit(solution)/shard_map/all_to_all | solution.py:266
  20.5 4.7 %collective-permute-start.2 = (bf16[2048,256]{1,0:T(8,128)(2,1)}, bf16[2048,256]{1,0:T(8,128)(2,1)}, u32[]{:S(2)}, u32[]{:S(2)}) collective-permute-start(bf16[2048,256]{1,0:T(8,128)(2,1)} %refs_10_.1), channel_id=1, source_target_pairs={{0,4},{2,6},{4,0},{6,2},{1,5},{3,7},{5,1},{7,3},{8,12},{10,14},{12... | collective-permute-start | bytes 3145736 | tf_op jit(solution)/shard_map/ppermute | solution.py:270
  25.2 2.8 %collective-permute-start.1 = (bf16[2048,256]{1,0:T(8,128)(2,1)}, bf16[2048,256]{1,0:T(8,128)(2,1)}, u32[]{:S(2)}, u32[]{:S(2)}) collective-permute-start(bf16[2048,256]{1,0:T(8,128)(2,1)} %refs_10_.1), channel_id=1, source_target_pairs={{0,6},{2,0},{4,2},{6,4},{1,7},{3,1},{5,3},{7,5},{8,14},{10,8},{12,... | collective-permute-start | bytes 3145736 | tf_op jit(solution)/shard_map/ppermute | solution.py:270
  28.0 2.5 %collective-permute-start = (bf16[2048,256]{1,0:T(8,128)(2,1)}, bf16[2048,256]{1,0:T(8,128)(2,1)}, u32[]{:S(2)}, u32[]{:S(2)}) collective-permute-start(bf16[2048,256]{1,0:T(8,128)(2,1)} %refs_10_.1), channel_id=1, source_target_pairs={{0,2},{2,4},{4,6},{6,0},{1,3},{3,5},{5,7},{7,1},{8,10},{10,12},{12... | collective-permute-start | bytes 3145736 | tf_op jit(solution)/shard_map/ppermute | solution.py:270
  30.5 17.4 %all-to-all-done.arrived = bf16[64,8,1024]{2,1,0:T(8,128)(2,1)} async-done(((bf16[64,8,1024]{2,1,0:T(8,128)(2,1)}), bf16[64,8,1024]{2,1,0:T(8,128)(2,1)}, u32[]{:S(2)}, u32[]{:S(2)}) %all-to-all-start) | async-done | bytes 1048608 | tf_op jit(solution)/shard_map/all_to_all | solution.py:266
  47.9 2.3 %shard_map.59 = bf16[64,8,1024]{2,1,0:T(8,128)(2,1)} custom-call(bf16[64,8,1024]{2,1,0:T(8,128)(2,1)} %all-to-all-done.arrived), custom_call_target="tpu_custom_call" | custom-call | flops 524288 | bytes 2097152 | tf_op jit(solution)/shard_map/pallas_call | solution.py:277
  50.1 0.0 copy-start
  50.1 8.1 %all-to-all-start.1 = ((bf16[64,8,1024]{2,1,0:T(8,128)(2,1)}), bf16[64,8,1024]{2,1,0:T(8,128)(2,1)}, u32[]{:S(2)}, u32[]{:S(2)}) async-start(bf16[64,8,1024]{2,1,0:T(8,128)(2,1)} %shard_map.59), calls=%async_computation.1 | async-start | bytes 2097152 | tf_op jit(solution)/shard_map/all_to_all | solution.py:292
  58.2 3.9 %collective-permute-start.4 = (bf16[2048,256]{1,0:T(8,128)(2,1)}, bf16[2048,256]{1,0:T(8,128)(2,1)}, u32[]{:S(2)}, u32[]{:S(2)}) collective-permute-start(bf16[2048,256]{1,0:T(8,128)(2,1)} %refs_10_.1), channel_id=1, source_target_pairs={{0,1},{1,0},{2,3},{3,2},{4,5},{5,4},{6,7},{7,6},{8,9},{9,8},{10,11... | collective-permute-start | bytes 3145736 | tf_op jit(solution)/shard_map/ppermute | solution.py:275
  62.1 0.0 collective-permute-done.2.refs_4_.refs_12_
  62.1 1.9 %collective-permute-start.3 = (bf16[2048,256]{1,0:T(8,128)(2,1)}, bf16[2048,256]{1,0:T(8,128)(2,1)}, u32[]{:S(2)}, u32[]{:S(2)}) collective-permute-start(bf16[2048,256]{1,0:T(8,128)(2,1)} %collective-permute-done.2.refs_4_.refs_12_), channel_id=1, source_target_pairs={{0,1},{1,0},{2,3},{3,2},{4,5},{5,4},{6,7},{7,6},{8,9},{9,8},{10,11... | collective-permute-start | bytes 3145736 | tf_op jit(solution)/shard_map/ppermute | solution.py:275
  64.0 6.9 %collective-permute-done.1.refs_5_.refs_15_ = bf16[2048,256]{1,0:T(8,128)(2,1)} collective-permute-done((bf16[2048,256]{1,0:T(8,128)(2,1)}, bf16[2048,256]{1,0:T(8,128)(2,1)}, u32[]{:S(2)}, u32[]{:S(2)}) %collective-permute-start.1) | collective-permute-done | bytes 1048608 | tf_op jit(solution)/shard_map/ppermute | solution.py:270
  70.9 3.5 %collective-permute-start.6 = (bf16[2048,256]{1,0:T(8,128)(2,1)}, bf16[2048,256]{1,0:T(8,128)(2,1)}, u32[]{:S(2)}, u32[]{:S(2)}) collective-permute-start(bf16[2048,256]{1,0:T(8,128)(2,1)} %collective-permute-done.1.refs_5_.refs_15_), channel_id=1, source_target_pairs={{0,1},{1,0},{2,3},{3,2},{4,5},{5,4},{6,7},{7,6},{8,9},{9,8},{10,11... | collective-permute-start | bytes 3145736 | tf_op jit(solution)/shard_map/ppermute | solution.py:275
  74.3 0.0 collective-permute-done.refs_4_.refs_14_
  74.3 1.9 %collective-permute-start.5 = (bf16[2048,256]{1,0:T(8,128)(2,1)}, bf16[2048,256]{1,0:T(8,128)(2,1)}, u32[]{:S(2)}, u32[]{:S(2)}) collective-permute-start(bf16[2048,256]{1,0:T(8,128)(2,1)} %collective-permute-done.refs_4_.refs_14_), channel_id=1, source_target_pairs={{0,1},{1,0},{2,3},{3,2},{4,5},{5,4},{6,7},{7,6},{8,9},{9,8},{10,11... | collective-permute-start | bytes 3145736 | tf_op jit(solution)/shard_map/ppermute | solution.py:275
  76.3 0.0 copy-done
  76.3 0.6 reshape.6.refs_2_
  76.9 0.6 pad_add_fusion.refs_0_
  77.5 0.0 collective-permute-done.4.refs_5_.refs_11_
  77.5 5.5 %shard_map.55 = (bf16[512,512]{1,0:T(8,128)(2,1)}, f32[512,8]{1,0:T(8,128)}) custom-call(s32[2]{0:T(128)} %pad_add_fusion.refs_0_, f32[4]{0:T(128)} %refs_1_.7, f32[8,256]{1,0:T(8,128)} %reshape.6.refs_2_, bf16[512,2048]{1,0:T(8,128)(2,1)} %refs_6_.1, bf16[2048,256]{1,0:T(8,128)(2,1)} %refs_10_.1, bf16[2048,256]{1,0:T(8,128)(2,1)} %collective-permute-done.4.refs_5_.refs_11_), custom_call_target="tpu_custom_call" | custom-call | flops 1073741824 | bytes 4718592 | tf_op jit(solution)/shard_map/pallas_call | solution.py:298
  83.0 0.0 collective-permute-done.3.refs_5_.refs_13_
  83.1 5.5 %shard_map.56 = (bf16[512,512]{1,0:T(8,128)(2,1)}, f32[512,8]{1,0:T(8,128)}) custom-call(s32[2]{0:T(128)} %pad_add_fusion.refs_0_, f32[4]{0:T(128)} %refs_1_.7, f32[8,256]{1,0:T(8,128)} %reshape.6.refs_2_, bf16[512,2048]{1,0:T(8,128)(2,1)} %refs_6_.1, bf16[2048,256]{1,0:T(8,128)(2,1)} %collective-permute-done.2.refs_4_.refs_12_, ...), custom_call_target="tpu_custom_call" | custom-call | flops 1073741824 | bytes 4718592 | tf_op jit(solution)/shard_map/pallas_call | solution.py:298
  88.5 5.5 %shard_map.57 = (bf16[512,512]{1,0:T(8,128)(2,1)}, f32[512,8]{1,0:T(8,128)}) custom-call(s32[2]{0:T(128)} %pad_add_fusion.refs_0_, f32[4]{0:T(128)} %refs_1_.7, f32[8,256]{1,0:T(8,128)} %reshape.6.refs_2_, bf16[512,2048]{1,0:T(8,128)(2,1)} %refs_6_.1, bf16[2048,256]{1,0:T(8,128)(2,1)} %collective-permute-done.refs_4_.refs_14_, ...), custom_call_target="tpu_custom_call" | custom-call | flops 1073741824 | bytes 4718592 | tf_op jit(solution)/shard_map/pallas_call | solution.py:298
  94.0 0.0 collective-permute-done.6.refs_17_
  94.0 0.0 collective-permute-done.5.refs_16_
  94.0 0.0 all-to-all-done.1
  94.1 11.4 %shard_map.60 = f32[4,512,256]{2,1,0:T(8,128)} custom-call(s32[2]{0:T(128)} %pad_add_fusion.refs_0_, f32[4]{0:T(128)} %refs_1_.7, f32[8,256]{1,0:T(8,128)} %reshape.6.refs_2_, f32[512,8]{1,0:T(8,128)} %get-tuple-element.13.refs_3_, bf16[2,256,1024]{2,1,0:T(8,128)(2,1)} %bitcast.2.refs_4_, bf16[512,256]{1,0:T(8,128)(2,1)} %refs_5_.1, ...), custom_call_target="tpu_custom_call" | custom-call | flops 2147483648 | bytes 5242880 | tf_op jit(solution)/shard_map/pallas_call | solution.py:325
  (1 shorter events, 0.0 us)
Async XLA Ops:
  3.1 44.7 %all-to-all-start = ((bf16[64,8,1024]{2,1,0:T(8,128)(2,1)}), bf16[64,8,1024]{2,1,0:T(8,128)(2,1)}, u32[]{:S(2)}, u32[]{:S(2)}) async-start(bf16[64,8,1024]{2,1,0:T(8,128)(2,1)} %shard_map.58), calls=%async_computation | async-start | bytes 2097152 | tf_op jit(solution)/shard_map/all_to_all | solution.py:266
  20.5 41.5 %collective-permute-start.2 = (bf16[2048,256]{1,0:T(8,128)(2,1)}, bf16[2048,256]{1,0:T(8,128)(2,1)}, u32[]{:S(2)}, u32[]{:S(2)}) collective-permute-start(bf16[2048,256]{1,0:T(8,128)(2,1)} %refs_10_.1), channel_id=1, source_target_pairs={{0,4},{2,6},{4,0},{6,2},{1,5},{3,7},{5,1},{7,3},{8,12},{10,14},{12... | collective-permute-start | bytes 3145736 | tf_op jit(solution)/shard_map/ppermute | solution.py:270
  25.2 45.7 %collective-permute-start.1 = (bf16[2048,256]{1,0:T(8,128)(2,1)}, bf16[2048,256]{1,0:T(8,128)(2,1)}, u32[]{:S(2)}, u32[]{:S(2)}) collective-permute-start(bf16[2048,256]{1,0:T(8,128)(2,1)} %refs_10_.1), channel_id=1, source_target_pairs={{0,6},{2,0},{4,2},{6,4},{1,7},{3,1},{5,3},{7,5},{8,14},{10,8},{12,... | collective-permute-start | bytes 3145736 | tf_op jit(solution)/shard_map/ppermute | solution.py:270
  28.0 46.4 %collective-permute-start = (bf16[2048,256]{1,0:T(8,128)(2,1)}, bf16[2048,256]{1,0:T(8,128)(2,1)}, u32[]{:S(2)}, u32[]{:S(2)}) collective-permute-start(bf16[2048,256]{1,0:T(8,128)(2,1)} %refs_10_.1), channel_id=1, source_target_pairs={{0,2},{2,4},{4,6},{6,0},{1,3},{3,5},{5,7},{7,1},{8,10},{10,12},{12... | collective-permute-start | bytes 3145736 | tf_op jit(solution)/shard_map/ppermute | solution.py:270
  50.1 26.1 %copy-start = (f32[2048]{0:T(1024)S(1)}, f32[2048]{0:T(1024)}, u32[]{:S(2)}) copy-start(f32[2048]{0:T(1024)} %param.8) | copy-start | bytes 24580
  50.1 43.9 %all-to-all-start.1 = ((bf16[64,8,1024]{2,1,0:T(8,128)(2,1)}), bf16[64,8,1024]{2,1,0:T(8,128)(2,1)}, u32[]{:S(2)}, u32[]{:S(2)}) async-start(bf16[64,8,1024]{2,1,0:T(8,128)(2,1)} %shard_map.59), calls=%async_computation.1 | async-start | bytes 2097152 | tf_op jit(solution)/shard_map/all_to_all | solution.py:292
  58.2 19.3 %collective-permute-start.4 = (bf16[2048,256]{1,0:T(8,128)(2,1)}, bf16[2048,256]{1,0:T(8,128)(2,1)}, u32[]{:S(2)}, u32[]{:S(2)}) collective-permute-start(bf16[2048,256]{1,0:T(8,128)(2,1)} %refs_10_.1), channel_id=1, source_target_pairs={{0,1},{1,0},{2,3},{3,2},{4,5},{5,4},{6,7},{7,6},{8,9},{9,8},{10,11... | collective-permute-start | bytes 3145736 | tf_op jit(solution)/shard_map/ppermute | solution.py:275
  62.1 21.0 %collective-permute-start.3 = (bf16[2048,256]{1,0:T(8,128)(2,1)}, bf16[2048,256]{1,0:T(8,128)(2,1)}, u32[]{:S(2)}, u32[]{:S(2)}) collective-permute-start(bf16[2048,256]{1,0:T(8,128)(2,1)} %collective-permute-done.2.refs_4_.refs_12_), channel_id=1, source_target_pairs={{0,1},{1,0},{2,3},{3,2},{4,5},{5,4},{6,7},{7,6},{8,9},{9,8},{10,11... | collective-permute-start | bytes 3145736 | tf_op jit(solution)/shard_map/ppermute | solution.py:275
  70.9 23.2 %collective-permute-start.6 = (bf16[2048,256]{1,0:T(8,128)(2,1)}, bf16[2048,256]{1,0:T(8,128)(2,1)}, u32[]{:S(2)}, u32[]{:S(2)}) collective-permute-start(bf16[2048,256]{1,0:T(8,128)(2,1)} %collective-permute-done.1.refs_5_.refs_15_), channel_id=1, source_target_pairs={{0,1},{1,0},{2,3},{3,2},{4,5},{5,4},{6,7},{7,6},{8,9},{9,8},{10,11... | collective-permute-start | bytes 3145736 | tf_op jit(solution)/shard_map/ppermute | solution.py:275
  74.3 19.7 %collective-permute-start.5 = (bf16[2048,256]{1,0:T(8,128)(2,1)}, bf16[2048,256]{1,0:T(8,128)(2,1)}, u32[]{:S(2)}, u32[]{:S(2)}) collective-permute-start(bf16[2048,256]{1,0:T(8,128)(2,1)} %collective-permute-done.refs_4_.refs_14_), channel_id=1, source_target_pairs={{0,1},{1,0},{2,3},{3,2},{4,5},{5,4},{6,7},{7,6},{8,9},{9,8},{10,11... | collective-permute-start | bytes 3145736 | tf_op jit(solution)/shard_map/ppermute | solution.py:275

commit v9 on v7

--- a/solution.py
+++ b/solution.py
@@ -167,14 +167,15 @@
     place, lambdas, squared, level, cross, traits, samples = refs[:7]
     parts = refs[7 : 7 + n_groups]
     blocks = refs[7 + n_groups : 7 + n_groups + n]
-    out, cross_v, joined, traits_v, samples_v, blocks_v = refs[-10:-4]
+    out, stacked, joined, traits_v, blocks_v, projected = refs[-10:-4]
     scaled, out_v, sems, out_sems = refs[-4:]
     depth = blocks[0].shape[1]
     width, span = cross.shape[1:]
-    n_l = lambdas.shape[0]
-    pairs = [(cross.at[half], cross_v.at[:, half * span : (half + 1) * span]) for half in range(2)]
+    pairs = [
+        (cross.at[half], stacked.at[:width, half * span : (half + 1) * span]) for half in range(2)
+    ]
     pairs += [(blocks[i], blocks_v.at[:, i * depth : (i + 1) * depth]) for i in range(n)]
-    pairs.append((samples, samples_v))
+    pairs.append((samples, stacked.at[width:, :]))
     at = 0
     for part in parts:
         pairs.append((part, joined.at[:, at : at + part.shape[1]]))
@@ -192,29 +193,36 @@
         copies[i + 2].wait()
         copies[i + 3].wait()
         here = slice(i * depth, (i + 2) * depth)
-        value = jnp.dot(cross_v[...], blocks_v[:, here], preferred_element_type=jnp.float32)
-        value = value.astype(jnp.bfloat16).astype(jnp.float32)
-        for j, block in enumerate(order[i : i + 2]):
-            columns = slice((i + j) * depth, (i + j + 1) * depth)
-            for l, shrink in enumerate(shrink_of(place, squared, lambdas, block, range(n_l))):
-                scaled[l * width : (l + 1) * width, columns] = (
-                    value[:, j * depth : (j + 1) * depth] * shrink
-                ).astype(jnp.bfloat16)
-    copies[n + 2].wait()
-    here = slice(at, n * depth)
-    value = jnp.dot(
-        samples_v[...], blocks_v[:, here], preferred_element_type=jnp.float32
-    ).astype(jnp.bfloat16)
-    joined[:, here] = value
+        last = i == n - 2
+        if last:
+            for copy in copies[n + 2 :]:
+                copy.wait()
+        value = jnp.dot(
+            stacked[...] if last else stacked[:width, :],
+            blocks_v[:, here],
+            preferred_element_type=jnp.float32,
+        ).astype(jnp.bfloat16)
+        projected[:, here] = value[:width]
+        if last:
+            value = value[width:]
+            joined[:, here] = value
+    n_l = lambdas.shape[0]
     total = level[...] + levels(value, place, squared, lambdas, order[at // depth :])
     inverse = 1.0 / jnp.maximum(1.0 - (total[:, :n_l] + total[:, n_l:]), 0.25)
-    for copy in copies[n + 3 :]:
-        copy.wait()
     results = []
     for pair in range(n_l // 2):
+        for i, block in enumerate(order):
+            here = slice(i * depth, (i + 1) * depth)
+            value = projected[:, here].astype(jnp.float32)
+            for j, shrink in enumerate(
+                shrink_of(place, squared, lambdas, block, (2 * pair, 2 * pair + 1))
+            ):
+                scaled[pair, j * width : (j + 1) * width, here] = (value * shrink).astype(
+                    jnp.bfloat16
+                )
         fitted = lax.dot_general(
             joined[...],
-            scaled[2 * pair * width : 2 * (pair + 1) * width],
+            scaled[pair],
             (((1,), (1,)), ((), ())),
             preferred_element_type=jnp.float32,
         )
@@ -328,12 +336,12 @@
         2 * rows * every + 2 * every * width + 4 * n_l * rows * width,
         FULL,
         [
-            pltpu.VMEM((width, features), bf16),
+            pltpu.VMEM((width + rows, features), bf16),
             pltpu.VMEM((rows, every), bf16),
             pltpu.VMEM((rows, width), bf16),
-            pltpu.VMEM((rows, features), bf16),
             pltpu.VMEM((features, every), bf16),
-            pltpu.VMEM((n_l * width, every), bf16),
+            pltpu.VMEM((width, every), bf16),
+            pltpu.VMEM((n_l // 2, 2 * width, every), bf16),
             pltpu.VMEM((n_l, rows, width), f32),
             dma((n_blocks + len(GROUPS) + 4,)),
             dma((n_l,)),

time: 106 us -> 106 us (level)
  no operation moved by 1% of the time
where the time goes in v9:
time: 106 us; the launch traced here: 105 us
  starting transfers between devices  46.6 us (44%)
  Pallas kernels  33.2 us (31%)
  waiting for transfers between devices  24.2 us (23%)
    all_to_all x1, starting transfers between devices, compute(): arrived = lax.all_to_all(partial, SAMP, 0, 0)  17.4 us
    all_to_all x1, waiting for transfers between devices, compute(): arrived = lax.all_to_all(partial, SAMP, 0, 0)  17.4 us
    pallas_call x3, Pallas kernels, components(): call(lambda *refs: components_body(first, order, *refs), (jax.ShapeDtypeS...  16.5 us
    pallas_call x1, Pallas kernels, compute(): call(lambda *refs: fitted_body(len(GROUPS), order, *refs), jax.ShapeDtype...  11.3 us
    ppermute x4, starting transfers between devices, compute(): blocks[shift, 1] = lax.ppermute(blocks[shift, 0], 'core', [(0, 1), (1, 0)])  11.1 us
    ppermute x3, starting transfers between devices, compute(): lax.ppermute(whitening, 'x', [(i, (i + shift) % n_x) for i in range(n_x)])  9.95 us
    all_to_all x1, starting transfers between devices, compute(): cross = lax.all_to_all(total, SAMP, 0, 0)  8.05 us
    ppermute x3, waiting for transfers between devices, compute(): lax.ppermute(whitening, 'x', [(i, (i + shift) % n_x) for i in range(n_x)])  6.87 us
  transfers between devices with their start and end apart: 9, of which 2 were waited for; matrix products, arithmetic and copies ran while one was open for 1% of the time, Pallas kernels for 18%

profile of v9, /device:TPU:1, one launch (start us, length us, event | category | flops | bytes accessed | tf_op | source)
XLA Modules:
  0.0 105.4 jit_solution(720081916390090073)
XLA Ops:
  0.0 3.1 %shard_map.58 = bf16[64,8,1024]{2,1,0:T(8,128)(2,1)} custom-call(bf16[512,2048]{1,0:T(8,128)(2,1)} %refs_6_.1, bf16[512,256]{1,0:T(8,128)(2,1)} %refs_5_.1), custom_call_target="tpu_custom_call" | custom-call | flops 536870912 | bytes 3407872 | tf_op jit(solution)/shard_map/pallas_call | solution.py:254
  3.1 17.4 %all-to-all-start = ((bf16[64,8,1024]{2,1,0:T(8,128)(2,1)}), bf16[64,8,1024]{2,1,0:T(8,128)(2,1)}, u32[]{:S(2)}, u32[]{:S(2)}) async-start(bf16[64,8,1024]{2,1,0:T(8,128)(2,1)} %shard_map.58), calls=%async_computation | async-start | bytes 2097152 | tf_op jit(solution)/shard_map/all_to_all | solution.py:270
  20.5 4.7 %collective-permute-start.2 = (bf16[2048,256]{1,0:T(8,128)(2,1)}, bf16[2048,256]{1,0:T(8,128)(2,1)}, u32[]{:S(2)}, u32[]{:S(2)}) collective-permute-start(bf16[2048,256]{1,0:T(8,128)(2,1)} %refs_10_.1), channel_id=1, source_target_pairs={{0,4},{2,6},{4,0},{6,2},{1,5},{3,7},{5,1},{7,3},{8,12},{10,14},{12... | collective-permute-start | bytes 3145736 | tf_op jit(solution)/shard_map/ppermute | solution.py:274
  25.2 2.8 %collective-permute-start.1 = (bf16[2048,256]{1,0:T(8,128)(2,1)}, bf16[2048,256]{1,0:T(8,128)(2,1)}, u32[]{:S(2)}, u32[]{:S(2)}) collective-permute-start(bf16[2048,256]{1,0:T(8,128)(2,1)} %refs_10_.1), channel_id=1, source_target_pairs={{0,6},{2,0},{4,2},{6,4},{1,7},{3,1},{5,3},{7,5},{8,14},{10,8},{12,... | collective-permute-start | bytes 3145736 | tf_op jit(solution)/shard_map/ppermute | solution.py:274
  28.0 2.5 %collective-permute-start = (bf16[2048,256]{1,0:T(8,128)(2,1)}, bf16[2048,256]{1,0:T(8,128)(2,1)}, u32[]{:S(2)}, u32[]{:S(2)}) collective-permute-start(bf16[2048,256]{1,0:T(8,128)(2,1)} %refs_10_.1), channel_id=1, source_target_pairs={{0,2},{2,4},{4,6},{6,0},{1,3},{3,5},{5,7},{7,1},{8,10},{10,12},{12... | collective-permute-start | bytes 3145736 | tf_op jit(solution)/shard_map/ppermute | solution.py:274
  30.5 17.4 %all-to-all-done.arrived = bf16[64,8,1024]{2,1,0:T(8,128)(2,1)} async-done(((bf16[64,8,1024]{2,1,0:T(8,128)(2,1)}), bf16[64,8,1024]{2,1,0:T(8,128)(2,1)}, u32[]{:S(2)}, u32[]{:S(2)}) %all-to-all-start) | async-done | bytes 1048608 | tf_op jit(solution)/shard_map/all_to_all | solution.py:270
  47.9 2.3 %shard_map.59 = bf16[64,8,1024]{2,1,0:T(8,128)(2,1)} custom-call(bf16[64,8,1024]{2,1,0:T(8,128)(2,1)} %all-to-all-done.arrived), custom_call_target="tpu_custom_call" | custom-call | flops 524288 | bytes 2097152 | tf_op jit(solution)/shard_map/pallas_call | solution.py:281
  50.1 0.0 copy-start
  50.1 8.1 %all-to-all-start.1 = ((bf16[64,8,1024]{2,1,0:T(8,128)(2,1)}), bf16[64,8,1024]{2,1,0:T(8,128)(2,1)}, u32[]{:S(2)}, u32[]{:S(2)}) async-start(bf16[64,8,1024]{2,1,0:T(8,128)(2,1)} %shard_map.59), calls=%async_computation.1 | async-start | bytes 2097152 | tf_op jit(solution)/shard_map/all_to_all | solution.py:296
  58.2 3.9 %collective-permute-start.4 = (bf16[2048,256]{1,0:T(8,128)(2,1)}, bf16[2048,256]{1,0:T(8,128)(2,1)}, u32[]{:S(2)}, u32[]{:S(2)}) collective-permute-start(bf16[2048,256]{1,0:T(8,128)(2,1)} %refs_10_.1), channel_id=1, source_target_pairs={{0,1},{1,0},{2,3},{3,2},{4,5},{5,4},{6,7},{7,6},{8,9},{9,8},{10,11... | collective-permute-start | bytes 3145736 | tf_op jit(solution)/shard_map/ppermute | solution.py:279
  62.1 0.0 collective-permute-done.2.refs_4_.refs_12_
  62.1 1.9 %collective-permute-start.3 = (bf16[2048,256]{1,0:T(8,128)(2,1)}, bf16[2048,256]{1,0:T(8,128)(2,1)}, u32[]{:S(2)}, u32[]{:S(2)}) collective-permute-start(bf16[2048,256]{1,0:T(8,128)(2,1)} %collective-permute-done.2.refs_4_.refs_12_), channel_id=1, source_target_pairs={{0,1},{1,0},{2,3},{3,2},{4,5},{5,4},{6,7},{7,6},{8,9},{9,8},{10,11... | collective-permute-start | bytes 3145736 | tf_op jit(solution)/shard_map/ppermute | solution.py:279
  64.0 6.9 %collective-permute-done.1.refs_5_.refs_15_ = bf16[2048,256]{1,0:T(8,128)(2,1)} collective-permute-done((bf16[2048,256]{1,0:T(8,128)(2,1)}, bf16[2048,256]{1,0:T(8,128)(2,1)}, u32[]{:S(2)}, u32[]{:S(2)}) %collective-permute-start.1) | collective-permute-done | bytes 1048608 | tf_op jit(solution)/shard_map/ppermute | solution.py:274
  70.9 3.5 %collective-permute-start.6 = (bf16[2048,256]{1,0:T(8,128)(2,1)}, bf16[2048,256]{1,0:T(8,128)(2,1)}, u32[]{:S(2)}, u32[]{:S(2)}) collective-permute-start(bf16[2048,256]{1,0:T(8,128)(2,1)} %collective-permute-done.1.refs_5_.refs_15_), channel_id=1, source_target_pairs={{0,1},{1,0},{2,3},{3,2},{4,5},{5,4},{6,7},{7,6},{8,9},{9,8},{10,11... | collective-permute-start | bytes 3145736 | tf_op jit(solution)/shard_map/ppermute | solution.py:279
  74.3 0.0 collective-permute-done.refs_4_.refs_14_
  74.3 1.9 %collective-permute-start.5 = (bf16[2048,256]{1,0:T(8,128)(2,1)}, bf16[2048,256]{1,0:T(8,128)(2,1)}, u32[]{:S(2)}, u32[]{:S(2)}) collective-permute-start(bf16[2048,256]{1,0:T(8,128)(2,1)} %collective-permute-done.refs_4_.refs_14_), channel_id=1, source_target_pairs={{0,1},{1,0},{2,3},{3,2},{4,5},{5,4},{6,7},{7,6},{8,9},{9,8},{10,11... | collective-permute-start | bytes 3145736 | tf_op jit(solution)/shard_map/ppermute | solution.py:279
  76.3 0.0 copy-done
  76.3 0.6 reshape.6.refs_2_
  76.9 0.6 pad_add_fusion.refs_0_
  77.5 0.0 collective-permute-done.4.refs_5_.refs_11_
  77.5 5.5 %shard_map.55 = (bf16[512,512]{1,0:T(8,128)(2,1)}, f32[512,8]{1,0:T(8,128)}) custom-call(s32[2]{0:T(128)} %pad_add_fusion.refs_0_, f32[4]{0:T(128)} %refs_1_.7, f32[8,256]{1,0:T(8,128)} %reshape.6.refs_2_, bf16[512,2048]{1,0:T(8,128)(2,1)} %refs_6_.1, bf16[2048,256]{1,0:T(8,128)(2,1)} %refs_10_.1, bf16[2048,256]{1,0:T(8,128)(2,1)} %collective-permute-done.4.refs_5_.refs_11_), custom_call_target="tpu_custom_call" | custom-call | flops 1073741824 | bytes 4718592 | tf_op jit(solution)/shard_map/pallas_call | solution.py:302
  83.0 0.0 collective-permute-done.3.refs_5_.refs_13_
  83.1 5.5 %shard_map.56 = (bf16[512,512]{1,0:T(8,128)(2,1)}, f32[512,8]{1,0:T(8,128)}) custom-call(s32[2]{0:T(128)} %pad_add_fusion.refs_0_, f32[4]{0:T(128)} %refs_1_.7, f32[8,256]{1,0:T(8,128)} %reshape.6.refs_2_, bf16[512,2048]{1,0:T(8,128)(2,1)} %refs_6_.1, bf16[2048,256]{1,0:T(8,128)(2,1)} %collective-permute-done.2.refs_4_.refs_12_, ...), custom_call_target="tpu_custom_call" | custom-call | flops 1073741824 | bytes 4718592 | tf_op jit(solution)/shard_map/pallas_call | solution.py:302
  88.5 5.5 %shard_map.57 = (bf16[512,512]{1,0:T(8,128)(2,1)}, f32[512,8]{1,0:T(8,128)}) custom-call(s32[2]{0:T(128)} %pad_add_fusion.refs_0_, f32[4]{0:T(128)} %refs_1_.7, f32[8,256]{1,0:T(8,128)} %reshape.6.refs_2_, bf16[512,2048]{1,0:T(8,128)(2,1)} %refs_6_.1, bf16[2048,256]{1,0:T(8,128)(2,1)} %collective-permute-done.refs_4_.refs_14_, ...), custom_call_target="tpu_custom_call" | custom-call | flops 1073741824 | bytes 4718592 | tf_op jit(solution)/shard_map/pallas_call | solution.py:302
  94.0 0.0 collective-permute-done.6.refs_17_
  94.0 0.0 collective-permute-done.5.refs_16_
  94.0 0.0 all-to-all-done.1
  94.1 11.3 %shard_map.60 = f32[4,512,256]{2,1,0:T(8,128)} custom-call(s32[2]{0:T(128)} %pad_add_fusion.refs_0_, f32[4]{0:T(128)} %refs_1_.7, f32[8,256]{1,0:T(8,128)} %reshape.6.refs_2_, f32[512,8]{1,0:T(8,128)} %get-tuple-element.13.refs_3_, bf16[2,256,1024]{2,1,0:T(8,128)(2,1)} %bitcast.2.refs_4_, bf16[512,256]{1,0:T(8,128)(2,1)} %refs_5_.1, ...), custom_call_target="tpu_custom_call" | custom-call | flops 2147483648 | bytes 5242880 | tf_op jit(solution)/shard_map/pallas_call | solution.py:329
  (1 shorter events, 0.0 us)
Async XLA Ops:
  3.1 44.7 %all-to-all-start = ((bf16[64,8,1024]{2,1,0:T(8,128)(2,1)}), bf16[64,8,1024]{2,1,0:T(8,128)(2,1)}, u32[]{:S(2)}, u32[]{:S(2)}) async-start(bf16[64,8,1024]{2,1,0:T(8,128)(2,1)} %shard_map.58), calls=%async_computation | async-start | bytes 2097152 | tf_op jit(solution)/shard_map/all_to_all | solution.py:270
  20.5 41.5 %collective-permute-start.2 = (bf16[2048,256]{1,0:T(8,128)(2,1)}, bf16[2048,256]{1,0:T(8,128)(2,1)}, u32[]{:S(2)}, u32[]{:S(2)}) collective-permute-start(bf16[2048,256]{1,0:T(8,128)(2,1)} %refs_10_.1), channel_id=1, source_target_pairs={{0,4},{2,6},{4,0},{6,2},{1,5},{3,7},{5,1},{7,3},{8,12},{10,14},{12... | collective-permute-start | bytes 3145736 | tf_op jit(solution)/shard_map/ppermute | solution.py:274
  25.2 45.7 %collective-permute-start.1 = (bf16[2048,256]{1,0:T(8,128)(2,1)}, bf16[2048,256]{1,0:T(8,128)(2,1)}, u32[]{:S(2)}, u32[]{:S(2)}) collective-permute-start(bf16[2048,256]{1,0:T(8,128)(2,1)} %refs_10_.1), channel_id=1, source_target_pairs={{0,6},{2,0},{4,2},{6,4},{1,7},{3,1},{5,3},{7,5},{8,14},{10,8},{12,... | collective-permute-start | bytes 3145736 | tf_op jit(solution)/shard_map/ppermute | solution.py:274
  28.0 46.4 %collective-permute-start = (bf16[2048,256]{1,0:T(8,128)(2,1)}, bf16[2048,256]{1,0:T(8,128)(2,1)}, u32[]{:S(2)}, u32[]{:S(2)}) collective-permute-start(bf16[2048,256]{1,0:T(8,128)(2,1)} %refs_10_.1), channel_id=1, source_target_pairs={{0,2},{2,4},{4,6},{6,0},{1,3},{3,5},{5,7},{7,1},{8,10},{10,12},{12... | collective-permute-start | bytes 3145736 | tf_op jit(solution)/shard_map/ppermute | solution.py:274
  50.1 26.1 %copy-start = (f32[2048]{0:T(1024)S(1)}, f32[2048]{0:T(1024)}, u32[]{:S(2)}) copy-start(f32[2048]{0:T(1024)} %param.8) | copy-start | bytes 24580
  50.1 43.9 %all-to-all-start.1 = ((bf16[64,8,1024]{2,1,0:T(8,128)(2,1)}), bf16[64,8,1024]{2,1,0:T(8,128)(2,1)}, u32[]{:S(2)}, u32[]{:S(2)}) async-start(bf16[64,8,1024]{2,1,0:T(8,128)(2,1)} %shard_map.59), calls=%async_computation.1 | async-start | bytes 2097152 | tf_op jit(solution)/shard_map/all_to_all | solution.py:296
  58.2 19.3 %collective-permute-start.4 = (bf16[2048,256]{1,0:T(8,128)(2,1)}, bf16[2048,256]{1,0:T(8,128)(2,1)}, u32[]{:S(2)}, u32[]{:S(2)}) collective-permute-start(bf16[2048,256]{1,0:T(8,128)(2,1)} %refs_10_.1), channel_id=1, source_target_pairs={{0,1},{1,0},{2,3},{3,2},{4,5},{5,4},{6,7},{7,6},{8,9},{9,8},{10,11... | collective-permute-start | bytes 3145736 | tf_op jit(solution)/shard_map/ppermute | solution.py:279
  62.1 21.0 %collective-permute-start.3 = (bf16[2048,256]{1,0:T(8,128)(2,1)}, bf16[2048,256]{1,0:T(8,128)(2,1)}, u32[]{:S(2)}, u32[]{:S(2)}) collective-permute-start(bf16[2048,256]{1,0:T(8,128)(2,1)} %collective-permute-done.2.refs_4_.refs_12_), channel_id=1, source_target_pairs={{0,1},{1,0},{2,3},{3,2},{4,5},{5,4},{6,7},{7,6},{8,9},{9,8},{10,11... | collective-permute-start | bytes 3145736 | tf_op jit(solution)/shard_map/ppermute | solution.py:279
  70.9 23.2 %collective-permute-start.6 = (bf16[2048,256]{1,0:T(8,128)(2,1)}, bf16[2048,256]{1,0:T(8,128)(2,1)}, u32[]{:S(2)}, u32[]{:S(2)}) collective-permute-start(bf16[2048,256]{1,0:T(8,128)(2,1)} %collective-permute-done.1.refs_5_.refs_15_), channel_id=1, source_target_pairs={{0,1},{1,0},{2,3},{3,2},{4,5},{5,4},{6,7},{7,6},{8,9},{9,8},{10,11... | collective-permute-start | bytes 3145736 | tf_op jit(solution)/shard_map/ppermute | solution.py:279
  74.3 19.7 %collective-permute-start.5 = (bf16[2048,256]{1,0:T(8,128)(2,1)}, bf16[2048,256]{1,0:T(8,128)(2,1)}, u32[]{:S(2)}, u32[]{:S(2)}) collective-permute-start(bf16[2048,256]{1,0:T(8,128)(2,1)} %collective-permute-done.refs_4_.refs_14_), channel_id=1, source_target_pairs={{0,1},{1,0},{2,3},{3,2},{4,5},{5,4},{6,7},{7,6},{8,9},{9,8},{10,11... | collective-permute-start | bytes 3145736 | tf_op jit(solution)/shard_map/ppermute | solution.py:279
